TPU v7x, 256 devices: a whole 4x4x8 slice. The times are simulated.
256 devices in a mesh: patch: 64 (over z, y, x_hi), sub: 4 (over x_lo, core).
Axes of the slice: x: 4 (x_hi: 2, x_lo: 2; x = x_hi * 2 + x_lo), y: 4, z: 8, core: 2. Of those that a mesh axis runs over, the one named last changes fastest.
Arguments:
- pieces_image: float32 [4, 2048, 8, 256], P('sub', 'patch'), may hold values from -6 to 6
- pieces_variance: float32 [4, 2048, 8, 256], P('sub', 'patch'), may hold values from 0.5 to 2
- piece_patch: int32 [4, 2048, 1], P('sub', 'patch'), may hold values from 0 to 63; in each aligned block of 32 rows (0 to 31, 32 to 63, ..., all dimensions but the last counted through in order) at most 2 rows name the same one
- piece_cell: int32 [4, 2048], P('sub', 'patch'), may hold values from 0 to 31
- stamp_row: int32 [64, 48], P('patch', 'sub'), may hold values from 0 to 63
- stamp_col: int32 [64, 48], P('patch', 'sub'), may hold values from 0 to 255
- stamp_count: int32 [64, 4], P('patch', 'sub'), may hold values from 2 to 12, as said below
- warp_offsets: int32 [4], replicated, may hold values from 0 to 8
Outputs:
- difference: float32 [4, 64, 256, 256], P(None, 'patch', 'sub')
- significance: float32 [4, 64, 256, 256], P(None, 'patch', 'sub')
Inputs may be any that keep to these rules, and one draw needn't show every extreme that they name: `piece_patch`: the pieces of one device name the same patch at most 2 times, and in every draw some device names some patch exactly 2 times. `stamp_count`: stamps of a sub-tile whose index is this count or more are unused.
All inputs are finite; a program needn't handle non-finite values.
Results may differ from a plain program's by a relative error of at most 0.0003.
Values sent between devices are 32-bit elements; how exact they have to be, the bound alone decides.
A program may use at most 64 MiB of HBM per device.

v0:
```python
import math

import jax
import jax.numpy as jnp
from jax import lax
from jax.sharding import PartitionSpec as P

NCELL = 8
KR = 10
PR = 10
SH = 15
WARP = 4


SIGMAS = (0.75, 1.5, 3.0)
DEGREES = (4, 4, 3)
PSF_SIGMA = 2.0
SKY_VAR = 0.1
RIDGE = 0.5
EPS = 1e-05
HIGH = lax.Precision.HIGHEST


def sent_together(arrays, axis, split_dim, concat_dim, along):
    widths = [math.prod(a.shape[along:]) for a in arrays]
    both = jnp.concatenate(
        [a.reshape(*a.shape[:along], w) for a, w in zip(arrays, widths)], axis=along
    )
    result = lax.all_to_all(both, axis, split_axis=split_dim, concat_axis=concat_dim, tiled=True)
    blocks = jnp.split(result, [sum(widths[:k]) for k in range(1, len(widths))], axis=along)
    return tuple(
        (b.reshape(*result.shape[:along], *a.shape[along:]) for a, b in zip(arrays, blocks))
    )


def padded_2(cells, sides, width):
    for axis, dim in sides:
        count = lax.axis_size(axis)
        ends = count - 1
        head = lax.slice_in_dim(cells, 0, width, axis=dim)
        tail = lax.slice_in_dim(cells, cells.shape[dim] - width, cells.shape[dim], axis=dim)
        cells = jnp.concatenate(
            [
                lax.ppermute(tail, axis, [(i, (i + 1) % count) for i in range(ends)]),
                cells,
                lax.ppermute(head, axis, [((i + 1) % count, i) for i in range(ends)]),
            ],
            axis=dim,
        )
    return cells


def from_everyone(array, axis):
    copies = jnp.broadcast_to(array, (lax.axis_size(axis), *array.shape))
    return lax.all_to_all(copies, axis, split_axis=0, concat_axis=0, tiled=True)


def over_copies(array, axis):
    return from_everyone(array, axis).sum(axis=0)


def packed_total(arrays, axis):
    flat, at, done = (jnp.concatenate([a.reshape(-1) for a in arrays]), 0, [])
    subtotal = over_copies(flat, axis)
    for a in arrays:
        done.append(subtotal[at : at + a.size].reshape(a.shape))
        at += a.size
    return tuple(done)


def hermite(degree, argument):
    previous = jnp.ones_like(argument)
    if degree == 0:
        return previous
    current = argument
    for term_no in range(1, degree):
        previous, current = (current, argument * current - term_no * previous)
    return current


def shapes_at(offset):
    result = []
    for spread, degree in zip(SIGMAS, DEGREES):
        scaled = offset / spread
        envelope = jnp.exp(-0.5 * scaled * scaled)
        for term_no in range(degree + 1):
            result.append(hermite(term_no, scaled) * envelope)
    return jnp.stack(result)


def psf_value(offset, power):
    support = jnp.arange(-PR, PR + 1).astype(jnp.float32)
    summed = jnp.sum(jnp.exp(-0.5 * (support / PSF_SIGMA) ** 2))
    return (jnp.exp(-0.5 * (offset / PSF_SIGMA) ** 2) / summed) ** power


def group_pairs():
    result = []
    first_tap = 0
    for degree in DEGREES:
        members = []
        for row_tap in range(degree + 1):
            for col_tap in range(degree + 1 - row_tap):
                members.append((first_tap + row_tap, first_tap + col_tap))
        result.append(members)
        first_tap += degree + 1
    return result


def column_band(make_taps, col_count, radius):
    position = jnp.arange(col_count).astype(jnp.float32)
    offset = position[:, None] - position[None, :]
    inside = jnp.abs(offset) <= radius
    return jnp.where(inside, make_taps(offset), 0.0)


def row_band(make_taps, row_count, radius):
    out_position = jnp.arange(row_count).astype(jnp.float32)
    in_position = jnp.arange(row_count + 2 * radius).astype(jnp.float32)
    offset = in_position[None, :] - out_position[:, None] - radius
    inside = jnp.abs(offset) <= radius
    return jnp.where(inside, make_taps(offset), 0.0)


def local_gram(groups, weight, image):
    flat_weight = weight.reshape(-1)
    flat_image = image.reshape(-1)
    gram_rows = []
    right_parts = []
    edge_terms = []
    for basis_part in groups:
        weighted = basis_part * flat_weight[None, :]
        blocks = [jnp.einsum("kp,lp->kl", weighted, partner, precision=HIGH) for partner in groups]
        column = jnp.sum(weighted, axis=1)
        edge_terms.append(column)
        gram_rows.append(jnp.concatenate(blocks + [column[:, None]], axis=1))
        right_parts.append(jnp.einsum("kp,p->k", weighted, flat_image, precision=HIGH))
    corner = jnp.sum(flat_weight)
    last_row = jnp.concatenate(edge_terms + [corner[None]])
    gram_matrix = jnp.concatenate(gram_rows + [last_row[None, :]], axis=0)
    right_side = jnp.concatenate(right_parts + [jnp.sum(flat_weight * flat_image)[None]])
    return (gram_matrix, right_side)


def solve_kernel(gram_matrix, right_side, normalizer):
    gram_matrix = gram_matrix / normalizer
    right_side = right_side / normalizer
    scaling = 1.0 / jnp.sqrt(jnp.diagonal(gram_matrix) + EPS)
    system = gram_matrix * scaling[:, None] * scaling[None, :] + RIDGE * jnp.eye(
        gram_matrix.shape[0], dtype=jnp.float32
    )
    factor = jnp.linalg.cholesky(system)
    return jax.scipy.linalg.cho_solve((factor, True), right_side * scaling) * scaling


def local(
    pieces_image,
    pieces_variance,
    piece_patch,
    piece_cell,
    stamp_row,
    stamp_col,
    stamp_count,
    warp_offsets,
):
    patches = lax.axis_size("patch")
    subtiles = lax.axis_size("sub")
    piece_count = pieces_image.shape[1]
    cell_rows = pieces_image.shape[2]
    col_count = pieces_image.shape[3]
    visits = warp_offsets.shape[0]
    row_count = cell_rows * NCELL
    capacity = max(2, 2 * piece_count // patches)
    slot_total = patches * capacity
    images = pieces_image[0]
    variances = pieces_variance[0]
    targets = piece_patch[0, :, 0]
    cell_ids = piece_cell[0]
    position = jnp.arange(piece_count)
    earlier = position[None, :] < position[:, None]
    same_dest = (targets[:, None] == targets[None, :]) & earlier
    rank_in = jnp.sum(same_dest.astype(jnp.int32), axis=1)
    where_to = targets * capacity + rank_in
    sent_image = (
        jnp.zeros((slot_total, cell_rows, col_count), jnp.float32)
        .at[where_to]
        .set(images, mode="drop")
        .reshape(patches, capacity, cell_rows, col_count)
    )
    sent_var = (
        jnp.zeros((slot_total, cell_rows, col_count), jnp.float32)
        .at[where_to]
        .set(variances, mode="drop")
        .reshape(patches, capacity, cell_rows, col_count)
    )
    sent_cell = (
        jnp.full((slot_total,), -1.0, jnp.float32)
        .at[where_to]
        .set(cell_ids.astype(jnp.float32), mode="drop")
        .reshape(patches, capacity)
    )

    def combine(onehot, got_plane):
        return jnp.einsum("sq,qp->sp", onehot, got_plane.reshape(slot_total, -1), precision=HIGH)

    def shifted(cell_planes):
        padded = jnp.pad(
            cell_planes.reshape(visits, row_count, col_count), ((0, 0), (0, 0), (WARP, WARP))
        )
        return jax.vmap(
            lambda visit_plane, offset: lax.dynamic_slice_in_dim(
                visit_plane, offset, col_count, axis=1
            )
        )(padded, warp_offsets)

    got = sent_together((sent_image, sent_var, sent_cell), "patch", 0, 0, 2)
    wanted = jnp.arange(visits * NCELL).astype(jnp.float32)
    onehot = (got[2].reshape(-1)[None, :] == wanted[:, None]).astype(jnp.float32)
    image_cells = combine(onehot, got[0])
    var_cells = combine(onehot, got[1])
    science = shifted(image_cells)
    template = jnp.sum(science, axis=0) / visits
    unscaled = shapes_at(jnp.arange(-KR, KR + 1).astype(jnp.float32))
    norms = jnp.sqrt(jnp.sum(unscaled * unscaled, axis=1))
    basis_cols = column_band(lambda offset: shapes_at(offset) / norms[:, None, None], col_count, KR)
    inner = jnp.einsum("rc,fcd->frd", template, basis_cols, precision=HIGH)
    filtered = padded_2(inner, (("sub", 1),), KR)
    basis_rows = row_band(lambda offset: shapes_at(offset) / norms[:, None, None], row_count, KR)
    groups = []
    for members in group_pairs():
        groups.append(
            jnp.stack(
                [
                    jnp.dot(basis_rows[row_tap], filtered[col_tap], precision=HIGH).reshape(-1)
                    for row_tap, col_tap in members
                ]
            )
        )
    variance_field = shifted(var_cells)
    template_var = jnp.sum(variance_field, axis=0) / (visits * visits)
    slots = stamp_row.shape[1]
    my_first = lax.axis_index("sub") * row_count
    live_here = (jnp.arange(slots) < stamp_count[0, 0]).astype(jnp.int32)
    stamp_table = jnp.stack([stamp_row[0] + my_first, stamp_col[0], live_here])
    near_stamps = padded_2(stamp_table, (("sub", 1),), slots)
    my_rows = my_first + jnp.arange(row_count)
    row_in = (
        (jnp.abs(my_rows[None, :] - near_stamps[0][:, None]) <= SH) & (near_stamps[2][:, None] > 0)
    ).astype(jnp.float32)
    col_in = (jnp.abs(jnp.arange(col_count)[None, :] - near_stamps[1][:, None]) <= SH).astype(
        jnp.float32
    )
    stamp_mask = jnp.minimum(jnp.dot(row_in.T, col_in, precision=HIGH), 1.0)
    normalizer = subtiles * slots * (2 * SH + 1) ** 2
    totals = variance_field + template_var[None] + SKY_VAR
    coefficients = []
    for visit_no in range(visits):
        gram_local, right_local = local_gram(
            groups, stamp_mask / totals[visit_no], science[visit_no]
        )
        gram_matrix, right_side = packed_total((gram_local, right_local), "sub")
        coefficients.append(solve_kernel(gram_matrix, right_side, normalizer))
    diff_list = []
    for visit_no in range(visits):
        solved = coefficients[visit_no]
        model = jnp.zeros((row_count * col_count,), jnp.float32) + solved[-1]
        first_row = 0
        for basis_part in groups:
            part_size = basis_part.shape[0]
            model = model + jnp.einsum(
                "k,kp->p", solved[first_row : first_row + part_size], basis_part, precision=HIGH
            )
            first_row += part_size
        diff_list.append(science[visit_no] - model.reshape(row_count, col_count))
    difference = jnp.stack(diff_list)
    col_psf_one = column_band(lambda offset: psf_value(offset, 1), col_count, PR)
    col_psf_two = column_band(lambda offset: psf_value(offset, 2), col_count, PR)
    row_psf_one = row_band(lambda offset: psf_value(offset, 1), row_count, PR)
    row_psf_two = row_band(lambda offset: psf_value(offset, 2), row_count, PR)
    num_cols = jnp.einsum("vrc,cd->vrd", difference / totals, col_psf_one, precision=HIGH)
    den_cols = jnp.einsum("vrc,cd->vrd", 1.0 / totals, col_psf_two, precision=HIGH)
    stacked = jnp.concatenate([num_cols, den_cols], axis=0)
    rimmed_detect = padded_2(stacked, (("sub", 1),), PR)
    numerator = jnp.einsum("rs,vsc->vrc", row_psf_one, rimmed_detect[:visits], precision=HIGH)
    denominator = jnp.einsum("rs,vsc->vrc", row_psf_two, rimmed_detect[visits:], precision=HIGH)
    significance = numerator / jnp.sqrt(denominator)
    return (difference[:, None], significance[:, None])


def solution(mesh):
    in_specs = (
        P("sub", "patch", None, None),
        P("sub", "patch", None, None),
        P("sub", "patch", None),
        P("sub", "patch"),
        P("patch", "sub"),
        P("patch", "sub"),
        P("patch", "sub"),
        P(),
    )
    out_specs = (P(None, "patch", "sub", None), P(None, "patch", "sub", None))
    return jax.shard_map(local, mesh=mesh, in_specs=in_specs, out_specs=out_specs, check_vma=False)
```

profile of v0, /device:TPU:1, one launch (start us, length us, event | category | flops | bytes accessed | tf_op | source)
XLA Modules:
  0.0 344.2 jit_solution(15062160902907326135)
XLA Ops:
  2.6 4.5 %collective-permute-start.2 = (s32[3,12]{1,0:T(4,128)S(1)}, s32[3,12]{1,0:T(4,128)S(1)}, u32[]{:S(2)}, u32[]{:S(2)}) collective-permute-start(s32[3,12]{1,0:T(4,128)S(1)} %pad_add_fusion), channel_id=1, source_target_pairs={{0,1},{1,2},{2,3},{4,5},{5,6},{6,7},{8,9},{9,10},{10,11},{12,13},{... | collective-permute-start | bytes 440 | tf_op jit(solution)/shard_map/ppermute | solution.py:44
  7.1 1.9 collective-permute-start.3
  10.7 2.8 scatter_fusion
  17.6 2.0 pad_maximum_fusion
  19.7 14.3 %all-to-all-start = ((f32[64,2,4097]{2,1,0:T(2,128)}), f32[64,2,4097]{2,1,0:T(2,128)S(1)}, u32[]{:S(2)}, u32[]{:S(2)}) async-start(f32[64,2,4097]{2,1,0:T(2,128)} %pad_maximum_fusion), calls=%async_computation | async-start | bytes 4325376 | tf_op jit(solution)/shard_map/all_to_all | solution.py:29
  48.9 38.0 %all-to-all-done = f32[64,2,4097]{2,1,0:T(2,128)S(1)} async-done(((f32[64,2,4097]{2,1,0:T(2,128)}), f32[64,2,4097]{2,1,0:T(2,128)S(1)}, u32[]{:S(2)}, u32[]{:S(2)}) %all-to-all-start) | async-done | bytes 2097696 | tf_op jit(solution)/shard_map/all_to_all | solution.py:29
  88.6 2.9 reshape_reshape.18
  96.5 4.9 %fusion.6 = f32[14,64,256]{2,1,0:T(8,128)S(1)} fusion(f32[14,256,256]{2,1,0:T(8,128)} %fusion.221, f32[14]{0:T(128)S(1)} %sqrt.22, pred[256,256]{1,0:T(8,128)(4,1)S(1)} %fusion.210, f32[64,256]{1,0:T(8,128)S(1)} %copy.184), kind=kOutput, calls=%fused_computation.16 | convolution fusion | flops 706494464 | bytes 4718648 | tf_op jit(solution)/shard_map/rc,fcd->frd/dot_general | solution.py:226
  102.3 3.0 collective-permute-start
  105.4 2.2 collective-permute-start.1
  114.2 2.0 fusion.248
  135.2 2.7 stack.19
  137.9 2.1 fusion.103
  140.0 1.9 fusion.110
  141.8 3.1 stack.21
  145.0 1.9 fusion.113
  146.9 2.1 fusion.101
  155.9 2.8 stack.22
  158.7 2.7 fusion.116
  161.4 2.1 fusion.99
  163.5 2.1 fusion.95
  165.6 2.1 fusion.93
  167.7 2.1 fusion.91
  169.8 2.1 fusion.87
  171.9 2.1 fusion.85
  174.0 2.1 fusion.83
  178.8 1.9 fusion.125
  180.7 1.9 fusion.122
  196.7 2.1 fusion.59
  198.8 1.9 fusion.134
  205.8 1.9 fusion.53
  218.2 1.9 fusion.143
  220.1 1.9 fusion.140
  242.0 3.4 all-to-all-start.1
  260.2 3.3 all-to-all-start.2
  264.9 3.7 %cholesky.74 = f32[41,41]{1,0:T(8,128)S(1)} custom-call(f32[41,41]{1,0:T(8,128)S(1)} %fusion.307), custom_call_target="Cholesky" | custom-call | tf_op jit(solution)/shard_map/jit(cholesky)/cholesky | solution.py:152
  270.0 3.1 custom-call.22
  276.1 3.5 %all-to-all-start.3 = ((f32[4,1,1722]{2,1,0:T(1,128)}), f32[4,1,1722]{2,1,0:T(1,128)S(1)}, u32[]{:S(2)}, u32[]{:S(2)}) async-start(f32[4,1,1722]{2,1,0:T(1,128)} %broadcast_in_dim.192), calls=%async_computation.3 | async-start | bytes 57344 | tf_op jit(solution)/shard_map/all_to_all | solution.py:55
  281.1 3.7 %cholesky.85 = f32[41,41]{1,0:T(8,128)S(1)} custom-call(f32[41,41]{1,0:T(8,128)S(1)} %fusion.304), custom_call_target="Cholesky" | custom-call | tf_op jit(solution)/shard_map/jit(cholesky)/cholesky | solution.py:152
  286.3 3.1 custom-call.23
  294.2 3.3 all-to-all-start.4
  299.0 3.7 %cholesky.96 = f32[41,41]{1,0:T(8,128)S(1)} custom-call(f32[41,41]{1,0:T(8,128)S(1)} %fusion.301), custom_call_target="Cholesky" | custom-call | tf_op jit(solution)/shard_map/jit(cholesky)/cholesky | solution.py:152
  304.1 3.1 custom-call.24
  314.8 3.7 %cholesky.107 = f32[41,41]{1,0:T(8,128)S(1)} custom-call(f32[41,41]{1,0:T(8,128)S(1)} %fusion.298), custom_call_target="Cholesky" | custom-call | tf_op jit(solution)/shard_map/jit(cholesky)/cholesky | solution.py:152
  320.0 3.1 custom-call.25
  331.1 3.5 %collective-permute-start.4 = (f32[8,10,256]{2,1,0:T(8,128)S(1)}, f32[8,10,256]{2,1,0:T(8,128)S(1)}, u32[]{:S(2)}, u32[]{:S(2)}) collective-permute-start(f32[8,10,256]{2,1,0:T(8,128)S(1)} %get-tuple-element.48), channel_id=1, source_target_pairs={{0,1},{1,2},{2,3},{4,5},{5,6},{6,7},{8,9},{9,10},{10,11},{12,13},{... | collective-permute-start | bytes 245768 | tf_op jit(solution)/shard_map/ppermute | solution.py:44
  334.6 1.9 collective-permute-start.5
  337.3 3.6 %collective-permute-done.5 = f32[8,10,256]{2,1,0:T(8,128)S(1)} collective-permute-done((f32[8,10,256]{2,1,0:T(8,128)S(1)}, f32[8,10,256]{2,1,0:T(8,128)S(1)}, u32[]{:S(2)}, u32[]{:S(2)}) %collective-permute-start.5) | collective-permute-done | bytes 81952 | tf_op jit(solution)/shard_map/ppermute | solution.py:46
  (427 shorter events, 164.6 us)
Async XLA Ops:
  2.6 46.2 %collective-permute-start.2 = (s32[3,12]{1,0:T(4,128)S(1)}, s32[3,12]{1,0:T(4,128)S(1)}, u32[]{:S(2)}, u32[]{:S(2)}) collective-permute-start(s32[3,12]{1,0:T(4,128)S(1)} %pad_add_fusion), channel_id=1, source_target_pairs={{0,1},{1,2},{2,3},{4,5},{5,6},{6,7},{8,9},{9,10},{10,11},{12,13},{... | collective-permute-start | bytes 440 | tf_op jit(solution)/shard_map/ppermute | solution.py:44
  7.1 41.7 %collective-permute-start.3 = (s32[3,12]{1,0:T(4,128)S(1)}, s32[3,12]{1,0:T(4,128)S(1)}, u32[]{:S(2)}, u32[]{:S(2)}) collective-permute-start(s32[3,12]{1,0:T(4,128)S(1)} %pad_add_fusion), channel_id=1, source_target_pairs={{1,0},{2,1},{3,2},{5,4},{6,5},{7,6},{9,8},{10,9},{11,10},{13,12},{... | collective-permute-start | bytes 440 | tf_op jit(solution)/shard_map/ppermute | solution.py:46
  14.5 2.2 copy-start.40
  19.7 15.4 %copy-start.41 = (s32[4]{0:T(128)S(1)}, s32[4]{0:T(128)}, u32[]{:S(2)}) copy-start(s32[4]{0:T(128)} %param.18) | copy-start | bytes 52
  19.7 67.3 %all-to-all-start = ((f32[64,2,4097]{2,1,0:T(2,128)}), f32[64,2,4097]{2,1,0:T(2,128)S(1)}, u32[]{:S(2)}, u32[]{:S(2)}) async-start(f32[64,2,4097]{2,1,0:T(2,128)} %pad_maximum_fusion), calls=%async_computation | async-start | bytes 4325376 | tf_op jit(solution)/shard_map/all_to_all | solution.py:29
  43.4 5.4 %copy-start.39 = (s32[1,12]{1,0:T(1,128)S(1)}, s32[1,12]{1,0:T(1,128)}, u32[]{:S(2)}) copy-start(s32[1,12]{1,0:T(1,128)} %param.16) | copy-start | bytes 148
  96.5 11.0 %copy-start = (f32[64,2,2048]{2,1,0:T(2,128)S(1)}, f32[64,2,2048]{2,1,0:T(2,128)}, u32[]{:S(2)}) copy-start(f32[64,2,2048]{2,1,0:T(2,128)} %get-tuple-element.44) | copy-start | bytes 3145732
  101.4 6.1 %copy-start.2 = (f32[14,64,256]{2,1,0:T(8,128)}, f32[14,64,256]{2,1,0:T(8,128)S(1)}, u32[]{:S(2)}) copy-start(f32[14,64,256]{2,1,0:T(8,128)S(1)} %fusion.6) | copy-start | bytes 2752516
  102.3 13.8 %collective-permute-start = (f32[14,10,256]{2,1,0:T(8,128)}, f32[14,10,256]{2,1,0:T(8,128)}, u32[]{:S(2)}, u32[]{:S(2)}) collective-permute-start(f32[14,10,256]{2,1,0:T(8,128)} %get-tuple-element.46), channel_id=1, source_target_pairs={{0,1},{1,2},{2,3},{4,5},{5,6},{6,7},{8,9},{9,10},{10,11},{12,13},{... | collective-permute-start | bytes 430088 | tf_op jit(solution)/shard_map/ppermute | solution.py:44
  105.4 10.8 %collective-permute-start.1 = (f32[14,10,256]{2,1,0:T(8,128)}, f32[14,10,256]{2,1,0:T(8,128)}, u32[]{:S(2)}, u32[]{:S(2)}) collective-permute-start(f32[14,10,256]{2,1,0:T(8,128)} %get-tuple-element.47), channel_id=1, source_target_pairs={{1,0},{2,1},{3,2},{5,4},{6,5},{7,6},{9,8},{10,9},{11,10},{13,12},{... | collective-permute-start | bytes 430088 | tf_op jit(solution)/shard_map/ppermute | solution.py:46
  111.9 2.1 copy-start.8
  112.0 2.1 copy-start.6
  112.0 4.1 %copy-start.14 = (f32[4,64,256]{2,1,0:T(8,128)}, f32[4,64,256]{2,1,0:T(8,128)S(1)}, u32[]{:S(2)}) copy-start(f32[4,64,256]{2,1,0:T(8,128)S(1)} %add_add_fusion) | copy-start | bytes 786436
  113.2 31.8 %copy-start.5 = (f32[1,1,64,256]{3,1,2,0:T(1,128)}, f32[1,1,64,256]{3,1,2,0:T(1,128)S(1)}, u32[]{:S(2)}) copy-start(f32[1,1,64,256]{3,1,2,0:T(1,128)S(1)} %copy.278) | copy-start | bytes 196612
  114.1 2.1 copy-start.3
  176.0 2.8 copy-start.4
  236.0 1.7 copy-start.37
  236.0 1.8 copy-start.36
  236.0 3.8 %copy-start.24 = (f32[15,15]{1,0:T(8,128)S(1)}, f32[15,15]{1,0:T(8,128)}, u32[]{:S(2)}) copy-start(f32[15,15]{1,0:T(8,128)} %fusion.103) | copy-start | bytes 2704
  236.0 3.8 %copy-start.25 = (f32[15,15]{1,0:T(8,128)S(1)}, f32[15,15]{1,0:T(8,128)}, u32[]{:S(2)}) copy-start(f32[15,15]{1,0:T(8,128)} %fusion.101) | copy-start | bytes 2704
  236.0 3.8 %copy-start.27 = (f32[15,10]{1,0:T(8,128)S(1)}, f32[15,10]{1,0:T(8,128)}, u32[]{:S(2)}) copy-start(f32[15,10]{1,0:T(8,128)} %fusion.99) | copy-start | bytes 1804
  236.0 3.8 %copy-start.28 = (f32[15,15]{1,0:T(8,128)S(1)}, f32[15,15]{1,0:T(8,128)}, u32[]{:S(2)}) copy-start(f32[15,15]{1,0:T(8,128)} %fusion.95) | copy-start | bytes 2704
  236.0 3.8 %copy-start.29 = (f32[15,15]{1,0:T(8,128)S(1)}, f32[15,15]{1,0:T(8,128)}, u32[]{:S(2)}) copy-start(f32[15,15]{1,0:T(8,128)} %fusion.93) | copy-start | bytes 2704
  236.0 3.8 %copy-start.30 = (f32[15,10]{1,0:T(8,128)S(1)}, f32[15,10]{1,0:T(8,128)}, u32[]{:S(2)}) copy-start(f32[15,10]{1,0:T(8,128)} %fusion.91) | copy-start | bytes 1804
  236.0 3.8 %copy-start.31 = (f32[10,15]{1,0:T(8,128)S(1)}, f32[10,15]{1,0:T(8,128)}, u32[]{:S(2)}) copy-start(f32[10,15]{1,0:T(8,128)} %fusion.87) | copy-start | bytes 1804
  236.0 3.8 %copy-start.32 = (f32[10,15]{1,0:T(8,128)S(1)}, f32[10,15]{1,0:T(8,128)}, u32[]{:S(2)}) copy-start(f32[10,15]{1,0:T(8,128)} %fusion.85) | copy-start | bytes 1804
  236.1 3.8 %copy-start.33 = (f32[10,10]{1,0:T(8,128)S(1)}, f32[10,10]{1,0:T(8,128)}, u32[]{:S(2)}) copy-start(f32[10,10]{1,0:T(8,128)} %fusion.83) | copy-start | bytes 1204
  236.1 14.2 %copy-start.35 = (f32[10]{0:T(128)S(1)}, f32[10]{0:T(128)}, u32[]{:S(2)}) copy-start(f32[10]{0:T(128)} %get-tuple-element.26) | copy-start | bytes 124
  236.1 17.2 %copy-start.34 = (f32[10]{0:T(128)S(1)}, f32[10]{0:T(128)}, u32[]{:S(2)}) copy-start(f32[10]{0:T(128)} %get-tuple-element.27) | copy-start | bytes 124
  236.1 18.7 %copy-start.26 = (f32[10,10]{1,0:T(8,128)S(1)}, f32[10,10]{1,0:T(8,128)}, u32[]{:S(2)}) copy-start(f32[10,10]{1,0:T(8,128)} %fusion.59) | copy-start | bytes 1204
  242.0 17.5 %all-to-all-start.1 = ((f32[4,1,1722]{2,1,0:T(1,128)}), f32[4,1,1722]{2,1,0:T(1,128)S(1)}, u32[]{:S(2)}, u32[]{:S(2)}) async-start(f32[4,1,1722]{2,1,0:T(1,128)} %broadcast_in_dim.178), calls=%async_computation.1 | async-start | bytes 57344 | tf_op jit(solution)/shard_map/all_to_all | solution.py:55
  260.2 15.3 %all-to-all-start.2 = ((f32[4,1,1722]{2,1,0:T(1,128)}), f32[4,1,1722]{2,1,0:T(1,128)S(1)}, u32[]{:S(2)}, u32[]{:S(2)}) async-start(f32[4,1,1722]{2,1,0:T(1,128)} %broadcast_in_dim.185), calls=%async_computation.2 | async-start | bytes 57344 | tf_op jit(solution)/shard_map/all_to_all | solution.py:55
  276.1 17.5 %all-to-all-start.3 = ((f32[4,1,1722]{2,1,0:T(1,128)}), f32[4,1,1722]{2,1,0:T(1,128)S(1)}, u32[]{:S(2)}, u32[]{:S(2)}) async-start(f32[4,1,1722]{2,1,0:T(1,128)} %broadcast_in_dim.192), calls=%async_computation.3 | async-start | bytes 57344 | tf_op jit(solution)/shard_map/all_to_all | solution.py:55
  294.2 19.1 %all-to-all-start.4 = ((f32[4,1,1722]{2,1,0:T(1,128)}), f32[4,1,1722]{2,1,0:T(1,128)S(1)}, u32[]{:S(2)}, u32[]{:S(2)}) async-start(f32[4,1,1722]{2,1,0:T(1,128)} %broadcast_in_dim.199), calls=%async_computation.4 | async-start | bytes 57344 | tf_op jit(solution)/shard_map/all_to_all | solution.py:55
  324.7 2.7 copy-start.13
  324.7 2.7 copy-start.16
  324.7 2.7 copy-start.17
  324.7 2.8 copy-start.18
  325.4 2.8 copy-start.11
  325.4 2.8 copy-start.19
  325.4 2.8 copy-start.20
  325.4 2.8 copy-start.21
  325.4 3.5 %copy-start.9 = (f32[1,64,256]{2,1,0:T(8,128)S(1)}, f32[1,64,256]{2,1,0:T(8,128)}, u32[]{:S(2)}) copy-start(f32[1,64,256]{2,1,0:T(8,128)} %copy-done.8) | copy-start | bytes 196612
  325.4 3.5 %copy-start.22 = (f32[1,16384]{1,0:T(1,128)S(1)}, f32[1,16384]{1,0:T(1,128)}, u32[]{:S(2)}) copy-start(f32[1,16384]{1,0:T(1,128)} %fusion.354) | copy-start | bytes 196612
  326.1 3.6 %copy-start.7 = (f32[1,64,256]{2,1,0:T(8,128)S(1)}, f32[1,64,256]{2,1,0:T(8,128)}, u32[]{:S(2)}) copy-start(f32[1,64,256]{2,1,0:T(8,128)} %copy-done.6) | copy-start | bytes 196612
  326.1 3.6 %copy-start.15 = (f32[4,64,256]{2,1,0:T(8,128)S(1)}, f32[4,64,256]{2,1,0:T(8,128)}, u32[]{:S(2)}) copy-start(f32[4,64,256]{2,1,0:T(8,128)} %copy-done.14) | copy-start | bytes 786436
  331.1 6.2 %collective-permute-start.4 = (f32[8,10,256]{2,1,0:T(8,128)S(1)}, f32[8,10,256]{2,1,0:T(8,128)S(1)}, u32[]{:S(2)}, u32[]{:S(2)}) collective-permute-start(f32[8,10,256]{2,1,0:T(8,128)S(1)} %get-tuple-element.48), channel_id=1, source_target_pairs={{0,1},{1,2},{2,3},{4,5},{5,6},{6,7},{8,9},{9,10},{10,11},{12,13},{... | collective-permute-start | bytes 245768 | tf_op jit(solution)/shard_map/ppermute | solution.py:44
  334.6 6.3 %collective-permute-start.5 = (f32[8,10,256]{2,1,0:T(8,128)S(1)}, f32[8,10,256]{2,1,0:T(8,128)S(1)}, u32[]{:S(2)}, u32[]{:S(2)}) collective-permute-start(f32[8,10,256]{2,1,0:T(8,128)S(1)} %get-tuple-element.49), channel_id=1, source_target_pairs={{1,0},{2,1},{3,2},{5,4},{6,5},{7,6},{9,8},{10,9},{11,10},{13,12},{... | collective-permute-start | bytes 245768 | tf_op jit(solution)/shard_map/ppermute | solution.py:46
  (5 other events, 6.7 us)
where the time goes:
time: 349 us; the launch traced here: 344 us
  matrix products  120 us (34%)
  other arithmetic  67.5 us (19%)
  local copies, waits for them, and re-layouts  67.1 us (19%)
  starting transfers between devices  44.8 us (13%)
  waiting for transfers between devices  41.7 us (12%)
    dot_general x36, matrix products, local_gram(): jnp.einsum('kp,lp->kl', weighted, partner, precision=HIGH)  60.3 us
    all_to_all x1, waiting for transfers between devices, sent_together(): lax.all_to_all(both, axis, split_axis=split_dim, concat_axis=concat_dim,...  38 us
    dot_general x12, matrix products, local_gram(): jnp.einsum('kp,p->k', weighted, flat_image, precision=HIGH)  23.5 us
    unnamed x136, local copies, waits for them, and re-layouts  18 us
    another operation x12, other arithmetic, solve_kernel(): factor = jnp.linalg.cholesky(system)  17.9 us
    another operation x8, other arithmetic, solve_kernel(): jax.scipy.linalg.cho_solve((factor, True), right_side * scaling) * scaling  15.2 us
    all_to_all x1, starting transfers between devices, sent_together(): lax.all_to_all(both, axis, split_axis=split_dim, concat_axis=concat_dim,...  14.3 us
    all_to_all x4, starting transfers between devices, from_everyone(): return lax.all_to_all(copies, axis, split_axis=0, concat_axis=0, tiled=True)  13.4 us
  transfers between devices with their start and end apart: 11, of which 2 were waited for; matrix products, arithmetic and copies ran while one was open for 26% of the time, Pallas kernels for 0%

commit v1 on v0

v1 whole, which is shorter than its diff:
```python
import functools
import math

import jax
import jax.numpy as jnp
import numpy as np
from jax import lax
from jax.experimental import pallas as pl
from jax.experimental.pallas import tpu as pltpu
from jax.sharding import PartitionSpec as P

V = 4
NCELL = 8
CR = 8
RT = 64
CW = 256
KR = 10
PR = 10
SH = 15
WARP = 4
NB = 40
NP = 32
SIGMAS = (0.75, 1.5, 3.0)
DEGREES = (4, 4, 3)
PSF_SIGMA = 2.0
SKY_VAR = 0.1
RIDGE = 0.5
EPS = 1e-05
HIGH = lax.Precision.HIGHEST

NT = 14
XR = 48
TE = 128
CE = 96
TH = 24
SR = 16
HALO = TH + 2 * V * SR
VMEM_LIMIT = 56 * 1024 * 1024
WHOLE = pl.BlockSpec(memory_space=pltpu.VMEM)
SCALARS = pl.BlockSpec(memory_space=pltpu.SMEM)


def tap_values():
    u = np.arange(-KR, KR + 1).astype(np.float64)
    rows = []
    for sigma, degree in zip(SIGMAS, DEGREES):
        t = u / sigma
        env = np.exp(-0.5 * t * t)
        he = [np.ones_like(t), t]
        for n in range(1, degree):
            he.append(t * he[n] - n * he[n - 1])
        for n in range(degree + 1):
            h = he[n] * env
            rows.append(h / np.sqrt(np.sum(h * h)))
    return np.stack(rows)


def psf_values():
    u = np.arange(-PR, PR + 1).astype(np.float64)
    g = np.exp(-0.5 * (u / PSF_SIGMA) ** 2)
    return g / g.sum()


def split_np(a):
    a = a.astype(np.float32)
    hi = a.astype(jnp.bfloat16)
    lo = (a - hi.astype(np.float32)).astype(jnp.bfloat16)
    return hi, lo


def band(taps, rows, cols, first):
    radius = (len(taps) - 1) // 2
    out = np.zeros((rows, cols))
    for r in range(rows):
        for u in range(-radius, radius + 1):
            c = r + first + u
            if 0 <= c < cols:
                out[r, c] = taps[u + radius]
    return out


def constants():
    taps = tap_values()
    bands = np.concatenate([band(taps[j], CE, TE, SR) for j in range(NT)], axis=0)
    hi, lo = split_np(bands)
    row_bands = np.concatenate([hi, lo], axis=1)
    p = psf_values()
    cols, rows = [], []
    for f in (p, p * p):
        cols += list(split_np(band(f, CW, CW, 0)))
        h, l = split_np(band(f, RT, CE, SR))
        rows.append(np.concatenate([h, l, h], axis=1))
    return row_bands, np.stack(cols), np.stack(rows)


def members_of():
    result, first_tap, first = [], 0, 0
    for degree in DEGREES:
        index = {}
        for i in range(degree + 1):
            for j in range(degree + 1 - i):
                index[(i, j)] = first + len(index)
        result.append((first_tap, degree, index))
        first_tap += degree + 1
        first += len(index)
    return result


def split(x):
    hi = x.astype(jnp.bfloat16)
    return hi, (x - hi.astype(jnp.float32)).astype(jnp.bfloat16)


def mm(a, b):
    return jnp.dot(a, b, preferred_element_type=jnp.float32)


def pack_kernel(patch, cell, image, variance, out, out_cell, count):
    def clear(n, _):
        out_cell[n] = -1
        return 0

    def clear_count(n, _):
        count[n] = 0
        return 0

    slots = out.shape[0]
    lax.fori_loop(0, slots, clear, 0)
    lax.fori_loop(0, slots // 2, clear_count, 0)

    def place(n, _):
        q = patch[n]
        rank = count[q]
        count[q] = rank + 1
        slot = 2 * q + rank
        out_cell[slot] = cell[n]
        out[slot, 0:CR, :] = image[n]
        out[slot, CR : 2 * CR, :] = variance[n]
        return 0

    lax.fori_loop(0, image.shape[0], place, 0)


def combine_kernel(cells, warp, got, science, variance, template, up, down, acc):
    acc[...] = jnp.zeros_like(acc)

    def add(n, _):
        c = cells[n]
        c = jnp.where(c < 0, V * NCELL, c)
        acc[c] += got[n]
        return 0

    lax.fori_loop(0, got.shape[0], add, 0)
    col = lax.broadcasted_iota(jnp.int32, (CR, CW), 1)
    for v in range(V):
        off = warp[v]
        turn = jnp.where(off <= WARP, WARP - off, CW + WARP - off)
        source = col + (off - WARP)
        inside = (source >= 0) & (source < CW)
        for c in range(NCELL):
            rows = slice(c * CR, (c + 1) * CR)
            a = acc[v * NCELL + c, 0:CR, :]
            b = acc[v * NCELL + c, CR : 2 * CR, :]
            science[v, rows, :] = jnp.where(inside, pltpu.roll(a, turn, 1), 0.0)
            variance[v, rows, :] = jnp.where(inside, pltpu.roll(b, turn, 1), 0.0)
    template[...] = (science[0] + science[1] + science[2] + science[3]) / V
    up[0:TH, :] = template[0:TH, :]
    down[0:TH, :] = template[RT - TH : RT, :]
    for v in range(V):
        s_at, w_at = TH + v * SR, TH + (V + v) * SR
        up[s_at : s_at + SR, :] = science[v, 0:SR, :]
        up[w_at : w_at + SR, :] = variance[v, 0:SR, :]
        down[s_at : s_at + SR, :] = science[v, RT - SR : RT, :]
        down[w_at : w_at + SR, :] = variance[v, RT - SR : RT, :]


def gram_kernel(
    science, variance, template, above, below, mask, row_bands,
    basis, gram, text, filt, xleft, xright, weight, acc,
):
    taps = tap_values()

    def put(k, image):
        at = pl.ds(k, RT, stride=XR)
        xleft[at, :] = image[:, 0:128]
        xright[at, :] = image[:, 128:CW]

    zero8 = jnp.zeros((8, CW), jnp.float32)
    text[0:8, :] = zero8
    text[8:32, :] = above[0:TH, :]
    text[32:96, :] = template[...]
    text[96:120, :] = below[0:TH, :]
    text[120:128, :] = zero8
    col = lax.broadcasted_iota(jnp.int32, (8, CW), 1)

    def columns(i, _):
        rows = pl.ds(pl.multiple_of(i * 8, 8), 8)
        t = text[rows, :]
        sums = [None] * NT
        for u in range(0, KR + 1):
            if u:
                plus = jnp.where(col < CW - u, pltpu.roll(t, CW - u, 1), 0.0)
                minus = jnp.where(col >= u, pltpu.roll(t, u, 1), 0.0)
                even, odd = plus + minus, plus - minus
            first = 0
            for degree in DEGREES:
                for n in range(degree + 1):
                    j = first + n
                    h = float(np.float32(taps[j, KR + u]))
                    if u == 0:
                        sums[j] = t * h if n % 2 == 0 else None
                    else:
                        term = (even if n % 2 == 0 else odd) * h
                        sums[j] = term if sums[j] is None else sums[j] + term
                first += degree + 1
        for j in range(NT):
            filt[j, rows, :] = sums[j]
        return 0

    lax.fori_loop(0, TE // 8, columns, 0)

    for first_tap, degree, index in members_of():
        for j in range(degree + 1):
            count = degree + 1 - j
            lhs = row_bands[first_tap * CE : (first_tap + count) * CE, :]
            fh, fl = split(filt[first_tap + j])
            y = mm(lhs, jnp.concatenate([fh, fh], axis=0)) + mm(lhs[:, 0:TE], fl)
            for i in range(count):
                k = index[(i, j)]
                image = y[i * CE : (i + 1) * CE, :]
                basis[k] = image
                put(k, image[SR : SR + RT, :])
    put(NB, jnp.ones((RT, CW), jnp.float32))
    for v in range(V):
        put(NB + 1 + v, science[v])
    for n in range(NB + 1 + V, XR):
        put(n, jnp.zeros((RT, CW), jnp.float32))

    q = (variance[0] + variance[1] + variance[2] + variance[3]) / (V * V)
    m = mask[...]
    for v in range(V):
        weight[v] = m / (variance[v] + q + SKY_VAR)

    acc[...] = jnp.zeros_like(acc)
    step = 4

    def rows_of(i, _):
        lefts, rights = [], []
        for r0 in range(step):
            r = i * step + r0
            at = pl.ds(pl.multiple_of(r * XR, 8), XR)
            x = jnp.concatenate([xleft[at, :], xright[at, :]], axis=1)
            xh, xl = split(x)
            rights.append(jnp.concatenate([xh, xl, jnp.zeros((32, CW), jnp.bfloat16)], axis=0))
            his, los = [], []
            for v in range(V):
                lh, ll = split(x * weight[v, pl.ds(r, 1), :])
                his.append(lh)
                los.append(ll)
            lefts.append(jnp.concatenate(his + los, axis=0))
        left = jnp.concatenate(lefts, axis=1)
        right = jnp.concatenate(rights, axis=1)
        acc[...] += lax.dot_general(
            left, right, (((1,), (1,)), ((), ())), preferred_element_type=jnp.float32
        )
        return 0

    lax.fori_loop(0, RT // step, rows_of, 0)
    high = acc[0 : V * XR, :]
    total = high + pltpu.roll(high, 128 - XR, 1) + acc[V * XR : 2 * V * XR, :]
    lane = lax.broadcasted_iota(jnp.int32, total.shape, 1)
    total = jnp.where(lane < XR, total, 0.0)
    gram[...] = total[0 : 2 * XR, :] + pltpu.roll(total[2 * XR : 4 * XR, :], 64, 1)


def pick(x, index):
    return jnp.take_along_axis(x, index, axis=1, mode="promise_in_bounds")


def final_kernel(
    normalizer, sub, gathered, basis, science, variance, above, below, cols, rows,
    difference, significance, coef, dplane, iplane,
):
    total = gathered[0] + gathered[1] + gathered[2] + gathered[3]
    total = total * (1.0 / normalizer)
    row = lax.broadcasted_iota(jnp.int32, (XR, 128), 0)
    lane = lax.broadcasted_iota(jnp.int32, (XR, 128), 1)
    part = lane // 64
    j = lane - part * 64
    base = part * 64
    halves, scales = [], []
    for half in range(2):
        a = total[half * XR : (half + 1) * XR, :]
        v = half + 2 * part
        e_col = lax.rsqrt(pick(a, base + row) + EPS)
        diag = jnp.sum(jnp.where(row == j, a, 0.0), axis=0, keepdims=True)
        e_row = lax.rsqrt(diag + EPS)
        scaled = a * e_col
        system = jnp.where(j <= NB, scaled * e_row, jnp.where(j == NB + 1 + v, scaled, 0.0))
        system = system + jnp.where(row == j, RIDGE, 0.0)
        halves.append(system)
        scales.append(e_col)
    for k in range(NB + 1):
        for half in range(2):
            a = halves[half]
            pivot_row = jnp.broadcast_to(a[k : k + 1, :], (XR, 128))
            pivot = pick(pivot_row, base + k)
            column = pick(a, base + k)
            column = jnp.where(row == k, pivot - 1.0, column)
            halves[half] = a - column * (pivot_row / pivot)
    for half in range(2):
        v = half + 2 * part
        a = pick(halves[half], base + NB + 1 + v) * scales[half]
        coef[half * XR : (half + 1) * XR, :] = pick(a, lane * 0)
        coef[(half + 2) * XR : (half + 3) * XR, :] = pick(a, lane * 0 + 64)

    me = sub[0]

    def block(b, _):
        at = pl.multiple_of(b * 8, 8)
        grow = lax.broadcasted_iota(jnp.int32, (8, CW), 0) + (b * 8 - SR)
        valid = ((grow >= 0) | (me > 0)) & ((grow < RT) | (me < 3))
        edge_a, edge_b = b < 2, b >= 10
        inner = pl.ds(pl.multiple_of(jnp.clip(b - 2, 0, 7) * 8, 8), 8)
        top = jnp.clip(b, 0, 1) * 8
        low = jnp.clip(b - 10, 0, 1) * 8

        def pull(own, first, v):
            at_a = pl.ds(pl.multiple_of(first + v * SR + top, 8), 8)
            at_b = pl.ds(pl.multiple_of(first + v * SR + low, 8), 8)
            return jnp.where(edge_a, above[at_a, :], jnp.where(edge_b, below[at_b, :], own[v, inner, :]))

        s = [pull(science, TH, v) for v in range(V)]
        w = [pull(variance, TH + V * SR, v) for v in range(V)]
        q = (w[0] + w[1] + w[2] + w[3]) / (V * V)
        acc = [s[v] - jnp.concatenate([coef[v * XR + NB : v * XR + NB + 1, :]] * 2, axis=1) for v in range(V)]
        for k in range(NB):
            c = basis[k, pl.ds(at, 8), :]
            for v in range(V):
                a = coef[v * XR + k : v * XR + k + 1, :]
                acc[v] = acc[v] - c * jnp.concatenate([a, a], axis=1)
        for v in range(V):
            inverse = jnp.where(valid, 1.0 / (w[v] + q + SKY_VAR), 0.0)
            plane = pl.ds(pl.multiple_of(v * CE + b * 8, 8), 8)
            dplane[plane, :] = acc[v] * inverse
            iplane[plane, :] = inverse

        @pl.when((b >= 2) & (b < 10))
        def _():
            for v in range(V):
                difference[v, inner, :] = acc[v]

        return 0

    lax.fori_loop(0, CE // 8, block, 0)
    filtered = []
    for n, plane in enumerate((dplane, iplane)):
        hi, lo = split(plane[...])
        ph, plo = cols[2 * n], cols[2 * n + 1]
        y = mm(hi, ph) + mm(lo, ph) + mm(hi, plo)
        yh, yl = split(y)
        outs = []
        for v in range(V):
            a = slice(v * CE, (v + 1) * CE)
            outs.append(mm(rows[n], jnp.concatenate([yh[a], yh[a], yl[a]], axis=0)))
        filtered.append(outs)
    for v in range(V):
        significance[v] = filtered[0][v] * lax.rsqrt(filtered[1][v])


def shape(*dims, dtype=jnp.float32):
    return jax.ShapeDtypeStruct(dims, dtype)


def params():
    return pltpu.CompilerParams(vmem_limit_bytes=VMEM_LIMIT)


def local(
    pieces_image, pieces_variance, piece_patch, piece_cell,
    stamp_row, stamp_col, stamp_count, warp_offsets,
):
    patches = lax.axis_size("patch")
    subtiles = lax.axis_size("sub")
    slot_total = 2 * patches
    me = lax.axis_index("sub")
    up_pairs = [(i + 1, i) for i in range(subtiles - 1)]
    down_pairs = [(i, i + 1) for i in range(subtiles - 1)]

    slots = stamp_row.shape[1]
    my_first = me * RT
    live_here = (jnp.arange(slots) < stamp_count[0, 0]).astype(jnp.int32)
    table = jnp.stack([stamp_row[0] + my_first, stamp_col[0], live_here])
    near = jnp.concatenate(
        [lax.ppermute(table, "sub", down_pairs), table, lax.ppermute(table, "sub", up_pairs)], axis=1
    )
    my_rows = my_first + jnp.arange(RT)
    row_in = (
        (jnp.abs(my_rows[None, :] - near[0][:, None]) <= SH) & (near[2][:, None] > 0)
    ).astype(jnp.bfloat16)
    col_in = (jnp.abs(jnp.arange(CW)[None, :] - near[1][:, None]) <= SH).astype(jnp.bfloat16)
    mask = jnp.minimum(jnp.dot(row_in.T, col_in, preferred_element_type=jnp.float32), 1.0)

    sent, sent_cell = pl.pallas_call(
        pack_kernel,
        out_shape=(shape(slot_total, 2 * CR, CW), shape(slot_total, dtype=jnp.int32)),
        in_specs=[SCALARS, SCALARS, WHOLE, WHOLE],
        out_specs=(WHOLE, SCALARS),
        scratch_shapes=[pltpu.SMEM((patches,), jnp.int32)],
        compiler_params=params(),
        name="pack",
    )(piece_patch.reshape(-1), piece_cell.reshape(-1), pieces_image[0], pieces_variance[0])
    got_cell = lax.all_to_all(
        sent_cell.reshape(patches, 2), "patch", split_axis=0, concat_axis=0, tiled=True
    )
    got = lax.all_to_all(
        sent.reshape(patches, 4 * CR, CW), "patch", split_axis=0, concat_axis=0, tiled=True
    )
    field = shape(V, RT, CW)
    science, variance, template, up, down = pl.pallas_call(
        combine_kernel,
        out_shape=(field, field, shape(RT, CW), shape(HALO, CW), shape(HALO, CW)),
        in_specs=[SCALARS, SCALARS, WHOLE],
        out_specs=(WHOLE,) * 5,
        scratch_shapes=[pltpu.VMEM((V * NCELL + 1, 2 * CR, CW), jnp.float32)],
        compiler_params=params(),
        name="combine",
    )(got_cell.reshape(-1), warp_offsets, got.reshape(slot_total, 2 * CR, CW))
    above = lax.ppermute(down, "sub", down_pairs)
    below = lax.ppermute(up, "sub", up_pairs)

    row_bands, cols, rows = constants()
    basis, gram = pl.pallas_call(
        gram_kernel,
        out_shape=(shape(NB, CE, CW), shape(2 * XR, 128)),
        in_specs=[WHOLE] * 7,
        out_specs=(WHOLE,) * 2,
        scratch_shapes=[
            pltpu.VMEM((TE, CW), jnp.float32),
            pltpu.VMEM((NT, TE, CW), jnp.float32),
            pltpu.VMEM((RT * XR, 128), jnp.float32),
            pltpu.VMEM((RT * XR, 128), jnp.float32),
            pltpu.VMEM((V, RT, CW), jnp.float32),
            pltpu.VMEM((2 * V * XR, 128), jnp.float32),
        ],
        compiler_params=params(),
        name="gram",
    )(science, variance, template, above, below, mask, jnp.asarray(row_bands))
    copies = jnp.broadcast_to(gram, (subtiles, *gram.shape))
    gathered = lax.all_to_all(copies, "sub", split_axis=0, concat_axis=0, tiled=True)

    normalizer = float(subtiles * slots * (2 * SH + 1) ** 2)
    difference, significance = pl.pallas_call(
        functools.partial(final_kernel, normalizer),
        out_shape=(field, field),
        in_specs=[SCALARS] + [WHOLE] * 8,
        out_specs=(WHOLE,) * 2,
        scratch_shapes=[
            pltpu.VMEM((V * XR, 128), jnp.float32),
            pltpu.VMEM((V * CE, CW), jnp.float32),
            pltpu.VMEM((V * CE, CW), jnp.float32),
        ],
        compiler_params=params(),
        name="final",
    )(
        me.reshape(1).astype(jnp.int32), gathered, basis, science, variance, above, below,
        jnp.asarray(cols), jnp.asarray(rows),
    )
    return (difference[:, None], significance[:, None])


def solution(mesh):
    in_specs = (
        P("sub", "patch", None, None),
        P("sub", "patch", None, None),
        P("sub", "patch", None),
        P("sub", "patch"),
        P("patch", "sub"),
        P("patch", "sub"),
        P("patch", "sub"),
        P(),
    )
    out_specs = (P(None, "patch", "sub", None), P(None, "patch", "sub", None))
    return jax.shard_map(local, mesh=mesh, in_specs=in_specs, out_specs=out_specs, check_vma=False)
```

time: 349 us -> 135 us (0.39); the launches traced: 344 us -> 135 us
  matrix products: 120 us -> 0.9 us
  other arithmetic: 67.5 us -> 0.84 us
  local copies, waits for them, and re-layouts: 67.1 us -> 4.83 us
  blocking collectives: 0 us -> 32 us
  Pallas kernels: 0 us -> 31.5 us
  starting transfers between devices: 44.8 us -> 19.9 us
    dot_general x108 -> x1, matrix products: 118 us -> 0.9 us  [local(): jnp.dot(row_in.T, col_in, preferred_element_type=jnp.float32)]
    another operation x23 -> x1, other arithmetic: 34.8 us -> 0.01 us  [local(): table = jnp.stack([stamp_row[0] + my_first, stamp_col[0], live_here])]
    all_to_all x0 -> x2, blocking collectives: none -> 32 us  [the longest x1 25.7 us: local(): lax.all_to_all(sent_cell.reshape(patches, 2), 'patch', split_axis=0, conc...]
    pallas_call x0 -> x4, Pallas kernels: none -> 31.5 us  [the longest x1 13.9 us: local(): pl.pallas_call(gram_kernel, out_shape=(shape(NB, CE, CW), shape(2 * XR, 1...]
    all_to_all x5 -> x1, starting transfers between devices: 27.7 us -> 4.83 us  [local(): lax.all_to_all(sent.reshape(patches, 4 * CR, CW), 'patch', split_axis=0,...]
    unnamed x136 -> x10, local copies, waits for them, and re-layouts: 18 us -> 2 us
    another operation x11 -> x0, local copies, waits for them, and re-layouts: 14.1 us -> none  [the longest x3 8.65 us: local(): jnp.stack([jnp.dot(basis_rows[row_tap], filtered[col_tap], precision=HIGH...]
    unnamed x27 -> x0, other arithmetic: 13.1 us -> none
  transfers between devices with their start and end apart: 11 -> 5, of which waited for: 2 -> 3; matrix products, arithmetic and copies ran while one was open for 26% -> 2% of each run, Pallas kernels for 0% -> 0%
where the time goes in v1:
time: 135 us
  waiting for transfers between devices  43.5 us (32%)
  blocking collectives  32 us (24%)
  Pallas kernels  31.5 us (23%)
  starting transfers between devices  19.9 us (15%)
  local copies, waits for them, and re-layouts  4.83 us (4%)
  between operations  1.42 us (1%)
    all_to_all x1, waiting for transfers between devices, local(): lax.all_to_all(sent.reshape(patches, 4 * CR, CW), 'patch', split_axis=0,...  38.6 us
    all_to_all x1, blocking collectives, local(): lax.all_to_all(sent_cell.reshape(patches, 2), 'patch', split_axis=0, conc...  25.7 us
    pallas_call x1, Pallas kernels, local(): pl.pallas_call(gram_kernel, out_shape=(shape(NB, CE, CW), shape(2 * XR, 1...  13.9 us
    pallas_call x1, Pallas kernels, local(): pl.pallas_call(functools.partial(final_kernel, normalizer), out_shape=(fi...  9.94 us
    ppermute x1, starting transfers between devices, local(): above = lax.ppermute(down, 'sub', down_pairs)  6.98 us
    all_to_all x1, blocking collectives, local(): lax.all_to_all(copies, 'sub', split_axis=0, concat_axis=0, tiled=True)  6.24 us
    all_to_all x1, starting transfers between devices, local(): lax.all_to_all(sent.reshape(patches, 4 * CR, CW), 'patch', split_axis=0,...  4.83 us
    ppermute x1, starting transfers between devices, local(): lax.ppermute(table, 'sub', up_pairs)  4.01 us
  transfers between devices with their start and end apart: 5, of which 3 were waited for; matrix products, arithmetic and copies ran while one was open for 2% of the time, Pallas kernels for 0%

profile of v1, /device:TPU:1, one launch (start us, length us, event | category | flops | bytes accessed | tf_op | source)
XLA Modules:
  0.0 134.8 jit_solution(2956299777532661205)
XLA Ops:
  0.6 3.9 %pack.1 = (f32[128,16,256]{2,1,0:T(8,128)}, s32[128]{0:T(128)}) custom-call(s32[32]{0:T(128)} %bitcast.27, s32[32]{0:T(128)} %bitcast.28, f32[32,8,256]{2,1,0:T(8,128)} %bitcast.24, f32[32,8,256]{2,1,0:T(8,128)} %bitcast.25), custom_call_target="tpu_custom_call" | custom-call | tf_op jit(solution)/shard_map/pack/pallas_call | solution.py:404
  4.5 0.8 all_to_all.12
  5.3 25.7 %all_to_all.19 = s32[64,1,2]{2,1,0:T(1,128)S(1)} all-to-all(s32[64,1,2]{2,1,0:T(1,128)S(1)} %bitcast.26), channel_id=1, replica_groups=mesh['patch'=64,'sub'=4] {'patch'}, dimensions={0} | all-to-all | bytes 1024 | tf_op jit(solution)/shard_map/all_to_all | solution.py:413
  31.1 0.0 copy-start.4
  31.1 0.0 copy-start.3
  31.1 4.8 %all-to-all-start.1 = ((f32[64,32,256]{2,1,0:T(8,128)}), f32[64,32,256]{2,1,0:T(8,128)S(1)}, u32[]{:S(2)}, u32[]{:S(2)}) async-start(f32[64,32,256]{2,1,0:T(8,128)} %bitcast.23), calls=%async_computation.1 | async-start | bytes 4194304 | tf_op jit(solution)/shard_map/all_to_all | solution.py:416
  36.6 0.0 copy-done.4
  36.6 0.0 copy-done.3
  36.6 4.0 %collective-permute-start.3 = (s32[3,12]{1,0:T(4,128)S(1)}, s32[3,12]{1,0:T(4,128)S(1)}, u32[]{:S(2)}, u32[]{:S(2)}) collective-permute-start(s32[3,12]{1,0:T(4,128)S(1)} %pad_add_fusion), channel_id=1, source_target_pairs={{1,0},{2,1},{3,2},{5,4},{6,5},{7,6},{9,8},{10,9},{11,10},{13,12},{... | collective-permute-start | bytes 440 | tf_op jit(solution)/shard_map/ppermute | solution.py:395
  40.7 2.1 %collective-permute-start.2 = (s32[3,12]{1,0:T(4,128)S(1)}, s32[3,12]{1,0:T(4,128)S(1)}, u32[]{:S(2)}, u32[]{:S(2)}) collective-permute-start(s32[3,12]{1,0:T(4,128)S(1)} %pad_add_fusion), channel_id=1, source_target_pairs={{0,1},{1,2},{2,3},{4,5},{5,6},{6,7},{8,9},{9,10},{10,11},{12,13},{... | collective-permute-start | bytes 440 | tf_op jit(solution)/shard_map/ppermute | solution.py:395
  42.8 0.0 collective-permute-done.3
  42.8 0.9 collective-permute-done.2
  43.7 0.1 pad_add_fusion.1
  43.8 0.5 broadcast.22
  44.3 0.7 reduce.3
  45.1 0.7 reshape.55.cells
  45.8 38.6 %all-to-all-done.1 = f32[64,32,256]{2,1,0:T(8,128)S(1)} async-done(((f32[64,32,256]{2,1,0:T(8,128)}), f32[64,32,256]{2,1,0:T(8,128)S(1)}, u32[]{:S(2)}, u32[]{:S(2)}) %all-to-all-start.1) | async-done | bytes 2097184 | tf_op jit(solution)/shard_map/all_to_all | solution.py:416
  84.4 0.0 copy-start
  84.4 1.3 copy-done
  85.7 3.8 %combine.1 = (f32[4,64,256]{2,1,0:T(8,128)}, f32[4,64,256]{2,1,0:T(8,128)}, f32[64,256]{1,0:T(8,128)}, f32[152,256]{1,0:T(8,128)}, f32[152,256]{1,0:T(8,128)}) custom-call(s32[128]{0:T(128)} %reshape.55.cells, s32[4]{0:T(128)} %warp.1, f32[128,16,256]{2,1,0:T(8,128)} %bitcast.22), custom_call_target="tpu_custom_call" | custom-call | tf_op jit(solution)/shard_map/combine/pallas_call | solution.py:420
  89.5 7.0 %collective-permute-start = (f32[152,256]{1,0:T(8,128)}, f32[152,256]{1,0:T(8,128)S(1)}, u32[]{:S(2)}, u32[]{:S(2)}) collective-permute-start(f32[152,256]{1,0:T(8,128)} %get-tuple-element.18), channel_id=1, source_target_pairs={{0,1},{1,2},{2,3},{4,5},{5,6},{6,7},{8,9},{9,10},{10,11},{12,13},{... | collective-permute-start | bytes 466952 | tf_op jit(solution)/shard_map/ppermute | solution.py:429
  96.5 1.9 %collective-permute-start.1 = (f32[152,256]{1,0:T(8,128)}, f32[152,256]{1,0:T(8,128)S(1)}, u32[]{:S(2)}, u32[]{:S(2)}) collective-permute-start(f32[152,256]{1,0:T(8,128)} %get-tuple-element.19), channel_id=1, source_target_pairs={{1,0},{2,1},{3,2},{5,4},{6,5},{7,6},{9,8},{10,9},{11,10},{13,12},{... | collective-permute-start | bytes 466952 | tf_op jit(solution)/shard_map/ppermute | solution.py:430
  98.4 0.9 convolution_minimum_fusion.mask
  99.3 0.0 collective-permute-done.above
  99.3 0.0 copy-start.1
  99.3 3.9 %collective-permute-done.1.below = f32[152,256]{1,0:T(8,128)S(1)} collective-permute-done((f32[152,256]{1,0:T(8,128)}, f32[152,256]{1,0:T(8,128)S(1)}, u32[]{:S(2)}, u32[]{:S(2)}) %collective-permute-start.1) | collective-permute-done | bytes 155680 | tf_op jit(solution)/shard_map/ppermute | solution.py:430
  103.2 0.0 copy-start.2
  103.2 0.0 copy-done.1
  103.3 0.7 copy-done.2
  103.9 13.9 %gram.1 = (f32[40,96,256]{2,1,0:T(8,128)}, f32[96,128]{1,0:T(8,128)}) custom-call(f32[4,64,256]{2,1,0:T(8,128)} %get-tuple-element.15.science, f32[4,64,256]{2,1,0:T(8,128)} %get-tuple-element.16.variance, f32[64,256]{1,0:T(8,128)} %get-tuple-element.17.template, f32[152,256]{1,0:T(8,128)} %copy-done.1, f32[152,256]{1,0:T(8,128)} %copy-done.2, ...), custom_call_target="tpu_custom_call" | custom-call | tf_op jit(solution)/shard_map/gram/pallas_call | solution.py:433
  117.8 0.8 broadcast_in_dim.11
  118.7 6.2 %all_to_all.20.gathered = f32[4,96,128]{2,1,0:T(8,128)} all-to-all(f32[4,96,128]{2,1,0:T(8,128)S(1)} %broadcast_in_dim.11), channel_id=1, replica_groups=mesh['patch'=64,'sub'=4] {'sub'}, dimensions={0} | all-to-all | bytes 393216 | tf_op jit(solution)/shard_map/all_to_all | solution.py:450
  124.9 9.9 %final.1 = (f32[4,64,256]{2,1,0:T(8,128)}, f32[4,64,256]{2,1,0:T(8,128)}) custom-call(s32[1]{0:T(128)} %bitcast.sub, f32[4,96,128]{2,1,0:T(8,128)} %all_to_all.20.gathered, f32[40,96,256]{2,1,0:T(8,128)} %get-tuple-element.21.basis, f32[4,64,256]{2,1,0:T(8,128)} %get-tuple-element.15.science, f32[4,64,256]{2,1,0:T(8,128)} %get-tuple-element.16.variance, ...), custom_call_target="tpu_custom_call" | custom-call | tf_op jit(solution)/shard_map/final/pallas_call | solution.py:453
  (6 shorter events, 0.0 us)
Async XLA Ops:
  31.1 5.5 %copy-start.4 = (s32[1,12]{1,0:T(1,128)S(1)}, s32[1,12]{1,0:T(1,128)}, u32[]{:S(2)}) copy-start(s32[1,12]{1,0:T(1,128)} %param.15) | copy-start | bytes 148
  31.1 5.5 %copy-start.3 = (s32[1,12]{1,0:T(1,128)S(1)}, s32[1,12]{1,0:T(1,128)}, u32[]{:S(2)}) copy-start(s32[1,12]{1,0:T(1,128)} %param.16) | copy-start | bytes 148
  31.1 53.3 %all-to-all-start.1 = ((f32[64,32,256]{2,1,0:T(8,128)}), f32[64,32,256]{2,1,0:T(8,128)S(1)}, u32[]{:S(2)}, u32[]{:S(2)}) async-start(f32[64,32,256]{2,1,0:T(8,128)} %bitcast.23), calls=%async_computation.1 | async-start | bytes 4194304 | tf_op jit(solution)/shard_map/all_to_all | solution.py:416
  36.6 6.2 %collective-permute-start.3 = (s32[3,12]{1,0:T(4,128)S(1)}, s32[3,12]{1,0:T(4,128)S(1)}, u32[]{:S(2)}, u32[]{:S(2)}) collective-permute-start(s32[3,12]{1,0:T(4,128)S(1)} %pad_add_fusion), channel_id=1, source_target_pairs={{1,0},{2,1},{3,2},{5,4},{6,5},{7,6},{9,8},{10,9},{11,10},{13,12},{... | collective-permute-start | bytes 440 | tf_op jit(solution)/shard_map/ppermute | solution.py:395
  40.7 3.1 %collective-permute-start.2 = (s32[3,12]{1,0:T(4,128)S(1)}, s32[3,12]{1,0:T(4,128)S(1)}, u32[]{:S(2)}, u32[]{:S(2)}) collective-permute-start(s32[3,12]{1,0:T(4,128)S(1)} %pad_add_fusion), channel_id=1, source_target_pairs={{0,1},{1,2},{2,3},{4,5},{5,6},{6,7},{8,9},{9,10},{10,11},{12,13},{... | collective-permute-start | bytes 440 | tf_op jit(solution)/shard_map/ppermute | solution.py:395
  84.4 1.3 copy-start
  89.5 9.8 %collective-permute-start = (f32[152,256]{1,0:T(8,128)}, f32[152,256]{1,0:T(8,128)S(1)}, u32[]{:S(2)}, u32[]{:S(2)}) collective-permute-start(f32[152,256]{1,0:T(8,128)} %get-tuple-element.18), channel_id=1, source_target_pairs={{0,1},{1,2},{2,3},{4,5},{5,6},{6,7},{8,9},{9,10},{10,11},{12,13},{... | collective-permute-start | bytes 466952 | tf_op jit(solution)/shard_map/ppermute | solution.py:429
  96.5 6.8 %collective-permute-start.1 = (f32[152,256]{1,0:T(8,128)}, f32[152,256]{1,0:T(8,128)S(1)}, u32[]{:S(2)}, u32[]{:S(2)}) collective-permute-start(f32[152,256]{1,0:T(8,128)} %get-tuple-element.19), channel_id=1, source_target_pairs={{1,0},{2,1},{3,2},{5,4},{6,5},{7,6},{9,8},{10,9},{11,10},{13,12},{... | collective-permute-start | bytes 466952 | tf_op jit(solution)/shard_map/ppermute | solution.py:430
  99.3 3.9 %copy-start.1 = (f32[152,256]{1,0:T(8,128)}, f32[152,256]{1,0:T(8,128)S(1)}, u32[]{:S(2)}) copy-start(f32[152,256]{1,0:T(8,128)S(1)} %collective-permute-done.above) | copy-start | bytes 466948
  103.2 0.7 copy-start.2

commit v2 on v1

--- a/solution.py
+++ b/solution.py
@@ -26,7 +26,7 @@
 SKY_VAR = 0.1
 RIDGE = 0.5
 EPS = 1e-05
-HIGH = lax.Precision.HIGHEST
+MESH = pl.DeviceIdType.MESH
 
 NT = 14
 XR = 48
@@ -34,8 +34,8 @@
 CE = 96
 TH = 24
 SR = 16
-HALO = TH + 2 * V * SR
-VMEM_LIMIT = 56 * 1024 * 1024
+HALO = TH + V * SR
+VMEM_LIMIT = 16 * 1024 * 1024
 WHOLE = pl.BlockSpec(memory_space=pltpu.VMEM)
 SCALARS = pl.BlockSpec(memory_space=pltpu.SMEM)
 
@@ -115,39 +115,126 @@
     return jnp.dot(a, b, preferred_element_type=jnp.float32)
 
 
-def pack_kernel(patch, cell, image, variance, out, out_cell, count):
+def pack_kernel(patch, cell, image, variance, out_image, out_variance, out_cell, count, slot_cell):
+    patches = out_image.shape[0]
+
     def clear(n, _):
-        out_cell[n] = -1
-        return 0
-
-    def clear_count(n, _):
         count[n] = 0
-        return 0
-
-    slots = out.shape[0]
-    lax.fori_loop(0, slots, clear, 0)
-    lax.fori_loop(0, slots // 2, clear_count, 0)
+        slot_cell[2 * n] = -1
+        slot_cell[2 * n + 1] = -1
+        return 0
+
+    lax.fori_loop(0, patches, clear, 0)
 
     def place(n, _):
         q = patch[n]
         rank = count[q]
         count[q] = rank + 1
-        slot = 2 * q + rank
-        out_cell[slot] = cell[n]
-        out[slot, 0:CR, :] = image[n]
-        out[slot, CR : 2 * CR, :] = variance[n]
+        slot_cell[2 * q + rank] = cell[n]
+        rows = pl.ds(pl.multiple_of(rank * CR, CR), CR)
+        out_image[q, rows, :] = image[n]
+        out_variance[q, rows, :] = variance[n]
         return 0
 
     lax.fori_loop(0, image.shape[0], place, 0)
-
-
-def combine_kernel(cells, warp, got, science, variance, template, up, down, acc):
+    lane = lax.broadcasted_iota(jnp.int32, (1, 128), 1)
+
+    def tell(q, _):
+        out_cell[q] = jnp.where(lane == 0, slot_cell[2 * q], slot_cell[2 * q + 1])
+        return 0
+
+    lax.fori_loop(0, patches, tell, 0)
+
+
+def exchange_kernel(cells, stamps, got_cells, got_stamps, send, recv, ring_send, ring_recv, own):
+    patches = cells.shape[0]
+    subtiles = lax.axis_size("sub")
+    me, sub = lax.axis_index("patch"), lax.axis_index("sub")
+    right, left = lax.rem(sub + 1, subtiles), lax.rem(sub + subtiles - 1, subtiles)
+    barrier = pltpu.get_barrier_semaphore()
+
+    def greet(d, _):
+        q = lax.rem(me + d, patches)
+        pl.semaphore_signal(barrier, inc=1, device_id={"patch": q}, device_id_type=MESH)
+        return 0
+
+    lax.fori_loop(1, patches, greet, 0)
+    for s in (left, right):
+        pl.semaphore_signal(barrier, inc=1, device_id={"sub": s}, device_id_type=MESH)
+    pl.semaphore_wait(barrier, patches + 1)
+
+    def copy(d, to, at):
+        return pltpu.make_async_remote_copy(
+            src_ref=cells.at[to], dst_ref=got_cells.at[at], send_sem=send.at[d],
+            recv_sem=recv.at[d], device_id={"patch": to}, device_id_type=MESH,
+        )
+
+    def start(d, _):
+        copy(d, lax.rem(me + d, patches), me).start()
+        return 0
+
+    lax.fori_loop(1, patches, start, 0)
+    rings = [
+        pltpu.make_async_remote_copy(
+            src_ref=stamps, dst_ref=got_stamps.at[n], send_sem=ring_send.at[n],
+            recv_sem=ring_recv.at[n], device_id={"sub": to}, device_id_type=MESH,
+        )
+        for n, to in enumerate((right, left))
+    ]
+    for ring in rings:
+        ring.start()
+    mine = pltpu.make_async_copy(cells.at[me], got_cells.at[me], own)
+    mine.start()
+    mine.wait()
+
+    def finish(d, _):
+        copy(d, lax.rem(me + d, patches), me).wait_send()
+        source = lax.rem(me + patches - d, patches)
+        copy(d, source, source).wait_recv()
+        return 0
+
+    lax.fori_loop(1, patches, finish, 0)
+    for ring in rings:
+        ring.wait()
+
+
+def gather_kernel(part, gathered, send, recv, own):
+    subtiles = gathered.shape[0]
+    sub = lax.axis_index("sub")
+    peers = [lax.rem(sub + d, subtiles) for d in range(1, subtiles)]
+    barrier = pltpu.get_barrier_semaphore()
+    for s in peers:
+        pl.semaphore_signal(barrier, inc=1, device_id={"sub": s}, device_id_type=MESH)
+    pl.semaphore_wait(barrier, subtiles - 1)
+    copies = [
+        pltpu.make_async_remote_copy(
+            src_ref=part, dst_ref=gathered.at[sub], send_sem=send.at[n], recv_sem=recv.at[n],
+            device_id={"sub": s}, device_id_type=MESH,
+        )
+        for n, s in enumerate(peers)
+    ]
+    for copy in copies:
+        copy.start()
+    mine = pltpu.make_async_copy(part, gathered.at[sub], own)
+    mine.start()
+    mine.wait()
+    for n, copy in enumerate(copies):
+        copy.wait_send()
+        source = lax.rem(sub + subtiles - 1 - n, subtiles)
+        pltpu.make_async_remote_copy(
+            src_ref=part, dst_ref=gathered.at[source], send_sem=send.at[n], recv_sem=recv.at[n],
+            device_id={"sub": source}, device_id_type=MESH,
+        ).wait_recv()
+
+
+def combine(cells, warp, got, out, acc):
     acc[...] = jnp.zeros_like(acc)
 
-    def add(n, _):
-        c = cells[n]
-        c = jnp.where(c < 0, V * NCELL, c)
-        acc[c] += got[n]
+    def add(q, _):
+        for rank in range(2):
+            c = cells[q, 0, rank]
+            c = jnp.where(c < 0, V * NCELL, c)
+            acc[c] += got[q, rank * CR : (rank + 1) * CR, :]
         return 0
 
     lax.fori_loop(0, got.shape[0], add, 0)
@@ -158,26 +245,32 @@
         source = col + (off - WARP)
         inside = (source >= 0) & (source < CW)
         for c in range(NCELL):
-            rows = slice(c * CR, (c + 1) * CR)
-            a = acc[v * NCELL + c, 0:CR, :]
-            b = acc[v * NCELL + c, CR : 2 * CR, :]
-            science[v, rows, :] = jnp.where(inside, pltpu.roll(a, turn, 1), 0.0)
-            variance[v, rows, :] = jnp.where(inside, pltpu.roll(b, turn, 1), 0.0)
+            a = acc[v * NCELL + c]
+            out[v, c * CR : (c + 1) * CR, :] = jnp.where(inside, pltpu.roll(a, turn, 1), 0.0)
+
+
+def image_kernel(cells, warp, got, science, template, up, down, acc):
+    combine(cells, warp, got, science, acc)
     template[...] = (science[0] + science[1] + science[2] + science[3]) / V
     up[0:TH, :] = template[0:TH, :]
     down[0:TH, :] = template[RT - TH : RT, :]
     for v in range(V):
-        s_at, w_at = TH + v * SR, TH + (V + v) * SR
-        up[s_at : s_at + SR, :] = science[v, 0:SR, :]
-        up[w_at : w_at + SR, :] = variance[v, 0:SR, :]
-        down[s_at : s_at + SR, :] = science[v, RT - SR : RT, :]
-        down[w_at : w_at + SR, :] = variance[v, RT - SR : RT, :]
-
-
-def gram_kernel(
-    science, variance, template, above, below, mask, row_bands,
-    basis, gram, text, filt, xleft, xright, weight, acc,
+        at = TH + v * SR
+        up[at : at + SR, :] = science[v, 0:SR, :]
+        down[at : at + SR, :] = science[v, RT - SR : RT, :]
+
+
+def variance_kernel(cells, warp, got, token, variance, up, down, acc):
+    combine(cells, warp, got, variance, acc)
+    for v in range(V):
+        up[v * SR : (v + 1) * SR, :] = variance[v, 0:SR, :]
+        down[v * SR : (v + 1) * SR, :] = variance[v, RT - SR : RT, :]
+
+
+def basis_kernel(
+    science, template, above, below, row_bands, basis, xleft, xright, token, text, filt,
 ):
+    token[...] = jnp.zeros_like(token)
     taps = tap_values()
 
     def put(k, image):
@@ -236,6 +329,8 @@
     for n in range(NB + 1 + V, XR):
         put(n, jnp.zeros((RT, CW), jnp.float32))
 
+
+def gram_kernel(variance, mask, xleft, xright, gram, weight, acc):
     q = (variance[0] + variance[1] + variance[2] + variance[3]) / (V * V)
     m = mask[...]
     for v in range(V):
@@ -278,7 +373,7 @@
 
 
 def final_kernel(
-    normalizer, sub, gathered, basis, science, variance, above, below, cols, rows,
+    normalizer, sub, gathered, basis, science, variance, s_above, s_below, w_above, w_below, cols, rows,
     difference, significance, coef, dplane, iplane,
 ):
     total = gathered[0] + gathered[1] + gathered[2] + gathered[3]
@@ -325,13 +420,13 @@
         top = jnp.clip(b, 0, 1) * 8
         low = jnp.clip(b - 10, 0, 1) * 8
 
-        def pull(own, first, v):
+        def pull(own, above, below, first, v):
             at_a = pl.ds(pl.multiple_of(first + v * SR + top, 8), 8)
             at_b = pl.ds(pl.multiple_of(first + v * SR + low, 8), 8)
             return jnp.where(edge_a, above[at_a, :], jnp.where(edge_b, below[at_b, :], own[v, inner, :]))
 
-        s = [pull(science, TH, v) for v in range(V)]
-        w = [pull(variance, TH + V * SR, v) for v in range(V)]
+        s = [pull(science, s_above, s_below, TH, v) for v in range(V)]
+        w = [pull(variance, w_above, w_below, 0, v) for v in range(V)]
         q = (w[0] + w[1] + w[2] + w[3]) / (V * V)
         acc = [s[v] - jnp.concatenate([coef[v * XR + NB : v * XR + NB + 1, :]] * 2, axis=1) for v in range(V)]
         for k in range(NB):
@@ -372,8 +467,12 @@
     return jax.ShapeDtypeStruct(dims, dtype)
 
 
-def params():
-    return pltpu.CompilerParams(vmem_limit_bytes=VMEM_LIMIT)
+def params(**more):
+    return pltpu.CompilerParams(vmem_limit_bytes=VMEM_LIMIT, **more)
+
+
+def costs(us):
+    return pl.CostEstimate(flops=int(us * 1e8), bytes_accessed=int(us * 2e6), transcendentals=0)
 
 
 def local(
@@ -382,78 +481,127 @@
 ):
     patches = lax.axis_size("patch")
     subtiles = lax.axis_size("sub")
-    slot_total = 2 * patches
     me = lax.axis_index("sub")
     up_pairs = [(i + 1, i) for i in range(subtiles - 1)]
     down_pairs = [(i, i + 1) for i in range(subtiles - 1)]
-
     slots = stamp_row.shape[1]
-    my_first = me * RT
-    live_here = (jnp.arange(slots) < stamp_count[0, 0]).astype(jnp.int32)
-    table = jnp.stack([stamp_row[0] + my_first, stamp_col[0], live_here])
-    near = jnp.concatenate(
-        [lax.ppermute(table, "sub", down_pairs), table, lax.ppermute(table, "sub", up_pairs)], axis=1
-    )
-    my_rows = my_first + jnp.arange(RT)
-    row_in = (
-        (jnp.abs(my_rows[None, :] - near[0][:, None]) <= SH) & (near[2][:, None] > 0)
-    ).astype(jnp.bfloat16)
-    col_in = (jnp.abs(jnp.arange(CW)[None, :] - near[1][:, None]) <= SH).astype(jnp.bfloat16)
-    mask = jnp.minimum(jnp.dot(row_in.T, col_in, preferred_element_type=jnp.float32), 1.0)
-
-    sent, sent_cell = pl.pallas_call(
+    dma = pltpu.SemaphoreType.DMA
+
+    half = shape(patches, 2 * CR, CW)
+    sent_image, sent_variance, sent_cell = pl.pallas_call(
         pack_kernel,
-        out_shape=(shape(slot_total, 2 * CR, CW), shape(slot_total, dtype=jnp.int32)),
+        out_shape=(half, half, shape(patches, 1, 128, dtype=jnp.int32)),
         in_specs=[SCALARS, SCALARS, WHOLE, WHOLE],
-        out_specs=(WHOLE, SCALARS),
-        scratch_shapes=[pltpu.SMEM((patches,), jnp.int32)],
+        out_specs=(WHOLE,) * 3,
+        scratch_shapes=[pltpu.SMEM((patches,), jnp.int32), pltpu.SMEM((2 * patches,), jnp.int32)],
         compiler_params=params(),
         name="pack",
     )(piece_patch.reshape(-1), piece_cell.reshape(-1), pieces_image[0], pieces_variance[0])
-    got_cell = lax.all_to_all(
-        sent_cell.reshape(patches, 2), "patch", split_axis=0, concat_axis=0, tiled=True
+
+    table = jnp.concatenate(
+        [stamp_row, stamp_col, stamp_count, jnp.zeros((1, 127 - 2 * slots), jnp.int32)], axis=1
     )
-    got = lax.all_to_all(
-        sent.reshape(patches, 4 * CR, CW), "patch", split_axis=0, concat_axis=0, tiled=True
+    got_cell, got_stamps = pl.pallas_call(
+        exchange_kernel,
+        out_shape=(shape(patches, 1, 128, dtype=jnp.int32), shape(2, 1, 128, dtype=jnp.int32)),
+        in_specs=[WHOLE] * 2,
+        out_specs=(WHOLE,) * 2,
+        scratch_shapes=[dma((patches,)), dma((patches,)), dma((2,)), dma((2,)), dma],
+        compiler_params=params(collective_id=0, has_side_effects=True),
+        name="exchange",
+    )(sent_cell, table)
+    sent_image, sent_variance, got_cell, got_stamps = lax.optimization_barrier(
+        (sent_image, sent_variance, got_cell, got_stamps)
     )
+    got_image = lax.all_to_all(sent_image, "patch", split_axis=0, concat_axis=0, tiled=True)
+    got_variance = lax.all_to_all(sent_variance, "patch", split_axis=0, concat_axis=0, tiled=True)
+
+    near = jnp.concatenate([got_stamps[0], table, got_stamps[1]], axis=0)
+    shift = jnp.arange(-1, 2)[:, None]
+    present = (me + shift >= 0) & (me + shift < subtiles)
+    centre_row = (near[:, 0:slots] + shift * RT).reshape(-1)
+    centre_col = near[:, slots : 2 * slots].reshape(-1)
+    live = (present & (jnp.arange(slots)[None, :] < near[:, 2 * slots : 2 * slots + 1])).reshape(-1)
+    row_in = ((jnp.abs(jnp.arange(RT)[None, :] - centre_row[:, None]) <= SH) & live[:, None]).astype(
+        jnp.bfloat16
+    )
+    col_in = (jnp.abs(jnp.arange(CW)[None, :] - centre_col[:, None]) <= SH).astype(jnp.bfloat16)
+    mask = jnp.minimum(jnp.dot(row_in.T, col_in, preferred_element_type=jnp.float32), 1.0)
+
     field = shape(V, RT, CW)
-    science, variance, template, up, down = pl.pallas_call(
-        combine_kernel,
-        out_shape=(field, field, shape(RT, CW), shape(HALO, CW), shape(HALO, CW)),
+    cells_acc = [pltpu.VMEM((V * NCELL + 1, CR, CW), jnp.float32)]
+    rim = shape(HALO, CW)
+    science, template, up, down = pl.pallas_call(
+        image_kernel,
+        out_shape=(field, shape(RT, CW), rim, rim),
         in_specs=[SCALARS, SCALARS, WHOLE],
-        out_specs=(WHOLE,) * 5,
-        scratch_shapes=[pltpu.VMEM((V * NCELL + 1, 2 * CR, CW), jnp.float32)],
+        out_specs=(WHOLE,) * 4,
+        scratch_shapes=cells_acc,
         compiler_params=params(),
-        name="combine",
-    )(got_cell.reshape(-1), warp_offsets, got.reshape(slot_total, 2 * CR, CW))
-    above = lax.ppermute(down, "sub", down_pairs)
-    below = lax.ppermute(up, "sub", up_pairs)
+        cost_estimate=costs(3),
+        name="image",
+    )(got_cell, warp_offsets, got_image)
+    s_above = lax.ppermute(down, "sub", down_pairs)
+    s_below = lax.ppermute(up, "sub", up_pairs)
 
     row_bands, cols, rows = constants()
-    basis, gram = pl.pallas_call(
-        gram_kernel,
-        out_shape=(shape(NB, CE, CW), shape(2 * XR, 128)),
-        in_specs=[WHOLE] * 7,
-        out_specs=(WHOLE,) * 2,
+    half_rows = shape(RT * XR, 128)
+    basis, xleft, xright, token = pl.pallas_call(
+        basis_kernel,
+        out_shape=(shape(NB, CE, CW), half_rows, half_rows, shape(8, 128)),
+        in_specs=[WHOLE] * 5,
+        out_specs=(WHOLE,) * 4,
         scratch_shapes=[
             pltpu.VMEM((TE, CW), jnp.float32),
             pltpu.VMEM((NT, TE, CW), jnp.float32),
-            pltpu.VMEM((RT * XR, 128), jnp.float32),
-            pltpu.VMEM((RT * XR, 128), jnp.float32),
+        ],
+        compiler_params=params(),
+        cost_estimate=costs(8),
+        name="basis",
+    )(science, template, s_above, s_below, jnp.asarray(row_bands))
+
+    rim = shape(V * SR, CW)
+    variance, up, down = pl.pallas_call(
+        variance_kernel,
+        out_shape=(field, rim, rim),
+        in_specs=[SCALARS, SCALARS, WHOLE, WHOLE],
+        out_specs=(WHOLE,) * 3,
+        scratch_shapes=cells_acc,
+        compiler_params=params(),
+        cost_estimate=costs(3),
+        name="variance",
+    )(got_cell, warp_offsets, got_variance, token)
+    w_above = lax.ppermute(down, "sub", down_pairs)
+    w_below = lax.ppermute(up, "sub", up_pairs)
+
+    gram = pl.pallas_call(
+        gram_kernel,
+        out_shape=shape(2 * XR, 128),
+        in_specs=[WHOLE] * 4,
+        out_specs=WHOLE,
+        scratch_shapes=[
             pltpu.VMEM((V, RT, CW), jnp.float32),
             pltpu.VMEM((2 * V * XR, 128), jnp.float32),
         ],
         compiler_params=params(),
+        cost_estimate=costs(7),
         name="gram",
-    )(science, variance, template, above, below, mask, jnp.asarray(row_bands))
-    copies = jnp.broadcast_to(gram, (subtiles, *gram.shape))
-    gathered = lax.all_to_all(copies, "sub", split_axis=0, concat_axis=0, tiled=True)
+    )(variance, mask, xleft, xright)
+    gathered = pl.pallas_call(
+        gather_kernel,
+        out_shape=shape(subtiles, 2 * XR, 128),
+        in_specs=[WHOLE],
+        out_specs=WHOLE,
+        scratch_shapes=[dma((subtiles - 1,)), dma((subtiles - 1,)), dma],
+        compiler_params=params(collective_id=1, has_side_effects=True),
+        name="gather",
+    )(gram)
 
     normalizer = float(subtiles * slots * (2 * SH + 1) ** 2)
     difference, significance = pl.pallas_call(
         functools.partial(final_kernel, normalizer),
         out_shape=(field, field),
-        in_specs=[SCALARS] + [WHOLE] * 8,
+        in_specs=[SCALARS] + [WHOLE] * 10,
         out_specs=(WHOLE,) * 2,
         scratch_shapes=[
             pltpu.VMEM((V * XR, 128), jnp.float32),
@@ -461,10 +609,11 @@
             pltpu.VMEM((V * CE, CW), jnp.float32),
         ],
         compiler_params=params(),
+        cost_estimate=costs(10),
         name="final",
     )(
-        me.reshape(1).astype(jnp.int32), gathered, basis, science, variance, above, below,
-        jnp.asarray(cols), jnp.asarray(rows),
+        me.reshape(1).astype(jnp.int32), gathered, basis, science, variance, s_above, s_below,
+        w_above, w_below, jnp.asarray(cols), jnp.asarray(rows),
     )
     return (difference[:, None], significance[:, None])
 

time: 135 us -> 130 us (0.963)
  waiting for transfers between devices: 43.5 us -> 8.09 us
  Pallas kernels: 31.5 us -> 49.2 us
  blocking collectives: 32 us -> 36.5 us
  starting transfers between devices: 19.9 us -> 23.7 us
  local copies, waits for them, and re-layouts: 4.83 us -> 8.11 us
    all_to_all x1, waiting for transfers between devices: 38.6 us -> 3.4 us  [local(): lax.all_to_all(sent_variance, 'patch', split_axis=0, concat_axis=0, tiled...]
    pallas_call x3 -> x7, Pallas kernels: 21.6 us -> 41.7 us  [the longest x1 18.1 us: local(): pl.pallas_call(exchange_kernel, out_shape=(shape(patches, 1, 128, dtype=j...]
    unnamed x10 -> x30, local copies, waits for them, and re-layouts: 2 us -> 7.67 us
    all_to_all x2 -> x1, blocking collectives: 32 us -> 36.5 us  [local(): lax.all_to_all(sent_image, 'patch', split_axis=0, concat_axis=0, tiled=True)]
    all_to_all x1, starting transfers between devices: 4.83 us -> 8.79 us  [local(): lax.all_to_all(sent_variance, 'patch', split_axis=0, concat_axis=0, tiled...]
    pallas_call x1, Pallas kernels: 9.94 us -> 7.52 us  [local(): pl.pallas_call(functools.partial(final_kernel, normalizer), out_shape=(fi...]
  transfers between devices with their start and end apart: 5 -> 5, of which waited for: 3 -> 2; matrix products, arithmetic and copies ran while one was open for 2% -> 1% of each run, Pallas kernels for 0% -> 14%
where the time goes in v2:
time: 130 us; the launch traced here: 129 us
  Pallas kernels  49.2 us (38%)
  blocking collectives  36.5 us (28%)
  starting transfers between devices  23.7 us (18%)
  local copies, waits for them, and re-layouts  8.11 us (6%)
  waiting for transfers between devices  8.09 us (6%)
  between operations  1.49 us (1%)
    all_to_all x1, blocking collectives, local(): lax.all_to_all(sent_image, 'patch', split_axis=0, concat_axis=0, tiled=True)  36.5 us
    pallas_call x1, Pallas kernels, local(): pl.pallas_call(exchange_kernel, out_shape=(shape(patches, 1, 128, dtype=j...  18.1 us
    all_to_all x1, starting transfers between devices, local(): lax.all_to_all(sent_variance, 'patch', split_axis=0, concat_axis=0, tiled...  8.79 us
    unnamed x30, local copies, waits for them, and re-layouts  7.67 us
    pallas_call x1, Pallas kernels, local(): pl.pallas_call(functools.partial(final_kernel, normalizer), out_shape=(fi...  7.52 us
    ppermute x1, starting transfers between devices, local(): w_above = lax.ppermute(down, 'sub', down_pairs)  6.85 us
    pallas_call x1, Pallas kernels, local(): pl.pallas_call(gram_kernel, out_shape=shape(2 * XR, 128), in_specs=[WHOLE...  6.36 us
    pallas_call x1, Pallas kernels, local(): pl.pallas_call(gather_kernel, out_shape=shape(subtiles, 2 * XR, 128), in_...  4.98 us
  transfers between devices with their start and end apart: 5, of which 2 were waited for; matrix products, arithmetic and copies ran while one was open for 1% of the time, Pallas kernels for 14%

profile of v2, /device:TPU:1, one launch (start us, length us, event | category | flops | bytes accessed | tf_op | source)
XLA Modules:
  0.0 129.0 jit_solution(4476810364147567389)
XLA Ops:
  1.3 0.0 copy-start.3
  1.3 0.9 copy-done.3
  2.2 0.0 copy-start.4
  2.2 0.9 copy-done.4
  3.2 0.0 copy-start.9
  3.2 0.7 copy-done.9
  3.8 0.7 copy-done.10
  4.5 2.9 %pack.1 = (f32[64,16,256]{2,1,0:T(8,128)S(1)}, f32[64,16,256]{2,1,0:T(8,128)}, s32[64,1,128]{2,1,0:T(1,128)S(1)}) custom-call(s32[32]{0:T(128)S(1)} %bitcast.17, s32[32]{0:T(128)S(1)} %bitcast.18, f32[32,8,256]{2,1,0:T(8,128)S(1)} %bitcast.15, f32[32,8,256]{2,1,0:T(8,128)S(1)} %bitcast.16), custom_call_target="tpu_custom_call" | custom-call | tf_op jit(solution)/shard_map/pack/pallas_call | solution.py:491
  7.3 0.7 pad_add_fusion.1.stamps
  8.1 18.1 %exchange.1 = (s32[64,1,128]{2,1,0:T(1,128)S(1)}, s32[2,1,128]{2,1,0:T(1,128)S(1)}) custom-call(s32[64,1,128]{2,1,0:T(1,128)S(1)} %get-tuple-element.26.cells, s32[1,128]{1,0:T(1,128)S(1)} %pad_add_fusion.1.stamps), custom_call_target="tpu_custom_call" | custom-call | tf_op jit(solution)/shard_map/exchange/pallas_call | solution.py:504
  26.3 36.5 %all_to_all.10.got = f32[64,16,256]{2,1,0:T(8,128)S(1)} all-to-all(f32[64,16,256]{2,1,0:T(8,128)S(1)} %get-tuple-element.31), channel_id=1, replica_groups=mesh['patch'=64,'sub'=4] {'patch'}, dimensions={0} | all-to-all | bytes 2097152 | tf_op jit(solution)/shard_map/all_to_all | solution.py:516
  62.7 8.8 %all-to-all-start = ((f32[64,16,256]{2,1,0:T(8,128)}), f32[64,16,256]{2,1,0:T(8,128)}, u32[]{:S(2)}, u32[]{:S(2)}) async-start(f32[64,16,256]{2,1,0:T(8,128)} %get-tuple-element.30), calls=%async_computation | async-start | bytes 2097152 | tf_op jit(solution)/shard_map/all_to_all | solution.py:517
  71.6 0.0 copy-done.13
  71.6 0.0 copy-done.14
  71.6 0.1 pad_add_fusion
  71.7 0.1 slice_add_fusion
  71.7 0.1 sub.35
  71.8 0.1 sub.31
  71.9 0.2 slice_reduce_fusion
  72.1 0.1 fusion.7
  72.2 0.1 and.35
  72.3 0.0 copy-done.11
  72.3 2.1 %image.1 = (f32[4,64,256]{2,1,0:T(8,128)S(1)}, f32[64,256]{1,0:T(8,128)S(1)}, f32[88,256]{1,0:T(8,128)S(1)}, f32[88,256]{1,0:T(8,128)S(1)}) custom-call(s32[64,1,128]{2,1,0:T(1,128)S(1)} %get-tuple-element.29.cells, s32[4]{0:T(128)S(1)} %copy-done.11, f32[64,16,256]{2,1,0:T(8,128)S(1)} %all_to_all.10.got), custom_call_target="tpu_custom_call" | custom-call | flops 300000000 | bytes 6000000 | tf_op jit(solution)/shard_map/image/pallas_call | solution.py:534
  74.4 4.3 %collective-permute-start = (f32[88,256]{1,0:T(8,128)S(1)}, f32[88,256]{1,0:T(8,128)S(1)}, u32[]{:S(2)}, u32[]{:S(2)}) collective-permute-start(f32[88,256]{1,0:T(8,128)S(1)} %get-tuple-element.34), channel_id=1, source_target_pairs={{0,1},{1,2},{2,3},{4,5},{5,6},{6,7},{8,9},{9,10},{10,11},{12,13},{... | collective-permute-start | bytes 270344 | tf_op jit(solution)/shard_map/ppermute | solution.py:544
  78.7 1.9 %collective-permute-start.1 = (f32[88,256]{1,0:T(8,128)S(1)}, f32[88,256]{1,0:T(8,128)S(1)}, u32[]{:S(2)}, u32[]{:S(2)}) collective-permute-start(f32[88,256]{1,0:T(8,128)S(1)} %get-tuple-element.35), channel_id=1, source_target_pairs={{1,0},{2,1},{3,2},{5,4},{6,5},{7,6},{9,8},{10,9},{11,10},{13,12},{... | collective-permute-start | bytes 270344 | tf_op jit(solution)/shard_map/ppermute | solution.py:545
  80.6 0.9 convolution_minimum_fusion.mask
  81.5 0.0 collective-permute-done.above.s_above
  81.6 4.6 %collective-permute-done.1.below.s_below = f32[88,256]{1,0:T(8,128)S(1)} collective-permute-done((f32[88,256]{1,0:T(8,128)S(1)}, f32[88,256]{1,0:T(8,128)S(1)}, u32[]{:S(2)}, u32[]{:S(2)}) %collective-permute-start.1) | collective-permute-done | bytes 90144 | tf_op jit(solution)/shard_map/ppermute | solution.py:545
  86.2 1.1 copy-done.12
  87.3 4.8 %basis.1 = (f32[40,96,256]{2,1,0:T(8,128)S(1)}, f32[3072,128]{1,0:T(8,128)S(1)}, f32[3072,128]{1,0:T(8,128)S(1)}, f32[8,128]{1,0:T(8,128)S(1)}) custom-call(f32[4,64,256]{2,1,0:T(8,128)S(1)} %get-tuple-element.32.science, f32[64,256]{1,0:T(8,128)S(1)} %get-tuple-element.33.template, f32[88,256]{1,0:T(8,128)S(1)} %collective-permute-done.above.s_above, ...), custom_call_target="tpu_custom_call" | custom-call | flops 800000000 | bytes 16000000 | tf_op jit(solution)/shard_map/basis/pallas_call | solution.py:549
  92.1 0.0 copy-start
  92.1 1.9 %copy-done = f32[40,96,256]{2,1,0:T(8,128)} copy-done((f32[40,96,256]{2,1,0:T(8,128)}, f32[40,96,256]{2,1,0:T(8,128)S(1)}, u32[]{:S(2)}) %copy-start) | copy-done | bytes 3932184
  94.0 0.6 copy-done.6
  94.6 3.4 %all-to-all-done.got = f32[64,16,256]{2,1,0:T(8,128)} async-done(((f32[64,16,256]{2,1,0:T(8,128)}), f32[64,16,256]{2,1,0:T(8,128)}, u32[]{:S(2)}, u32[]{:S(2)}) %all-to-all-start) | async-done | bytes 1048608 | tf_op jit(solution)/shard_map/all_to_all | solution.py:517
  98.0 2.4 %variance.1 = (f32[4,64,256]{2,1,0:T(8,128)S(1)}, f32[64,256]{1,0:T(8,128)S(1)}, f32[64,256]{1,0:T(8,128)S(1)}) custom-call(s32[64,1,128]{2,1,0:T(1,128)S(1)} %get-tuple-element.29.cells, s32[4]{0:T(128)S(1)} %copy-done.11, f32[64,16,256]{2,1,0:T(8,128)} %all-to-all-done.got, f32[8,128]{1,0:T(8,128)S(1)} %get-tuple-element.36.token), custom_call_target="tpu_custom_call" | custom-call | flops 300000000 | bytes 6000000 | tf_op jit(solution)/shard_map/variance/pallas_call | solution.py:564
  100.5 6.8 %collective-permute-start.2 = (f32[64,256]{1,0:T(8,128)S(1)}, f32[64,256]{1,0:T(8,128)S(1)}, u32[]{:S(2)}, u32[]{:S(2)}) collective-permute-start(f32[64,256]{1,0:T(8,128)S(1)} %get-tuple-element.42), channel_id=1, source_target_pairs={{0,1},{1,2},{2,3},{4,5},{5,6},{6,7},{8,9},{9,10},{10,11},{12,13},{... | collective-permute-start | bytes 196616 | tf_op jit(solution)/shard_map/ppermute | solution.py:574
  107.3 1.9 %collective-permute-start.3 = (f32[64,256]{1,0:T(8,128)S(1)}, f32[64,256]{1,0:T(8,128)S(1)}, u32[]{:S(2)}, u32[]{:S(2)}) collective-permute-start(f32[64,256]{1,0:T(8,128)S(1)} %get-tuple-element.43), channel_id=1, source_target_pairs={{1,0},{2,1},{3,2},{5,4},{6,5},{7,6},{9,8},{10,9},{11,10},{13,12},{... | collective-permute-start | bytes 196616 | tf_op jit(solution)/shard_map/ppermute | solution.py:575
  109.3 0.0 copy-start.8
  109.3 0.8 copy-done.8
  110.1 6.4 %gram.1.part = f32[96,128]{1,0:T(8,128)S(1)} custom-call(f32[4,64,256]{2,1,0:T(8,128)S(1)} %get-tuple-element.37.variance, f32[64,256]{1,0:T(8,128)S(1)} %copy-done.8, f32[3072,128]{1,0:T(8,128)S(1)} %get-tuple-element.39.xleft, f32[3072,128]{1,0:T(8,128)S(1)} %get-tuple-element.40.xright), custom_call_target="tpu_custom_call" | custom-call | flops 700000000 | bytes 14000000 | tf_op jit(solution)/shard_map/gram/pallas_call | solution.py:577
  116.5 5.0 %gather.1.gathered = f32[4,96,128]{2,1,0:T(8,128)S(1)} custom-call(f32[96,128]{1,0:T(8,128)S(1)} %gram.1.part), custom_call_target="tpu_custom_call" | custom-call | tf_op jit(solution)/shard_map/gather/pallas_call | solution.py:590
  121.5 0.0 collective-permute-done.2.w_above
  121.5 0.0 collective-permute-done.3.w_below
  121.5 0.0 copy-done.1
  121.5 0.0 copy-done.2
  121.5 0.0 copy-done.5
  121.5 0.0 copy-done.7
  121.5 7.5 %final.1 = (f32[4,64,256]{2,1,0:T(8,128)}, f32[4,64,256]{2,1,0:T(8,128)}) custom-call(s32[1]{0:T(128)} %bitcast.sub, f32[4,96,128]{2,1,0:T(8,128)S(1)} %gather.1.gathered, f32[40,96,256]{2,1,0:T(8,128)S(1)} %copy-done.1, f32[4,64,256]{2,1,0:T(8,128)S(1)} %get-tuple-element.32.science, f32[4,64,256]{2,1,0:T(8,128)S(1)} %get-tuple-element.37.variance, ...), custom_call_target="tpu_custom_call" | custom-call | flops 1000000000 | bytes 20000000 | tf_op jit(solution)/shard_map/final/pallas_call | solution.py:601
  (14 shorter events, 0.0 us)
Async XLA Ops:
  1.3 1.0 copy-start.3
  2.2 0.9 copy-start.4
  3.2 0.7 copy-start.9
  3.8 0.7 copy-start.10
  62.7 8.8 %copy-start.13 = (s32[1,12]{1,0:T(1,128)S(1)}, s32[1,12]{1,0:T(1,128)}, u32[]{:S(2)}) copy-start(s32[1,12]{1,0:T(1,128)} %param.16) | copy-start | bytes 148
  62.7 8.8 %copy-start.14 = (s32[1,12]{1,0:T(1,128)S(1)}, s32[1,12]{1,0:T(1,128)}, u32[]{:S(2)}) copy-start(s32[1,12]{1,0:T(1,128)} %param.15) | copy-start | bytes 148
  62.7 9.5 %copy-start.11 = (s32[4]{0:T(128)S(1)}, s32[4]{0:T(128)}, u32[]{:S(2)}) copy-start(s32[4]{0:T(128)} %warp.3) | copy-start | bytes 52
  62.7 35.3 %all-to-all-start = ((f32[64,16,256]{2,1,0:T(8,128)}), f32[64,16,256]{2,1,0:T(8,128)}, u32[]{:S(2)}, u32[]{:S(2)}) async-start(f32[64,16,256]{2,1,0:T(8,128)} %get-tuple-element.30), calls=%async_computation | async-start | bytes 2097152 | tf_op jit(solution)/shard_map/all_to_all | solution.py:517
  74.4 7.1 %collective-permute-start = (f32[88,256]{1,0:T(8,128)S(1)}, f32[88,256]{1,0:T(8,128)S(1)}, u32[]{:S(2)}, u32[]{:S(2)}) collective-permute-start(f32[88,256]{1,0:T(8,128)S(1)} %get-tuple-element.34), channel_id=1, source_target_pairs={{0,1},{1,2},{2,3},{4,5},{5,6},{6,7},{8,9},{9,10},{10,11},{12,13},{... | collective-permute-start | bytes 270344 | tf_op jit(solution)/shard_map/ppermute | solution.py:544
  78.7 7.5 %collective-permute-start.1 = (f32[88,256]{1,0:T(8,128)S(1)}, f32[88,256]{1,0:T(8,128)S(1)}, u32[]{:S(2)}, u32[]{:S(2)}) collective-permute-start(f32[88,256]{1,0:T(8,128)S(1)} %get-tuple-element.35), channel_id=1, source_target_pairs={{1,0},{2,1},{3,2},{5,4},{6,5},{7,6},{9,8},{10,9},{11,10},{13,12},{... | collective-permute-start | bytes 270344 | tf_op jit(solution)/shard_map/ppermute | solution.py:545
  86.2 1.1 copy-start.12
  92.1 1.9 %copy-start = (f32[40,96,256]{2,1,0:T(8,128)}, f32[40,96,256]{2,1,0:T(8,128)S(1)}, u32[]{:S(2)}) copy-start(f32[40,96,256]{2,1,0:T(8,128)S(1)} %get-tuple-element.41.basis) | copy-start | bytes 11796484
  94.0 0.6 copy-start.6
  98.0 23.5 %copy-start.1 = (f32[40,96,256]{2,1,0:T(8,128)S(1)}, f32[40,96,256]{2,1,0:T(8,128)}, u32[]{:S(2)}) copy-start(f32[40,96,256]{2,1,0:T(8,128)} %copy-done) | copy-start | bytes 11796484
  100.5 21.0 %collective-permute-start.2 = (f32[64,256]{1,0:T(8,128)S(1)}, f32[64,256]{1,0:T(8,128)S(1)}, u32[]{:S(2)}, u32[]{:S(2)}) collective-permute-start(f32[64,256]{1,0:T(8,128)S(1)} %get-tuple-element.42), channel_id=1, source_target_pairs={{0,1},{1,2},{2,3},{4,5},{5,6},{6,7},{8,9},{9,10},{10,11},{12,13},{... | collective-permute-start | bytes 196616 | tf_op jit(solution)/shard_map/ppermute | solution.py:574
  107.3 14.2 %collective-permute-start.3 = (f32[64,256]{1,0:T(8,128)S(1)}, f32[64,256]{1,0:T(8,128)S(1)}, u32[]{:S(2)}, u32[]{:S(2)}) collective-permute-start(f32[64,256]{1,0:T(8,128)S(1)} %get-tuple-element.43), channel_id=1, source_target_pairs={{1,0},{2,1},{3,2},{5,4},{6,5},{7,6},{9,8},{10,9},{11,10},{13,12},{... | collective-permute-start | bytes 196616 | tf_op jit(solution)/shard_map/ppermute | solution.py:575
  109.3 0.8 copy-start.8
  110.1 11.4 %copy-start.2 = (bf16[4,256,256]{2,1,0:T(8,128)(2,1)S(1)}, bf16[4,256,256]{2,1,0:T(8,128)(2,1)}, u32[]{:S(2)}) copy-start(bf16[4,256,256]{2,1,0:T(8,128)(2,1)} %constant.9.clone.cols) | copy-start | bytes 1572868
  110.1 11.4 %copy-start.5 = (bf16[2,64,288]{2,1,0:T(8,128)(2,1)S(1)}, bf16[2,64,288]{2,1,0:T(8,128)(2,1)}, u32[]{:S(2)}) copy-start(bf16[2,64,288]{2,1,0:T(8,128)(2,1)} %constant.26.clone.rows) | copy-start | bytes 221188
  110.1 11.4 %copy-start.7 = (f32[88,256]{1,0:T(8,128)S(1)}, f32[88,256]{1,0:T(8,128)}, u32[]{:S(2)}) copy-start(f32[88,256]{1,0:T(8,128)} %copy-done.6) | copy-start | bytes 270340

commit v3 on v2

--- a/solution.py
+++ b/solution.py
@@ -35,6 +35,7 @@
 TH = 24
 SR = 16
 HALO = TH + V * SR
+BLOCK = 4 * CR
 VMEM_LIMIT = 16 * 1024 * 1024
 WHOLE = pl.BlockSpec(memory_space=pltpu.VMEM)
 SCALARS = pl.BlockSpec(memory_space=pltpu.SMEM)
@@ -116,7 +117,8 @@
 
 
 def pack_kernel(patch, cell, image, variance, out_image, out_variance, out_cell, count, slot_cell):
-    patches = out_image.shape[0]
+    patches = out_variance.shape[0]
+    out_image[...] = jnp.zeros_like(out_image)
 
     def clear(n, _):
         count[n] = 0
@@ -132,7 +134,10 @@
         count[q] = rank + 1
         slot_cell[2 * q + rank] = cell[n]
         rows = pl.ds(pl.multiple_of(rank * CR, CR), CR)
-        out_image[q, rows, :] = image[n]
+        a = image[n]
+        for half in range(2):
+            at = pl.multiple_of(q * BLOCK + half * 2 * CR + rank * CR, CR)
+            out_image[pl.ds(at, CR), :] = a[:, half * 128 : (half + 1) * 128]
         out_variance[q, rows, :] = variance[n]
         return 0
 
@@ -146,11 +151,65 @@
     lax.fori_loop(0, patches, tell, 0)
 
 
-def exchange_kernel(cells, stamps, got_cells, got_stamps, send, recv, ring_send, ring_recv, own):
+def stamp_mask(mask, stamps, got_stamps, sub, subtiles, slots):
+    row = lax.broadcasted_iota(jnp.int32, (RT, CW), 0)
+    col = lax.broadcasted_iota(jnp.int32, (RT, CW), 1)
+    flags = [(sub > 0).astype(jnp.int32), 1, (sub < subtiles - 1).astype(jnp.int32)]
+    mask[...] = jnp.zeros_like(mask)
+    for n, (flag, table) in enumerate(zip(flags, (got_stamps[0], stamps[...], got_stamps[1]))):
+        count = table[:, 2 * slots : 2 * slots + 1] * flag
+        for k in range(slots):
+            near_row = jnp.abs(row - (n - 1) * RT - table[:, k : k + 1]) <= SH
+            near_col = jnp.abs(col - table[:, slots + k : slots + k + 1]) <= SH
+            mask[...] = jnp.where(near_row & near_col & (count > k), 1.0, mask[...])
+
+
+def combine_image(cells, warp, got, out, left, right):
+    patches = cells.shape[0]
+    lane = lax.broadcasted_iota(jnp.int32, (patches, 128), 1)
+    table = cells[:, 0, :]
+    wide = jnp.concatenate(
+        [(table[:, rank : rank + 1] == lane).astype(jnp.float32) for rank in range(2)]
+        + [jnp.zeros((128 - 2 * patches, 128), jnp.float32)] * (2 * patches < 128),
+        axis=0,
+    )
+    chosen = jnp.transpose(wide)[0 : V * NCELL, :].astype(jnp.bfloat16)
+    for half, ref in enumerate((left, right)):
+        for r in range(CR):
+            x = jnp.concatenate(
+                [
+                    got[pl.ds(half * 2 * CR + rank * CR + r, patches, stride=BLOCK), :]
+                    for rank in range(2)
+                ]
+                + [jnp.zeros((128 - 2 * patches, 128), jnp.float32)] * (2 * patches < 128),
+                axis=0,
+            )
+            hi, rest = x.astype(jnp.bfloat16), x
+            rest = rest - hi.astype(jnp.float32)
+            mid, low = split(rest)
+            y = mm(chosen, jnp.concatenate([hi, mid, low], axis=1))
+            ref[pl.ds(r, V * NCELL, stride=CR), :] = y[:, 0:128] + y[:, 128:256] + y[:, 256:384]
+    col = lax.broadcasted_iota(jnp.int32, (RT, CW), 1)
+    for v in range(V):
+        rows = slice(v * RT, (v + 1) * RT)
+        off = jnp.full((RT, CW), warp[v], jnp.int32)
+        a = pltpu.roll(jnp.concatenate([left[rows, :], right[rows, :]], axis=1), WARP, 1)
+        for bit in range(4):
+            a = jnp.where((off & (1 << bit)) != 0, pltpu.roll(a, CW - (1 << bit), 1), a)
+        source = col + off - WARP
+        out[v] = jnp.where((source >= 0) & (source < CW), a, 0.0)
+
+
+def front_kernel(
+    slots, sent_image, sent_variance, cells, stamps, warp, row_bands,
+    science, basis, xleft, xright, got_variance, got_cells, got_stamps, above, below, mask,
+    got_image, left, right, template, up, down, text, filt,
+    send, recv, ring_send, ring_recv, own,
+):
     patches = cells.shape[0]
     subtiles = lax.axis_size("sub")
     me, sub = lax.axis_index("patch"), lax.axis_index("sub")
-    right, left = lax.rem(sub + 1, subtiles), lax.rem(sub + subtiles - 1, subtiles)
+    next_sub, last_sub = lax.rem(sub + 1, subtiles), lax.rem(sub + subtiles - 1, subtiles)
     barrier = pltpu.get_barrier_semaphore()
 
     def greet(d, _):
@@ -159,43 +218,92 @@
         return 0
 
     lax.fori_loop(1, patches, greet, 0)
-    for s in (left, right):
+    for s in (last_sub, next_sub):
         pl.semaphore_signal(barrier, inc=1, device_id={"sub": s}, device_id_type=MESH)
     pl.semaphore_wait(barrier, patches + 1)
 
-    def copy(d, to, at):
+    def block(q):
+        return pl.ds(pl.multiple_of(q * BLOCK, BLOCK), BLOCK)
+
+    def ends(n, source, to):
+        if n == 0:
+            return cells.at[to], got_cells.at[source]
+        if n == 1:
+            return sent_image.at[block(to), :], got_image.at[block(source), :]
+        return sent_variance.at[to], got_variance.at[source]
+
+    def copy(n, d, to, source):
+        src, dst = ends(n, source, to)
         return pltpu.make_async_remote_copy(
-            src_ref=cells.at[to], dst_ref=got_cells.at[at], send_sem=send.at[d],
-            recv_sem=recv.at[d], device_id={"patch": to}, device_id_type=MESH,
+            src_ref=src, dst_ref=dst, send_sem=send.at[n, d], recv_sem=recv.at[n, d],
+            device_id={"patch": to}, device_id_type=MESH,
         )
 
-    def start(d, _):
-        copy(d, lax.rem(me + d, patches), me).start()
-        return 0
-
-    lax.fori_loop(1, patches, start, 0)
-    rings = [
-        pltpu.make_async_remote_copy(
-            src_ref=stamps, dst_ref=got_stamps.at[n], send_sem=ring_send.at[n],
-            recv_sem=ring_recv.at[n], device_id={"sub": to}, device_id_type=MESH,
-        )
-        for n, to in enumerate((right, left))
-    ]
-    for ring in rings:
-        ring.start()
-    mine = pltpu.make_async_copy(cells.at[me], got_cells.at[me], own)
-    mine.start()
-    mine.wait()
+    def ring(n, src, dst):
+        return [
+            pltpu.make_async_remote_copy(
+                src_ref=s, dst_ref=r, send_sem=ring_send.at[n, k], recv_sem=ring_recv.at[n, k],
+                device_id={"sub": to}, device_id_type=MESH,
+            )
+            for k, (s, r, to) in enumerate(zip(src, dst, (next_sub, last_sub)))
+        ]
+
+    def start_first(d, _):
+        copy(0, d, lax.rem(me + d, patches), me).start()
+        copy(1, d, lax.rem(me + d, patches), me).start()
+        return 0
+
+    lax.fori_loop(1, patches, start_first, 0)
+    table_ring = ring(0, (stamps, stamps), (got_stamps.at[0], got_stamps.at[1]))
+    for c in table_ring:
+        c.start()
+
+    def start_last(d, _):
+        copy(2, d, lax.rem(me + d, patches), me).start()
+        return 0
+
+    lax.fori_loop(1, patches, start_last, 0)
+    mine = [pltpu.make_async_copy(*ends(n, me, me), own.at[n]) for n in range(3)]
+    for c in mine:
+        c.start()
+    for c in mine:
+        c.wait()
+
+    def wait_first(d, _):
+        source = lax.rem(me + patches - d, patches)
+        copy(0, d, source, source).wait_recv()
+        copy(1, d, source, source).wait_recv()
+        return 0
+
+    lax.fori_loop(1, patches, wait_first, 0)
+    combine_image(got_cells, warp, got_image, science, left, right)
+    template[...] = (science[0] + science[1] + science[2] + science[3]) / V
+    up[0:TH, :] = template[0:TH, :]
+    down[0:TH, :] = template[RT - TH : RT, :]
+    for v in range(V):
+        at = TH + v * SR
+        up[at : at + SR, :] = science[v, 0:SR, :]
+        down[at : at + SR, :] = science[v, RT - SR : RT, :]
+    rims = ring(1, (down, up), (above, below))
+    for c in rims:
+        c.start()
+    for c in table_ring:
+        c.wait()
+    stamp_mask(mask, stamps, got_stamps, sub, subtiles, slots)
+    for c in rims:
+        c.wait()
+    above[...] = above[...] * (sub > 0).astype(jnp.float32)
+    below[...] = below[...] * (sub < subtiles - 1).astype(jnp.float32)
+    basis_images(science, template, above, below, row_bands, basis, xleft, xright, text, filt)
 
     def finish(d, _):
-        copy(d, lax.rem(me + d, patches), me).wait_send()
         source = lax.rem(me + patches - d, patches)
-        copy(d, source, source).wait_recv()
+        for n in range(3):
+            copy(n, d, lax.rem(me + d, patches), me).wait_send()
+        copy(2, d, source, source).wait_recv()
         return 0
 
     lax.fori_loop(1, patches, finish, 0)
-    for ring in rings:
-        ring.wait()
 
 
 def gather_kernel(part, gathered, send, recv, own):
@@ -249,28 +357,16 @@
             out[v, c * CR : (c + 1) * CR, :] = jnp.where(inside, pltpu.roll(a, turn, 1), 0.0)
 
 
-def image_kernel(cells, warp, got, science, template, up, down, acc):
-    combine(cells, warp, got, science, acc)
-    template[...] = (science[0] + science[1] + science[2] + science[3]) / V
-    up[0:TH, :] = template[0:TH, :]
-    down[0:TH, :] = template[RT - TH : RT, :]
-    for v in range(V):
-        at = TH + v * SR
-        up[at : at + SR, :] = science[v, 0:SR, :]
-        down[at : at + SR, :] = science[v, RT - SR : RT, :]
-
-
-def variance_kernel(cells, warp, got, token, variance, up, down, acc):
+def variance_kernel(cells, warp, got, variance, up, down, acc):
     combine(cells, warp, got, variance, acc)
     for v in range(V):
         up[v * SR : (v + 1) * SR, :] = variance[v, 0:SR, :]
         down[v * SR : (v + 1) * SR, :] = variance[v, RT - SR : RT, :]
 
 
-def basis_kernel(
-    science, template, above, below, row_bands, basis, xleft, xright, token, text, filt,
+def basis_images(
+    science, template, above, below, row_bands, basis, xleft, xright, text, filt,
 ):
-    token[...] = jnp.zeros_like(token)
     taps = tap_values()
 
     def put(k, image):
@@ -488,9 +584,10 @@
     dma = pltpu.SemaphoreType.DMA
 
     half = shape(patches, 2 * CR, CW)
+    cell_rows = shape(patches, 1, 128, dtype=jnp.int32)
     sent_image, sent_variance, sent_cell = pl.pallas_call(
         pack_kernel,
-        out_shape=(half, half, shape(patches, 1, 128, dtype=jnp.int32)),
+        out_shape=(shape(patches * BLOCK, 128), half, cell_rows),
         in_specs=[SCALARS, SCALARS, WHOLE, WHOLE],
         out_specs=(WHOLE,) * 3,
         scratch_shapes=[pltpu.SMEM((patches,), jnp.int32), pltpu.SMEM((2 * patches,), jnp.int32)],
@@ -501,76 +598,47 @@
     table = jnp.concatenate(
         [stamp_row, stamp_col, stamp_count, jnp.zeros((1, 127 - 2 * slots), jnp.int32)], axis=1
     )
-    got_cell, got_stamps = pl.pallas_call(
-        exchange_kernel,
-        out_shape=(shape(patches, 1, 128, dtype=jnp.int32), shape(2, 1, 128, dtype=jnp.int32)),
-        in_specs=[WHOLE] * 2,
-        out_specs=(WHOLE,) * 2,
-        scratch_shapes=[dma((patches,)), dma((patches,)), dma((2,)), dma((2,)), dma],
-        compiler_params=params(collective_id=0, has_side_effects=True),
-        name="exchange",
-    )(sent_cell, table)
-    sent_image, sent_variance, got_cell, got_stamps = lax.optimization_barrier(
-        (sent_image, sent_variance, got_cell, got_stamps)
-    )
-    got_image = lax.all_to_all(sent_image, "patch", split_axis=0, concat_axis=0, tiled=True)
-    got_variance = lax.all_to_all(sent_variance, "patch", split_axis=0, concat_axis=0, tiled=True)
-
-    near = jnp.concatenate([got_stamps[0], table, got_stamps[1]], axis=0)
-    shift = jnp.arange(-1, 2)[:, None]
-    present = (me + shift >= 0) & (me + shift < subtiles)
-    centre_row = (near[:, 0:slots] + shift * RT).reshape(-1)
-    centre_col = near[:, slots : 2 * slots].reshape(-1)
-    live = (present & (jnp.arange(slots)[None, :] < near[:, 2 * slots : 2 * slots + 1])).reshape(-1)
-    row_in = ((jnp.abs(jnp.arange(RT)[None, :] - centre_row[:, None]) <= SH) & live[:, None]).astype(
-        jnp.bfloat16
-    )
-    col_in = (jnp.abs(jnp.arange(CW)[None, :] - centre_col[:, None]) <= SH).astype(jnp.bfloat16)
-    mask = jnp.minimum(jnp.dot(row_in.T, col_in, preferred_element_type=jnp.float32), 1.0)
-
+    row_bands, cols, rows = constants()
     field = shape(V, RT, CW)
-    cells_acc = [pltpu.VMEM((V * NCELL + 1, CR, CW), jnp.float32)]
     rim = shape(HALO, CW)
-    science, template, up, down = pl.pallas_call(
-        image_kernel,
-        out_shape=(field, shape(RT, CW), rim, rim),
-        in_specs=[SCALARS, SCALARS, WHOLE],
-        out_specs=(WHOLE,) * 4,
-        scratch_shapes=cells_acc,
-        compiler_params=params(),
-        cost_estimate=costs(3),
-        name="image",
-    )(got_cell, warp_offsets, got_image)
-    s_above = lax.ppermute(down, "sub", down_pairs)
-    s_below = lax.ppermute(up, "sub", up_pairs)
-
-    row_bands, cols, rows = constants()
     half_rows = shape(RT * XR, 128)
-    basis, xleft, xright, token = pl.pallas_call(
-        basis_kernel,
-        out_shape=(shape(NB, CE, CW), half_rows, half_rows, shape(8, 128)),
-        in_specs=[WHOLE] * 5,
-        out_specs=(WHOLE,) * 4,
+    vmem = pltpu.VMEM
+    science, basis, xleft, xright, got_variance, got_cell, _, s_above, s_below, mask = pl.pallas_call(
+        functools.partial(front_kernel, slots),
+        out_shape=(
+            field, shape(NB, CE, CW), half_rows, half_rows, half, cell_rows,
+            shape(2, 1, 128, dtype=jnp.int32), rim, rim, shape(RT, CW),
+        ),
+        in_specs=[WHOLE] * 4 + [SCALARS, WHOLE],
+        out_specs=(WHOLE,) * 10,
         scratch_shapes=[
-            pltpu.VMEM((TE, CW), jnp.float32),
-            pltpu.VMEM((NT, TE, CW), jnp.float32),
+            vmem((patches * BLOCK, 128), jnp.float32),
+            vmem((V * RT, 128), jnp.float32),
+            vmem((V * RT, 128), jnp.float32),
+            vmem((RT, CW), jnp.float32),
+            vmem((HALO, CW), jnp.float32),
+            vmem((HALO, CW), jnp.float32),
+            vmem((TE, CW), jnp.float32),
+            vmem((NT, TE, CW), jnp.float32),
+            dma((3, patches)), dma((3, patches)), dma((2, 2)), dma((2, 2)), dma((3,)),
         ],
-        compiler_params=params(),
-        cost_estimate=costs(8),
-        name="basis",
-    )(science, template, s_above, s_below, jnp.asarray(row_bands))
+        compiler_params=pltpu.CompilerParams(
+            vmem_limit_bytes=24 * 1024 * 1024, collective_id=0, has_side_effects=True
+        ),
+        name="front",
+    )(sent_image, sent_variance, sent_cell, table, warp_offsets, jnp.asarray(row_bands))
 
     rim = shape(V * SR, CW)
     variance, up, down = pl.pallas_call(
         variance_kernel,
         out_shape=(field, rim, rim),
-        in_specs=[SCALARS, SCALARS, WHOLE, WHOLE],
+        in_specs=[SCALARS, SCALARS, WHOLE],
         out_specs=(WHOLE,) * 3,
-        scratch_shapes=cells_acc,
+        scratch_shapes=[pltpu.VMEM((V * NCELL + 1, CR, CW), jnp.float32)],
         compiler_params=params(),
         cost_estimate=costs(3),
         name="variance",
-    )(got_cell, warp_offsets, got_variance, token)
+    )(got_cell, warp_offsets, got_variance)
     w_above = lax.ppermute(down, "sub", down_pairs)
     w_below = lax.ppermute(up, "sub", up_pairs)
 

time: 130 us -> 103 us (0.79)
  Pallas kernels: 49.2 us -> 86.9 us
  blocking collectives: 36.5 us -> 0 us
  starting transfers between devices: 23.7 us -> 6.2 us
  waiting for transfers between devices: 8.09 us -> 0.01 us
    pallas_call x4 -> x2, Pallas kernels: 27.9 us -> 66 us  [the longest x1 64.1 us: local(): pl.pallas_call(functools.partial(front_kernel, slots), out_shape=(field,...]
    all_to_all x1 -> x0, blocking collectives: 36.5 us -> none  [local(): lax.all_to_all(sent_image, 'patch', split_axis=0, concat_axis=0, tiled=True)]
    all_to_all x1 -> x0, starting transfers between devices: 8.79 us -> none  [local(): lax.all_to_all(sent_variance, 'patch', split_axis=0, concat_axis=0, tiled...]
    ppermute x2 -> x0, starting transfers between devices: 6.19 us -> none  [the longest x1 4.27 us: local(): s_above = lax.ppermute(down, 'sub', down_pairs)]
    ppermute x2 -> x0, waiting for transfers between devices: 4.68 us -> none  [the longest x1 4.65 us: local(): s_below = lax.ppermute(up, 'sub', up_pairs)]
    all_to_all x1 -> x0, waiting for transfers between devices: 3.4 us -> none  [local(): lax.all_to_all(sent_variance, 'patch', split_axis=0, concat_axis=0, tiled...]
    ppermute x1, starting transfers between devices: 6.85 us -> 4.28 us  [local(): w_above = lax.ppermute(down, 'sub', down_pairs)]
    unnamed x30 -> x20, local copies, waits for them, and re-layouts: 7.67 us -> 7.08 us
  transfers between devices with their start and end apart: 5 -> 2, of which waited for: 2 -> 0; matrix products, arithmetic and copies ran while one was open for 1% -> 0% of each run, Pallas kernels for 14% -> 11%
where the time goes in v3:
time: 103 us; the launch traced here: 102 us
  Pallas kernels  86.9 us (84%)
  local copies, waits for them, and re-layouts  7.08 us (7%)
  starting transfers between devices  6.2 us (6%)
  between operations  1.43 us (1%)
    pallas_call x1, Pallas kernels, local(): pl.pallas_call(functools.partial(front_kernel, slots), out_shape=(field,...  64.1 us
    pallas_call x1, Pallas kernels, local(): pl.pallas_call(functools.partial(final_kernel, normalizer), out_shape=(fi...  7.4 us
    unnamed x20, local copies, waits for them, and re-layouts  7.08 us
    pallas_call x1, Pallas kernels, local(): pl.pallas_call(gram_kernel, out_shape=shape(2 * XR, 128), in_specs=[WHOLE...  6.35 us
    pallas_call x1, Pallas kernels, local(): pl.pallas_call(gather_kernel, out_shape=shape(subtiles, 2 * XR, 128), in_...  4.99 us
    ppermute x1, starting transfers between devices, local(): w_above = lax.ppermute(down, 'sub', down_pairs)  4.28 us
    pallas_call x1, Pallas kernels, local(): pl.pallas_call(variance_kernel, out_shape=(field, rim, rim), in_specs=[SC...  2.14 us
  transfers between devices with their start and end apart: 2, of which 0 were waited for; matrix products, arithmetic and copies ran while one was open for 0% of the time, Pallas kernels for 11%

profile of v3, /device:TPU:1, one launch (start us, length us, event | category | flops | bytes accessed | tf_op | source)
XLA Modules:
  0.0 102.3 jit_solution(10748635537933392158)
XLA Ops:
  1.3 0.0 copy-start.4
  1.3 0.9 copy-done.4
  2.2 0.0 copy-start.5
  2.2 0.9 copy-done.5
  3.2 0.0 copy-start.8
  3.2 0.7 copy-done.8
  3.8 0.0 copy-start.9
  3.8 0.7 copy-done.9
  4.5 1.9 %pack.1 = (f32[2048,128]{1,0:T(8,128)S(1)}, f32[64,16,256]{2,1,0:T(8,128)S(1)}, s32[64,1,128]{2,1,0:T(1,128)S(1)}) custom-call(s32[32]{0:T(128)S(1)} %bitcast.15, s32[32]{0:T(128)S(1)} %bitcast.16, f32[32,8,256]{2,1,0:T(8,128)S(1)} %bitcast.13, f32[32,8,256]{2,1,0:T(8,128)S(1)} %bitcast.14), custom_call_target="tpu_custom_call" | custom-call | tf_op jit(solution)/shard_map/pack/pallas_call | solution.py:588
  6.4 0.8 bitcast_add_fusion.stamps
  7.2 0.0 copy-start.2
  7.2 1.1 %copy-done.2 = bf16[1344,256]{1,0:T(8,128)(2,1)S(1)} copy-done((bf16[1344,256]{1,0:T(8,128)(2,1)S(1)}, bf16[1344,256]{1,0:T(8,128)(2,1)}, u32[]{:S(2)}) %copy-start.2) | copy-done | bytes 688152
  8.3 0.0 copy-start.7
  8.3 0.7 copy-done.7
  8.9 64.1 %front.1 = (f32[4,64,256]{2,1,0:T(8,128)S(1)}, f32[40,96,256]{2,1,0:T(8,128)S(1)}, f32[3072,128]{1,0:T(8,128)S(1)}, f32[3072,128]{1,0:T(8,128)S(1)}, f32[64,16,2...) custom-call(f32[2048,128]{1,0:T(8,128)S(1)} %get-tuple-element.19.se, ...), custom_call_target="tpu_custom_call" | custom-call | tf_op jit(solution)/shard_map/front/pallas_call | solution.py:606
  73.0 0.0 copy-start
  73.0 2.1 %variance.1 = (f32[4,64,256]{2,1,0:T(8,128)S(1)}, f32[64,256]{1,0:T(8,128)S(1)}, f32[64,256]{1,0:T(8,128)S(1)}) custom-call(s32[64,1,128]{2,1,0:T(1,128)S(1)} %get-tuple-element.22.cells, s32[4]{0:T(128)S(1)} %copy-done.7, f32[64,16,256]{2,1,0:T(8,128)S(1)} %get-tuple-element.23.got), custom_call_target="tpu_custom_call" | custom-call | flops 300000000 | bytes 6000000 | tf_op jit(solution)/shard_map/variance/pallas_call | solution.py:632
  75.2 4.3 %collective-permute-start = (f32[64,256]{1,0:T(8,128)S(1)}, f32[64,256]{1,0:T(8,128)S(1)}, u32[]{:S(2)}, u32[]{:S(2)}) collective-permute-start(f32[64,256]{1,0:T(8,128)S(1)} %get-tuple-element.32), channel_id=1, source_target_pairs={{0,1},{1,2},{2,3},{4,5},{5,6},{6,7},{8,9},{9,10},{10,11},{12,13},{... | collective-permute-start | bytes 196616 | tf_op jit(solution)/shard_map/ppermute | solution.py:642
  79.4 1.9 %collective-permute-start.1 = (f32[64,256]{1,0:T(8,128)S(1)}, f32[64,256]{1,0:T(8,128)S(1)}, u32[]{:S(2)}, u32[]{:S(2)}) collective-permute-start(f32[64,256]{1,0:T(8,128)S(1)} %get-tuple-element.33), channel_id=1, source_target_pairs={{1,0},{2,1},{3,2},{5,4},{6,5},{7,6},{9,8},{10,9},{11,10},{13,12},{... | collective-permute-start | bytes 196616 | tf_op jit(solution)/shard_map/ppermute | solution.py:643
  81.4 0.0 copy-start.3
  81.4 0.0 copy-start.6
  81.4 6.3 %gram.1.part = f32[96,128]{1,0:T(8,128)S(1)} custom-call(f32[4,64,256]{2,1,0:T(8,128)S(1)} %get-tuple-element.24.variance, f32[64,256]{1,0:T(8,128)S(1)} %get-tuple-element.25.mask, f32[3072,128]{1,0:T(8,128)S(1)} %get-tuple-element.26.xleft, f32[3072,128]{1,0:T(8,128)S(1)} %get-tuple-element.27.xright), custom_call_target="tpu_custom_call" | custom-call | flops 700000000 | bytes 14000000 | tf_op jit(solution)/shard_map/gram/pallas_call | solution.py:645
  87.8 0.0 copy-done
  87.8 5.0 %gather.1.gathered = f32[4,96,128]{2,1,0:T(8,128)S(1)} custom-call(f32[96,128]{1,0:T(8,128)S(1)} %gram.1.part), custom_call_target="tpu_custom_call" | custom-call | tf_op jit(solution)/shard_map/gather/pallas_call | solution.py:658
  92.8 0.0 collective-permute-done.w_above
  92.8 0.0 collective-permute-done.1.w_below
  92.8 0.0 copy-done.3
  92.8 0.0 copy-done.6
  92.8 0.0 copy-start.1
  92.8 2.1 %copy-done.1 = f32[40,96,256]{2,1,0:T(8,128)S(1)} copy-done((f32[40,96,256]{2,1,0:T(8,128)S(1)}, f32[40,96,256]{2,1,0:T(8,128)}, u32[]{:S(2)}) %copy-start.1) | copy-done | bytes 3932184
  94.9 7.4 %final.1 = (f32[4,64,256]{2,1,0:T(8,128)}, f32[4,64,256]{2,1,0:T(8,128)}) custom-call(s32[1]{0:T(128)} %bitcast.sub, f32[4,96,128]{2,1,0:T(8,128)S(1)} %gather.1.gathered, f32[40,96,256]{2,1,0:T(8,128)S(1)} %copy-done.1, f32[4,64,256]{2,1,0:T(8,128)S(1)} %get-tuple-element.29.science, f32[4,64,256]{2,1,0:T(8,128)S(1)} %get-tuple-element.24.variance, ...), custom_call_target="tpu_custom_call" | custom-call | flops 1000000000 | bytes 20000000 | tf_op jit(solution)/shard_map/final/pallas_call | solution.py:669
  (1 shorter events, 0.0 us)
Async XLA Ops:
  1.3 1.0 copy-start.4
  2.2 0.9 copy-start.5
  3.2 0.7 copy-start.8
  3.8 0.7 copy-start.9
  7.2 1.1 %copy-start.2 = (bf16[1344,256]{1,0:T(8,128)(2,1)S(1)}, bf16[1344,256]{1,0:T(8,128)(2,1)}, u32[]{:S(2)}) copy-start(bf16[1344,256]{1,0:T(8,128)(2,1)} %constant.12.clone.row_bands) | copy-start | bytes 2064388
  8.3 0.7 copy-start.7
  73.0 14.8 %copy-start = (f32[40,96,256]{2,1,0:T(8,128)}, f32[40,96,256]{2,1,0:T(8,128)S(1)}, u32[]{:S(2)}) copy-start(f32[40,96,256]{2,1,0:T(8,128)S(1)} %get-tuple-element.28.basis) | copy-start | bytes 11796484
  75.2 17.6 %collective-permute-start = (f32[64,256]{1,0:T(8,128)S(1)}, f32[64,256]{1,0:T(8,128)S(1)}, u32[]{:S(2)}, u32[]{:S(2)}) collective-permute-start(f32[64,256]{1,0:T(8,128)S(1)} %get-tuple-element.32), channel_id=1, source_target_pairs={{0,1},{1,2},{2,3},{4,5},{5,6},{6,7},{8,9},{9,10},{10,11},{12,13},{... | collective-permute-start | bytes 196616 | tf_op jit(solution)/shard_map/ppermute | solution.py:642
  79.4 13.3 %collective-permute-start.1 = (f32[64,256]{1,0:T(8,128)S(1)}, f32[64,256]{1,0:T(8,128)S(1)}, u32[]{:S(2)}, u32[]{:S(2)}) collective-permute-start(f32[64,256]{1,0:T(8,128)S(1)} %get-tuple-element.33), channel_id=1, source_target_pairs={{1,0},{2,1},{3,2},{5,4},{6,5},{7,6},{9,8},{10,9},{11,10},{13,12},{... | collective-permute-start | bytes 196616 | tf_op jit(solution)/shard_map/ppermute | solution.py:643
  81.4 11.4 %copy-start.3 = (bf16[4,256,256]{2,1,0:T(8,128)(2,1)S(1)}, bf16[4,256,256]{2,1,0:T(8,128)(2,1)}, u32[]{:S(2)}) copy-start(bf16[4,256,256]{2,1,0:T(8,128)(2,1)} %constant.13.clone.cols) | copy-start | bytes 1572868
  81.4 11.4 %copy-start.6 = (bf16[2,64,288]{2,1,0:T(8,128)(2,1)S(1)}, bf16[2,64,288]{2,1,0:T(8,128)(2,1)}, u32[]{:S(2)}) copy-start(bf16[2,64,288]{2,1,0:T(8,128)(2,1)} %constant.14.clone.rows) | copy-start | bytes 221188
  92.8 2.1 %copy-start.1 = (f32[40,96,256]{2,1,0:T(8,128)S(1)}, f32[40,96,256]{2,1,0:T(8,128)}, u32[]{:S(2)}) copy-start(f32[40,96,256]{2,1,0:T(8,128)} %copy-done) | copy-start | bytes 11796484

commit v4 on v3

v4 whole, which is shorter than its diff:
```python
import functools
import math

import jax
import jax.numpy as jnp
import numpy as np
from jax import lax
from jax.experimental import pallas as pl
from jax.experimental.pallas import tpu as pltpu
from jax.sharding import PartitionSpec as P

V = 4
NCELL = 8
CR = 8
RT = 64
CW = 256
KR = 10
PR = 10
SH = 15
WARP = 4
NB = 40
NP = 32
SIGMAS = (0.75, 1.5, 3.0)
DEGREES = (4, 4, 3)
PSF_SIGMA = 2.0
SKY_VAR = 0.1
RIDGE = 0.5
EPS = 1e-05
MESH = pl.DeviceIdType.MESH

NT = 14
XR = 48
TE = 128
CE = 96
TH = 24
SR = 16
HALO = TH + V * SR
BLOCK = 4 * CR
NS = 12
OFFSETS = 2 * NS + 1
VMEM_LIMIT = 16 * 1024 * 1024
WHOLE = pl.BlockSpec(memory_space=pltpu.VMEM)
SCALARS = pl.BlockSpec(memory_space=pltpu.SMEM)


def tap_values():
    u = np.arange(-KR, KR + 1).astype(np.float64)
    rows = []
    for sigma, degree in zip(SIGMAS, DEGREES):
        t = u / sigma
        env = np.exp(-0.5 * t * t)
        he = [np.ones_like(t), t]
        for n in range(1, degree):
            he.append(t * he[n] - n * he[n - 1])
        for n in range(degree + 1):
            h = he[n] * env
            rows.append(h / np.sqrt(np.sum(h * h)))
    return np.stack(rows)


def psf_values():
    u = np.arange(-PR, PR + 1).astype(np.float64)
    g = np.exp(-0.5 * (u / PSF_SIGMA) ** 2)
    return g / g.sum()


def split_np(a):
    a = a.astype(np.float32)
    hi = a.astype(jnp.bfloat16)
    lo = (a - hi.astype(np.float32)).astype(jnp.bfloat16)
    return hi, lo


def band(taps, rows, cols, first):
    radius = (len(taps) - 1) // 2
    out = np.zeros((rows, cols))
    for r in range(rows):
        for u in range(-radius, radius + 1):
            c = r + first + u
            if 0 <= c < cols:
                out[r, c] = taps[u + radius]
    return out


def constants():
    taps = tap_values()
    bands = np.concatenate([band(taps[j], CE, TE, SR) for j in range(NT)], axis=0)
    hi, lo = split_np(bands)
    row_bands = np.concatenate([hi, lo], axis=1)
    p = psf_values()
    cols, rows = [], []
    for f in (p, p * p):
        cols += list(split_np(band(f, CW, CW, 0)))
        h, l = split_np(band(f, RT, CE, SR))
        rows.append(np.concatenate([h, l, h], axis=1))
    return row_bands, np.stack(cols), np.stack(rows)


def members_of():
    result, first_tap, first = [], 0, 0
    for degree in DEGREES:
        index = {}
        for i in range(degree + 1):
            for j in range(degree + 1 - i):
                index[(i, j)] = first + len(index)
        result.append((first_tap, degree, index))
        first_tap += degree + 1
        first += len(index)
    return result


def split(x):
    hi = x.astype(jnp.bfloat16)
    return hi, (x - hi.astype(jnp.float32)).astype(jnp.bfloat16)


def mm(a, b):
    return jnp.dot(a, b, preferred_element_type=jnp.float32)


def pack_kernel(
    patch, cell, image, variance, row, col, warp, live,
    out_image, out_variance, out_cell, table,
    image_in, variance_in, patch_in, cell_in, row_in, col_in, warp_in,
    count, slot_cell, sems,
):
    patches = out_cell.shape[0]
    slots = row.shape[1]
    pairs = (
        (patch, patch_in), (cell, cell_in), (image.at[0], image_in), (variance.at[0], variance_in),
        (row, row_in), (col, col_in), (warp, warp_in),
    )
    copies = [pltpu.make_async_copy(x, y, sems.at[n]) for n, (x, y) in enumerate(pairs)]
    for c in copies:
        c.start()
    out_image[...] = jnp.zeros_like(out_image)
    out_variance[...] = jnp.zeros_like(out_variance)

    def clear(n, _):
        count[n] = 0
        slot_cell[2 * n] = -1
        slot_cell[2 * n + 1] = -1
        return 0

    lax.fori_loop(0, patches, clear, 0)
    for c in copies:
        c.wait()

    def place(n, _):
        q = patch_in[n]
        rank = count[q]
        count[q] = rank + 1
        slot_cell[2 * q + rank] = cell_in[n]
        for x, y in ((image_in, out_image), (variance_in, out_variance)):
            a = x[n]
            for half in range(2):
                at = pl.multiple_of(q * BLOCK + half * 2 * CR + rank * CR, CR)
                y[pl.ds(at, CR), :] = a[:, half * 128 : (half + 1) * 128]
        return 0

    lax.fori_loop(0, image_in.shape[0], place, 0)
    lane = lax.broadcasted_iota(jnp.int32, (1, 128), 1)

    def tell(q, _):
        out_cell[q] = jnp.where(lane == 0, slot_cell[2 * q], slot_cell[2 * q + 1])
        return 0

    lax.fori_loop(0, patches, tell, 0)
    values = [row_in[0, n] for n in range(slots)] + [col_in[0, n] for n in range(slots)]
    values += [live[0, 0]] + [warp_in[v] for v in range(V)]
    line = jnp.zeros((1, 128), jnp.int32)
    for n, value in enumerate(values):
        line = jnp.where(lane == n, value, line)
    table[...] = line


def stamp_mask(mask, stamps, got_stamps, sub, subtiles, slots):
    row = lax.broadcasted_iota(jnp.int32, (RT, CW), 0)
    col = lax.broadcasted_iota(jnp.int32, (RT, CW), 1)
    flags = [(sub > 0).astype(jnp.int32), 1, (sub < subtiles - 1).astype(jnp.int32)]
    mask[...] = jnp.zeros_like(mask)
    for n, (flag, table) in enumerate(zip(flags, (got_stamps[0], stamps[...], got_stamps[1]))):
        count = table[:, 2 * slots : 2 * slots + 1] * flag
        for k in range(slots):
            near_row = jnp.abs(row - (n - 1) * RT - table[:, k : k + 1]) <= SH
            near_col = jnp.abs(col - table[:, slots + k : slots + k + 1]) <= SH
            mask[...] = jnp.where(near_row & near_col & (count > k), 1.0, mask[...])


def choose(cells):
    patches = cells.shape[0]
    lane = lax.broadcasted_iota(jnp.int32, (patches, 128), 1)
    table = cells[:, 0, :]
    wide = jnp.concatenate(
        [(table[:, rank : rank + 1] == lane).astype(jnp.float32) for rank in range(2)]
        + [jnp.zeros((128 - 2 * patches, 128), jnp.float32)] * (2 * patches < 128),
        axis=0,
    )
    return jnp.transpose(wide)[0 : V * NCELL, :].astype(jnp.bfloat16)


def combine(cells, table, got, out, left, right):
    patches = cells.shape[0]
    chosen = choose(cells)
    for half, ref in enumerate((left, right)):
        for r in range(CR):
            x = jnp.concatenate(
                [
                    got[pl.ds(half * 2 * CR + rank * CR + r, patches, stride=BLOCK), :]
                    for rank in range(2)
                ]
                + [jnp.zeros((128 - 2 * patches, 128), jnp.float32)] * (2 * patches < 128),
                axis=0,
            )
            hi = x.astype(jnp.bfloat16)
            mid, low = split(x - hi.astype(jnp.float32))
            y = mm(chosen, jnp.concatenate([hi, mid, low], axis=1))
            ref[pl.ds(r, V * NCELL, stride=CR), :] = y[:, 0:128] + y[:, 128:256] + y[:, 256:384]
    col = lax.broadcasted_iota(jnp.int32, (RT, CW), 1)
    for v in range(V):
        rows = slice(v * RT, (v + 1) * RT)
        off = jnp.broadcast_to(table[:, OFFSETS + v : OFFSETS + v + 1], (RT, CW))
        a = pltpu.roll(jnp.concatenate([left[rows, :], right[rows, :]], axis=1), WARP, 1)
        for bit in range(4):
            a = jnp.where((off & (1 << bit)) != 0, pltpu.roll(a, CW - (1 << bit), 1), a)
        source = col + off - WARP
        out[v, SR : SR + RT, :] = jnp.where((source >= 0) & (source < CW), a, 0.0)


def smooth(plane, col_hi, col_lo, row_taps):
    hi, lo = split(plane)
    yh, yl = split(mm(hi, col_hi) + mm(lo, col_hi) + mm(hi, col_lo))
    outs = []
    for v in range(V):
        a = slice(v * CE, (v + 1) * CE)
        outs.append(mm(row_taps, jnp.concatenate([yh[a], yh[a], yl[a]], axis=0)))
    return outs


def front_kernel(
    slots, sent_image, sent_variance, cells, stamps, row_bands_in, cols_in, rows_in,
    science, inverse, basis, gathered, root,
    got_image, got_variance, got_cells, got_stamps, left, right, template, up, down, above, below,
    text, filt, xleft, xright, mask, wide, wup, wdown, wabove, wbelow, weight, acc, gram,
    row_bands, cols, rows, send, recv, ring_send, ring_recv, all_send, all_recv, own,
):
    patches = cells.shape[0]
    subtiles = gathered.shape[0]
    me, sub = lax.axis_index("patch"), lax.axis_index("sub")
    peers = [lax.rem(sub + d, subtiles) for d in range(1, subtiles)]
    next_sub, last_sub = peers[0], peers[-1]
    has_above = (sub > 0).astype(jnp.float32)
    has_below = (sub < subtiles - 1).astype(jnp.float32)
    barrier = pltpu.get_barrier_semaphore()

    def greet(d, _):
        q = lax.rem(me + d, patches)
        pl.semaphore_signal(barrier, inc=1, device_id={"patch": q}, device_id_type=MESH)
        return 0

    lax.fori_loop(1, patches, greet, 0)
    for s in peers:
        pl.semaphore_signal(barrier, inc=1, device_id={"sub": s}, device_id_type=MESH)
    pl.semaphore_wait(barrier, patches - 1 + subtiles - 1)

    def block(q):
        return pl.ds(pl.multiple_of(q * BLOCK, BLOCK), BLOCK)

    def ends(n, source, to):
        if n == 0:
            return cells.at[to], got_cells.at[source]
        sent, got = (sent_image, got_image) if n == 1 else (sent_variance, got_variance)
        return sent.at[block(to), :], got.at[block(source), :]

    def copy(n, d, to, source):
        src, dst = ends(n, source, to)
        return pltpu.make_async_remote_copy(
            src_ref=src, dst_ref=dst, send_sem=send.at[n, d], recv_sem=recv.at[n, d],
            device_id={"patch": to}, device_id_type=MESH,
        )

    def ring(n, src, dst):
        return [
            pltpu.make_async_remote_copy(
                src_ref=s, dst_ref=r, send_sem=ring_send.at[n, k], recv_sem=ring_recv.at[n, k],
                device_id={"sub": to}, device_id_type=MESH,
            )
            for k, (s, r, to) in enumerate(zip(src, dst, (next_sub, last_sub)))
        ]

    def start_first(d, _):
        copy(0, d, lax.rem(me + d, patches), me).start()
        copy(1, d, lax.rem(me + d, patches), me).start()
        return 0

    lax.fori_loop(1, patches, start_first, 0)
    table_ring = ring(0, (stamps, stamps), (got_stamps.at[0], got_stamps.at[1]))
    for c in table_ring:
        c.start()

    def start_last(d, _):
        copy(2, d, lax.rem(me + d, patches), me).start()
        return 0

    lax.fori_loop(1, patches, start_last, 0)
    mine = [pltpu.make_async_copy(*ends(n, me, me), own.at[n]) for n in range(3)]
    fixed = ((row_bands_in, row_bands), (cols_in, cols), (rows_in, rows))
    mine += [pltpu.make_async_copy(x, y, own.at[3 + n]) for n, (x, y) in enumerate(fixed)]
    for c in mine:
        c.start()
    for c in mine:
        c.wait()
    for c in table_ring:
        c.wait()
    stamp_mask(mask, stamps, got_stamps, sub, subtiles, slots)

    def wait_first(d, _):
        source = lax.rem(me + patches - d, patches)
        copy(0, d, source, source).wait_recv()
        copy(1, d, source, source).wait_recv()
        return 0

    lax.fori_loop(1, patches, wait_first, 0)
    table = stamps[...]
    combine(got_cells, table, got_image, science, left, right)
    inner = slice(SR, SR + RT)
    template[...] = (science[0, inner] + science[1, inner] + science[2, inner] + science[3, inner]) / V
    up[0:TH, :] = template[0:TH, :]
    down[0:TH, :] = template[RT - TH : RT, :]
    for v in range(V):
        at = TH + v * SR
        up[at : at + SR, :] = science[v, SR : 2 * SR, :]
        down[at : at + SR, :] = science[v, RT : RT + SR, :]
    rims = ring(1, (down, up), (above, below))
    for c in rims:
        c.start()
    for c in rims:
        c.wait()
    above[...] = above[...] * has_above
    below[...] = below[...] * has_below
    for v in range(V):
        at = TH + v * SR
        science[v, 0:SR, :] = above[at : at + SR, :]
        science[v, SR + RT : CE, :] = below[at : at + SR, :]
    basis_images(science, template, above, below, row_bands, basis, xleft, xright, text, filt)

    def wait_last(d, _):
        source = lax.rem(me + patches - d, patches)
        copy(2, d, source, source).wait_recv()
        return 0

    lax.fori_loop(1, patches, wait_last, 0)
    combine(got_cells, table, got_variance, wide, left, right)
    for v in range(V):
        at = slice(v * SR, (v + 1) * SR)
        wup[at, :] = wide[v, SR : 2 * SR, :]
        wdown[at, :] = wide[v, RT : RT + SR, :]
    wrims = ring(2, (wdown, wup), (wabove, wbelow))
    for c in wrims:
        c.start()

    def invert(planes):
        q = (planes[0] + planes[1] + planes[2] + planes[3]) / (V * V)
        return [1.0 / (p + q + SKY_VAR) for p in planes]

    m = mask[...]
    for v, inv in enumerate(invert([wide[v, inner, :] for v in range(V)])):
        inverse[v * CE + SR : v * CE + SR + RT, :] = inv
        weight[v] = m * inv
    gram_of(weight, xleft, xright, acc, gram)
    parts = [
        pltpu.make_async_remote_copy(
            src_ref=gram, dst_ref=gathered.at[sub], send_sem=all_send.at[n], recv_sem=all_recv.at[n],
            device_id={"sub": s}, device_id_type=MESH,
        )
        for n, s in enumerate(peers)
    ]
    for c in parts:
        c.start()
    my_part = pltpu.make_async_copy(gram, gathered.at[sub], own.at[6])
    my_part.start()
    for c in wrims:
        c.wait()
    for ref, first, has in ((wabove, 0, has_above), (wbelow, SR + RT, has_below)):
        planes = [ref[v * SR : (v + 1) * SR, :] for v in range(V)]
        for v, inv in enumerate(invert(planes)):
            inverse[v * CE + first : v * CE + first + SR, :] = inv * has
    for v, den in enumerate(smooth(inverse[...], cols[2], cols[3], rows[1])):
        root[v] = lax.rsqrt(den)
    my_part.wait()
    for n, c in enumerate(parts):
        c.wait_send()
        source = peers[subtiles - 2 - n]
        pltpu.make_async_remote_copy(
            src_ref=gram, dst_ref=gathered.at[source], send_sem=all_send.at[n],
            recv_sem=all_recv.at[n], device_id={"sub": source}, device_id_type=MESH,
        ).wait_recv()

    def finish(d, _):
        for n in range(3):
            copy(n, d, lax.rem(me + d, patches), me).wait_send()
        return 0

    lax.fori_loop(1, patches, finish, 0)


def basis_images(
    science, template, above, below, row_bands, basis, xleft, xright, text, filt,
):
    taps = tap_values()

    def put(k, image):
        at = pl.ds(k, RT, stride=XR)
        xleft[at, :] = image[:, 0:128]
        xright[at, :] = image[:, 128:CW]

    zero8 = jnp.zeros((8, CW), jnp.float32)
    text[0:8, :] = zero8
    text[8:32, :] = above[0:TH, :]
    text[32:96, :] = template[...]
    text[96:120, :] = below[0:TH, :]
    text[120:128, :] = zero8
    col = lax.broadcasted_iota(jnp.int32, (8, CW), 1)

    def columns(i, _):
        rows = pl.ds(pl.multiple_of(i * 8, 8), 8)
        t = text[rows, :]
        sums = [None] * NT
        for u in range(0, KR + 1):
            if u:
                plus = jnp.where(col < CW - u, pltpu.roll(t, CW - u, 1), 0.0)
                minus = jnp.where(col >= u, pltpu.roll(t, u, 1), 0.0)
                even, odd = plus + minus, plus - minus
            first = 0
            for degree in DEGREES:
                for n in range(degree + 1):
                    j = first + n
                    h = float(np.float32(taps[j, KR + u]))
                    if u == 0:
                        sums[j] = t * h if n % 2 == 0 else None
                    else:
                        term = (even if n % 2 == 0 else odd) * h
                        sums[j] = term if sums[j] is None else sums[j] + term
                first += degree + 1
        for j in range(NT):
            filt[j, rows, :] = sums[j]
        return 0

    lax.fori_loop(0, TE // 8, columns, 0)

    for first_tap, degree, index in members_of():
        for j in range(degree + 1):
            count = degree + 1 - j
            lhs = row_bands[first_tap * CE : (first_tap + count) * CE, :]
            fh, fl = split(filt[first_tap + j])
            y = mm(lhs, jnp.concatenate([fh, fh], axis=0)) + mm(lhs[:, 0:TE], fl)
            for i in range(count):
                k = index[(i, j)]
                image = y[i * CE : (i + 1) * CE, :]
                basis[k] = image
                put(k, image[SR : SR + RT, :])
    put(NB, jnp.ones((RT, CW), jnp.float32))
    for v in range(V):
        put(NB + 1 + v, science[v, SR : SR + RT, :])
    for n in range(NB + 1 + V, XR):
        put(n, jnp.zeros((RT, CW), jnp.float32))


def gram_of(weight, xleft, xright, acc, gram):
    acc[...] = jnp.zeros_like(acc)
    step = 4

    def rows_of(i, _):
        lefts, rights = [], []
        for r0 in range(step):
            r = i * step + r0
            at = pl.ds(pl.multiple_of(r * XR, 8), XR)
            x = jnp.concatenate([xleft[at, :], xright[at, :]], axis=1)
            xh, xl = split(x)
            rights.append(jnp.concatenate([xh, xl, jnp.zeros((32, CW), jnp.bfloat16)], axis=0))
            his, los = [], []
            for v in range(V):
                lh, ll = split(x * weight[v, pl.ds(r, 1), :])
                his.append(lh)
                los.append(ll)
            lefts.append(jnp.concatenate(his + los, axis=0))
        left = jnp.concatenate(lefts, axis=1)
        right = jnp.concatenate(rights, axis=1)
        acc[...] += lax.dot_general(
            left, right, (((1,), (1,)), ((), ())), preferred_element_type=jnp.float32
        )
        return 0

    lax.fori_loop(0, RT // step, rows_of, 0)
    high = acc[0 : V * XR, :]
    total = high + pltpu.roll(high, 128 - XR, 1) + acc[V * XR : 2 * V * XR, :]
    lane = lax.broadcasted_iota(jnp.int32, total.shape, 1)
    total = jnp.where(lane < XR, total, 0.0)
    gram[...] = total[0 : 2 * XR, :] + pltpu.roll(total[2 * XR : 4 * XR, :], 64, 1)


def pick(x, index):
    return jnp.take_along_axis(x, index, axis=1, mode="promise_in_bounds")


def final_kernel(
    normalizer, gathered, basis, science, inverse, root, cols_in, rows_in,
    difference, significance, coef, dplane, cols, rows, sems,
):
    copies = [
        pltpu.make_async_copy(x, y, sems.at[n])
        for n, (x, y) in enumerate(((cols_in.at[0:2], cols), (rows_in.at[0], rows)))
    ]
    for c in copies:
        c.start()
    total = gathered[0] + gathered[1] + gathered[2] + gathered[3]
    total = total * (1.0 / normalizer)
    row = lax.broadcasted_iota(jnp.int32, (XR, 128), 0)
    lane = lax.broadcasted_iota(jnp.int32, (XR, 128), 1)
    part = lane // 64
    j = lane - part * 64
    base = part * 64
    halves, scales = [], []
    for half in range(2):
        a = total[half * XR : (half + 1) * XR, :]
        v = half + 2 * part
        e_col = lax.rsqrt(pick(a, base + row) + EPS)
        diag = jnp.sum(jnp.where(row == j, a, 0.0), axis=0, keepdims=True)
        e_row = lax.rsqrt(diag + EPS)
        scaled = a * e_col
        system = jnp.where(j <= NB, scaled * e_row, jnp.where(j == NB + 1 + v, scaled, 0.0))
        system = system + jnp.where(row == j, RIDGE, 0.0)
        halves.append(system)
        scales.append(e_col)
    for k in range(NB + 1):
        for half in range(2):
            a = halves[half]
            pivot_row = jnp.broadcast_to(a[k : k + 1, :], (XR, 128))
            pivot = pick(pivot_row, base + k)
            column = pick(a, base + k)
            column = jnp.where(row == k, pivot - 1.0, column)
            halves[half] = a - column * (pivot_row / pivot)
    for half in range(2):
        v = half + 2 * part
        a = pick(halves[half], base + NB + 1 + v) * scales[half]
        coef[half * XR : (half + 1) * XR, :] = pick(a, lane * 0)
        coef[(half + 2) * XR : (half + 3) * XR, :] = pick(a, lane * 0 + 64)

    def block(b, _):
        at = pl.ds(pl.multiple_of(b * 8, 8), 8)
        sums = []
        for v in range(V):
            a = coef[v * XR + NB : v * XR + NB + 1, :]
            sums.append(science[v, at, :] - jnp.concatenate([a, a], axis=1))
        for k in range(NB):
            c = basis[k, at, :]
            for v in range(V):
                a = coef[v * XR + k : v * XR + k + 1, :]
                sums[v] = sums[v] - c * jnp.concatenate([a, a], axis=1)
        for v in range(V):
            plane = pl.ds(pl.multiple_of(v * CE + b * 8, 8), 8)
            dplane[plane, :] = sums[v] * inverse[plane, :]

        @pl.when((b >= SR // 8) & (b < (SR + RT) // 8))
        def _():
            inner = pl.ds(pl.multiple_of(b * 8 - SR, 8), 8)
            for v in range(V):
                difference[v, inner, :] = sums[v]

        return 0

    lax.fori_loop(0, CE // 8, block, 0)
    for c in copies:
        c.wait()
    for v, num in enumerate(smooth(dplane[...], cols[0], cols[1], rows[...])):
        significance[v] = num * root[v]


def shape(*dims, dtype=jnp.float32):
    return jax.ShapeDtypeStruct(dims, dtype)


def params(**more):
    return pltpu.CompilerParams(vmem_limit_bytes=VMEM_LIMIT, **more)


def local(
    pieces_image, pieces_variance, piece_patch, piece_cell,
    stamp_row, stamp_col, stamp_count, warp_offsets,
):
    patches = lax.axis_size("patch")
    subtiles = lax.axis_size("sub")
    pieces = pieces_image.shape[1]
    slots = stamp_row.shape[1]
    dma, vmem, smem = pltpu.SemaphoreType.DMA, pltpu.VMEM, pltpu.SMEM
    far = pl.BlockSpec(memory_space=pltpu.HBM)

    def keep(*arrays):
        return [pltpu.with_memory_space_constraint(a, pltpu.HBM) for a in arrays]

    f32, i32, bf16 = jnp.float32, jnp.int32, jnp.bfloat16

    sent_shape = shape(patches * BLOCK, 128)
    sent_image, sent_variance, sent_cell, table = pl.pallas_call(
        pack_kernel,
        out_shape=(
            sent_shape, sent_shape, shape(patches, 1, 128, dtype=i32), shape(1, 128, dtype=i32),
        ),
        in_specs=[far] * 7 + [SCALARS],
        out_specs=(WHOLE,) * 4,
        scratch_shapes=[
            vmem((pieces, CR, CW), f32), vmem((pieces, CR, CW), f32),
            smem((pieces,), i32), smem((pieces,), i32),
            smem((1, slots), i32), smem((1, slots), i32), smem((V,), i32),
            smem((patches,), i32), smem((2 * patches,), i32), dma((7,)),
        ],
        compiler_params=params(),
        name="pack",
    )(
        *keep(
            piece_patch.reshape(-1), piece_cell.reshape(-1), pieces_image, pieces_variance,
            stamp_row, stamp_col, warp_offsets,
        ),
        stamp_count,
    )

    row_bands, cols, rows = keep(*[jnp.asarray(x) for x in constants()])
    rim, small_rim = vmem((HALO, CW), f32), vmem((V * SR, CW), f32)
    field = shape(V, RT, CW)
    science, inverse, basis, gathered, root = pl.pallas_call(
        functools.partial(front_kernel, slots),
        out_shape=(
            shape(V, CE, CW), shape(V * CE, CW), shape(NB, CE, CW), shape(subtiles, 2 * XR, 128), field,
        ),
        in_specs=[WHOLE] * 4 + [far] * 3,
        out_specs=(WHOLE,) * 5,
        scratch_shapes=[
            vmem((patches * BLOCK, 128), f32), vmem((patches * BLOCK, 128), f32),
            vmem((patches, 1, 128), i32), vmem((2, 1, 128), i32),
            vmem((V * RT, 128), f32), vmem((V * RT, 128), f32), vmem((RT, CW), f32),
            rim, rim, rim, rim,
            vmem((TE, CW), f32), vmem((NT, TE, CW), f32),
            vmem((RT * XR, 128), f32), vmem((RT * XR, 128), f32), vmem((RT, CW), f32),
            vmem((V, CE, CW), f32), small_rim, small_rim, small_rim, small_rim,
            vmem((V, RT, CW), f32), vmem((2 * V * XR, 128), f32), vmem((2 * XR, 128), f32),
            vmem(row_bands.shape, bf16), vmem(cols.shape, bf16), vmem(rows.shape, bf16),
            dma((3, patches)), dma((3, patches)), dma((3, 2)), dma((3, 2)),
            dma((subtiles - 1,)), dma((subtiles - 1,)), dma((7,)),
        ],
        compiler_params=pltpu.CompilerParams(
            vmem_limit_bytes=32 * 1024 * 1024, collective_id=0, has_side_effects=True
        ),
        name="front",
    )(sent_image, sent_variance, sent_cell, table, row_bands, cols, rows)

    normalizer = float(subtiles * slots * (2 * SH + 1) ** 2)
    difference, significance = pl.pallas_call(
        functools.partial(final_kernel, normalizer),
        out_shape=(field, field),
        in_specs=[WHOLE] * 5 + [far] * 2,
        out_specs=(WHOLE,) * 2,
        scratch_shapes=[
            vmem((V * XR, 128), f32), vmem((V * CE, CW), f32),
            vmem((2, CW, CW), bf16), vmem(rows.shape[1:], bf16), dma((2,)),
        ],
        compiler_params=params(),
        name="final",
    )(gathered, basis, science, inverse, root, cols, rows)
    return (difference[:, None], significance[:, None])


def solution(mesh):
    in_specs = (
        P("sub", "patch", None, None),
        P("sub", "patch", None, None),
        P("sub", "patch", None),
        P("sub", "patch"),
        P("patch", "sub"),
        P("patch", "sub"),
        P("patch", "sub"),
        P(),
    )
    out_specs = (P(None, "patch", "sub", None), P(None, "patch", "sub", None))
    return jax.shard_map(local, mesh=mesh, in_specs=in_specs, out_specs=out_specs, check_vma=False)
```

time: 103 us -> 85.9 us (0.83)
  local copies, waits for them, and re-layouts: 7.08 us -> 0 us
  starting transfers between devices: 6.2 us -> 0 us
  Pallas kernels: 86.9 us -> 84.5 us
    unnamed x20 -> x0, local copies, waits for them, and re-layouts: 7.08 us -> none
    ppermute x2 -> x0, starting transfers between devices: 6.2 us -> none  [the longest x1 4.28 us: local(): w_above = lax.ppermute(down, 'sub', down_pairs)]
    pallas_call x5 -> x2, Pallas kernels: 79.5 us -> 78 us  [the longest x1 76.1 us: local(): pl.pallas_call(functools.partial(front_kernel, slots), out_shape=(shape(V...]
  transfers between devices with their start and end apart: 2 -> 0, of which waited for: 0 -> 0; matrix products, arithmetic and copies ran while one was open for 0% -> 0% of each run, Pallas kernels for 11% -> 0%
where the time goes in v4:
time: 85.9 us; the launch traced here: 85.8 us
  Pallas kernels  84.5 us (98%)
  between operations  1.29 us (2%)
    pallas_call x1, Pallas kernels, local(): pl.pallas_call(functools.partial(front_kernel, slots), out_shape=(shape(V...  76.1 us
    pallas_call x1, Pallas kernels, local(): pl.pallas_call(functools.partial(final_kernel, normalizer), out_shape=(fi...  6.51 us
    pallas_call x1, Pallas kernels, local(): pl.pallas_call(pack_kernel, out_shape=(sent_shape, sent_shape, shape(patc...  1.94 us

profile of v4, /device:TPU:1, one launch (start us, length us, event | category | flops | bytes accessed | tf_op | source)
XLA Modules:
  0.0 85.8 jit_solution(8894896855695802051)
XLA Ops:
  1.3 1.9 %pack.1 = (f32[2048,128]{1,0:T(8,128)S(1)}, f32[2048,128]{1,0:T(8,128)S(1)}, s32[64,1,128]{2,1,0:T(1,128)S(1)}, s32[1,128]{1,0:T(1,128)S(1)}) custom-call(s32[32]{0:T(128)} %bitcast.8, s32[32]{0:T(128)} %bitcast.9, f32[1,32,8,256]{3,2,1,0:T(8,128)} %image.1, f32[1,32,8,256]{3,2,1,0:T(8,128)} %variance.1, s32[1,12]{1,0:T(1,128)} %row.1, s32[1,12]{1,0:T(1,128)} %col.1, ...), custom_call_target="tpu_custom_call" | custom-call | tf_op jit(solution)/shard_map/pack/pallas_call | solution.py:604
  3.2 76.1 %front.1 = (f32[4,96,256]{2,1,0:T(8,128)S(1)}, f32[384,256]{1,0:T(8,128)S(1)}, f32[40,96,256]{2,1,0:T(8,128)S(1)}, f32[4,96,128]{2,1,0:T(8,128)S(1)}, f32[4,64,256]{2,1,0:T(8,128)S(1)}) custom-call(f32[2048,128]{1,0:T(8,128)S(1)} %get-tuple-element.13.sent_image, f32[2048,128]{1,0:T(8,128)S(1)} %get-tuple-element.14.sent_variance, ...), custom_call_target="tpu_custom_call" | custom-call | tf_op jit(solution)/shard_map/front/pallas_call | solution.py:630
  79.3 6.5 %final.1 = (f32[4,64,256]{2,1,0:T(8,128)}, f32[4,64,256]{2,1,0:T(8,128)}) custom-call(f32[4,96,128]{2,1,0:T(8,128)S(1)} %get-tuple-element.17.gathered, f32[40,96,256]{2,1,0:T(8,128)S(1)} %get-tuple-element.18.basis, f32[4,96,256]{2,1,0:T(8,128)S(1)} %get-tuple-element.19.science, f32[384,256]{1,0:T(8,128)S(1)} %get-tuple-element.20.inverse, ...), custom_call_target="tpu_custom_call" | custom-call | tf_op jit(solution)/shard_map/final/pallas_call | solution.py:657

commit v5 on v4

--- a/solution.py
+++ b/solution.py
@@ -36,6 +36,8 @@
 SR = 16
 HALO = TH + V * SR
 BLOCK = 4 * CR
+RC = CR // 2
+PART = 4 * RC
 NS = 12
 OFFSETS = 2 * NS + 1
 VMEM_LIMIT = 16 * 1024 * 1024
@@ -120,7 +122,7 @@
 
 def pack_kernel(
     patch, cell, image, variance, row, col, warp, live,
-    out_image, out_variance, out_cell, table,
+    out_image, out_first, out_last, out_cell, table,
     image_in, variance_in, patch_in, cell_in, row_in, col_in, warp_in,
     count, slot_cell, sems,
 ):
@@ -134,7 +136,8 @@
     for c in copies:
         c.start()
     out_image[...] = jnp.zeros_like(out_image)
-    out_variance[...] = jnp.zeros_like(out_variance)
+    for ref in (out_first, out_last):
+        ref[...] = jnp.zeros_like(ref)
 
     def clear(n, _):
         count[n] = 0
@@ -151,13 +154,19 @@
         rank = count[q]
         count[q] = rank + 1
         slot_cell[2 * q + rank] = cell_in[n]
-        for x, y in ((image_in, out_image), (variance_in, out_variance)):
-            a = x[n]
-            for half in range(2):
-                at = pl.multiple_of(q * BLOCK + half * 2 * CR + rank * CR, CR)
-                y[pl.ds(at, CR), :] = a[:, half * 128 : (half + 1) * 128]
+        a, b = image_in[n], variance_in[n]
+        mine = upper == rank
+        for half in range(2):
+            lanes = slice(half * 128, (half + 1) * 128)
+            at = pl.multiple_of(q * BLOCK + half * 2 * CR + rank * CR, CR)
+            out_image[pl.ds(at, CR), :] = a[:, lanes]
+            at = pl.ds(pl.multiple_of(q * PART + half * CR, CR), CR)
+            for k, y in enumerate((out_first, out_last)):
+                rows = b[k * RC : (k + 1) * RC, lanes]
+                y[at, :] = jnp.where(mine, jnp.concatenate([rows, rows], axis=0), y[at, :])
         return 0
 
+    upper = lax.broadcasted_iota(jnp.int32, (CR, 128), 0) // RC
     lax.fori_loop(0, image_in.shape[0], place, 0)
     lane = lax.broadcasted_iota(jnp.int32, (1, 128), 1)
 
@@ -199,14 +208,12 @@
     return jnp.transpose(wide)[0 : V * NCELL, :].astype(jnp.bfloat16)
 
 
-def combine(cells, table, got, out, left, right):
-    patches = cells.shape[0]
-    chosen = choose(cells)
+def combine(chosen, patches, table, got, rows, put_field, left, right):
     for half, ref in enumerate((left, right)):
-        for r in range(CR):
+        for r in range(rows):
             x = jnp.concatenate(
                 [
-                    got[pl.ds(half * 2 * CR + rank * CR + r, patches, stride=BLOCK), :]
+                    got[pl.ds((half * 2 + rank) * rows + r, patches, stride=4 * rows), :]
                     for rank in range(2)
                 ]
                 + [jnp.zeros((128 - 2 * patches, 128), jnp.float32)] * (2 * patches < 128),
@@ -215,16 +222,17 @@
             hi = x.astype(jnp.bfloat16)
             mid, low = split(x - hi.astype(jnp.float32))
             y = mm(chosen, jnp.concatenate([hi, mid, low], axis=1))
-            ref[pl.ds(r, V * NCELL, stride=CR), :] = y[:, 0:128] + y[:, 128:256] + y[:, 256:384]
-    col = lax.broadcasted_iota(jnp.int32, (RT, CW), 1)
+            ref[pl.ds(r, V * NCELL, stride=rows), :] = y[:, 0:128] + y[:, 128:256] + y[:, 256:384]
+    size = NCELL * rows
+    col = lax.broadcasted_iota(jnp.int32, (size, CW), 1)
     for v in range(V):
-        rows = slice(v * RT, (v + 1) * RT)
-        off = jnp.broadcast_to(table[:, OFFSETS + v : OFFSETS + v + 1], (RT, CW))
-        a = pltpu.roll(jnp.concatenate([left[rows, :], right[rows, :]], axis=1), WARP, 1)
+        at = slice(v * size, (v + 1) * size)
+        off = jnp.broadcast_to(table[:, OFFSETS + v : OFFSETS + v + 1], (size, CW))
+        a = pltpu.roll(jnp.concatenate([left[at, :], right[at, :]], axis=1), WARP, 1)
         for bit in range(4):
             a = jnp.where((off & (1 << bit)) != 0, pltpu.roll(a, CW - (1 << bit), 1), a)
         source = col + off - WARP
-        out[v, SR : SR + RT, :] = jnp.where((source >= 0) & (source < CW), a, 0.0)
+        put_field(v, jnp.where((source >= 0) & (source < CW), a, 0.0))
 
 
 def smooth(plane, col_hi, col_lo, row_taps):
@@ -238,10 +246,10 @@
 
 
 def front_kernel(
-    slots, sent_image, sent_variance, cells, stamps, row_bands_in, cols_in, rows_in,
+    slots, sent_image, sent_first, sent_last, cells, stamps, row_bands_in, cols_in, rows_in,
     science, inverse, basis, gathered, root,
-    got_image, got_variance, got_cells, got_stamps, left, right, template, up, down, above, below,
-    text, filt, xleft, xright, mask, wide, wup, wdown, wabove, wbelow, weight, acc, gram,
+    got_image, got_first, got_last, got_cells, got_stamps, left, right, template, up, down, above, below,
+    text, filt, xleft, xright, mask, half_mask, wide, wup, wdown, wabove, wbelow, weight, acc, gram,
     row_bands, cols, rows, send, recv, ring_send, ring_recv, all_send, all_recv, own,
 ):
     patches = cells.shape[0]
@@ -263,20 +271,31 @@
         pl.semaphore_signal(barrier, inc=1, device_id={"sub": s}, device_id_type=MESH)
     pl.semaphore_wait(barrier, patches - 1 + subtiles - 1)
 
-    def block(q):
-        return pl.ds(pl.multiple_of(q * BLOCK, BLOCK), BLOCK)
-
-    def ends(n, source, to):
-        if n == 0:
-            return cells.at[to], got_cells.at[source]
-        sent, got = (sent_image, got_image) if n == 1 else (sent_variance, got_variance)
-        return sent.at[block(to), :], got.at[block(source), :]
-
-    def copy(n, d, to, source):
-        src, dst = ends(n, source, to)
+    pairs = (
+        (cells, got_cells, 1), (sent_image, got_image, BLOCK),
+        (sent_first, got_first, PART), (sent_last, got_last, PART),
+    )
+
+    def ends(n, to, source):
+        src, dst, size = pairs[n]
+        src_at = pl.ds(pl.multiple_of(to * size, size), size)
+        dst_at = pl.ds(pl.multiple_of(source * size, size), size)
+        return src.at[src_at], dst.at[dst_at]
+
+    def start(n, d):
+        to = lax.rem(me + d, patches)
+        src, dst = ends(n, to, me)
+        pltpu.make_async_remote_copy(
+            src_ref=src, dst_ref=dst, send_sem=send.at[n], recv_sem=recv.at[n],
+            device_id={"patch": to}, device_id_type=MESH,
+        ).start()
+
+    def whole(n):
+        src, dst, size = pairs[n]
+        at = pl.ds(0, (patches - 1) * size)
         return pltpu.make_async_remote_copy(
-            src_ref=src, dst_ref=dst, send_sem=send.at[n, d], recv_sem=recv.at[n, d],
-            device_id={"patch": to}, device_id_type=MESH,
+            src_ref=src.at[at], dst_ref=dst.at[at], send_sem=send.at[n], recv_sem=recv.at[n],
+            device_id={"patch": lax.rem(me + 1, patches)}, device_id_type=MESH,
         )
 
     def ring(n, src, dst):
@@ -289,8 +308,8 @@
         ]
 
     def start_first(d, _):
-        copy(0, d, lax.rem(me + d, patches), me).start()
-        copy(1, d, lax.rem(me + d, patches), me).start()
+        start(0, d)
+        start(1, d)
         return 0
 
     lax.fori_loop(1, patches, start_first, 0)
@@ -298,14 +317,16 @@
     for c in table_ring:
         c.start()
 
-    def start_last(d, _):
-        copy(2, d, lax.rem(me + d, patches), me).start()
-        return 0
-
-    lax.fori_loop(1, patches, start_last, 0)
-    mine = [pltpu.make_async_copy(*ends(n, me, me), own.at[n]) for n in range(3)]
+    for n in (2, 3):
+
+        def start_chunk(d, _):
+            start(n, d)
+            return 0
+
+        lax.fori_loop(1, patches, start_chunk, 0)
+    mine = [pltpu.make_async_copy(*ends(n, me, me), own.at[n]) for n in range(4)]
     fixed = ((row_bands_in, row_bands), (cols_in, cols), (rows_in, rows))
-    mine += [pltpu.make_async_copy(x, y, own.at[3 + n]) for n, (x, y) in enumerate(fixed)]
+    mine += [pltpu.make_async_copy(x, y, own.at[4 + n]) for n, (x, y) in enumerate(fixed)]
     for c in mine:
         c.start()
     for c in mine:
@@ -314,15 +335,19 @@
         c.wait()
     stamp_mask(mask, stamps, got_stamps, sub, subtiles, slots)
 
-    def wait_first(d, _):
-        source = lax.rem(me + patches - d, patches)
-        copy(0, d, source, source).wait_recv()
-        copy(1, d, source, source).wait_recv()
-        return 0
-
-    lax.fori_loop(1, patches, wait_first, 0)
+    for c in range(NCELL):
+        for k in range(2):
+            half_mask[k, c * RC : (c + 1) * RC, :] = mask[c * CR + k * RC : c * CR + (k + 1) * RC, :]
+    acc[...] = jnp.zeros_like(acc)
+    whole(0).wait_recv()
+    whole(1).wait_recv()
     table = stamps[...]
-    combine(got_cells, table, got_image, science, left, right)
+    chosen = choose(got_cells)
+
+    def put_science(v, field):
+        science[v, SR : SR + RT, :] = field
+
+    combine(chosen, patches, table, got_image, CR, put_science, left, right)
     inner = slice(SR, SR + RT)
     template[...] = (science[0, inner] + science[1, inner] + science[2, inner] + science[3, inner]) / V
     up[0:TH, :] = template[0:TH, :]
@@ -344,30 +369,36 @@
         science[v, SR + RT : CE, :] = below[at : at + SR, :]
     basis_images(science, template, above, below, row_bands, basis, xleft, xright, text, filt)
 
-    def wait_last(d, _):
-        source = lax.rem(me + patches - d, patches)
-        copy(2, d, source, source).wait_recv()
-        return 0
-
-    lax.fori_loop(1, patches, wait_last, 0)
-    combine(got_cells, table, got_variance, wide, left, right)
-    for v in range(V):
-        at = slice(v * SR, (v + 1) * SR)
-        wup[at, :] = wide[v, SR : 2 * SR, :]
-        wdown[at, :] = wide[v, RT : RT + SR, :]
-    wrims = ring(2, (wdown, wup), (wabove, wbelow))
-    for c in wrims:
-        c.start()
+    whole(0).wait_send()
+    whole(1).wait_send()
 
     def invert(planes):
         q = (planes[0] + planes[1] + planes[2] + planes[3]) / (V * V)
         return [1.0 / (p + q + SKY_VAR) for p in planes]
 
-    m = mask[...]
-    for v, inv in enumerate(invert([wide[v, inner, :] for v in range(V)])):
-        inverse[v * CE + SR : v * CE + SR + RT, :] = inv
-        weight[v] = m * inv
-    gram_of(weight, xleft, xright, acc, gram)
+    def put_wide(v, field):
+        wide[v] = field
+
+    wrims = ring(2, (wdown, wup), (wabove, wbelow))
+    for k, got in enumerate((got_first, got_last)):
+        whole(2 + k).wait_recv()
+        combine(chosen, patches, table, got, RC, put_wide, left, right)
+        for v in range(V):
+            for c in range(SR // CR):
+                at = slice(v * SR + c * CR + k * RC, v * SR + c * CR + (k + 1) * RC)
+                low = NCELL - SR // CR + c
+                wup[at, :] = wide[v, c * RC : (c + 1) * RC, :]
+                wdown[at, :] = wide[v, low * RC : (low + 1) * RC, :]
+        if k == 1:
+            for c in wrims:
+                c.start()
+        for v, inv in enumerate(invert([wide[v] for v in range(V)])):
+            weight[v] = half_mask[k] * inv
+            for c in range(NCELL):
+                first = v * CE + SR + c * CR + k * RC
+                inverse[first : first + RC, :] = inv[c * RC : (c + 1) * RC, :]
+        gram_of(k, weight, xleft, xright, acc)
+    gram_total(acc, gram)
     parts = [
         pltpu.make_async_remote_copy(
             src_ref=gram, dst_ref=gathered.at[sub], send_sem=all_send.at[n], recv_sem=all_recv.at[n],
@@ -377,7 +408,7 @@
     ]
     for c in parts:
         c.start()
-    my_part = pltpu.make_async_copy(gram, gathered.at[sub], own.at[6])
+    my_part = pltpu.make_async_copy(gram, gathered.at[sub], own.at[7])
     my_part.start()
     for c in wrims:
         c.wait()
@@ -396,12 +427,8 @@
             recv_sem=all_recv.at[n], device_id={"sub": source}, device_id_type=MESH,
         ).wait_recv()
 
-    def finish(d, _):
-        for n in range(3):
-            copy(n, d, lax.rem(me + d, patches), me).wait_send()
-        return 0
-
-    lax.fori_loop(1, patches, finish, 0)
+    whole(2).wait_send()
+    whole(3).wait_send()
 
 
 def basis_images(
@@ -466,32 +493,31 @@
         put(n, jnp.zeros((RT, CW), jnp.float32))
 
 
-def gram_of(weight, xleft, xright, acc, gram):
-    acc[...] = jnp.zeros_like(acc)
-    step = 4
-
-    def rows_of(i, _):
+def gram_of(k, weight, xleft, xright, acc):
+    def cell(i, _):
         lefts, rights = [], []
-        for r0 in range(step):
-            r = i * step + r0
+        for r0 in range(RC):
+            r = i * CR + k * RC + r0
             at = pl.ds(pl.multiple_of(r * XR, 8), XR)
             x = jnp.concatenate([xleft[at, :], xright[at, :]], axis=1)
             xh, xl = split(x)
             rights.append(jnp.concatenate([xh, xl, jnp.zeros((32, CW), jnp.bfloat16)], axis=0))
             his, los = [], []
             for v in range(V):
-                lh, ll = split(x * weight[v, pl.ds(r, 1), :])
+                lh, ll = split(x * weight[v, pl.ds(i * RC + r0, 1), :])
                 his.append(lh)
                 los.append(ll)
             lefts.append(jnp.concatenate(his + los, axis=0))
-        left = jnp.concatenate(lefts, axis=1)
-        right = jnp.concatenate(rights, axis=1)
         acc[...] += lax.dot_general(
-            left, right, (((1,), (1,)), ((), ())), preferred_element_type=jnp.float32
+            jnp.concatenate(lefts, axis=1), jnp.concatenate(rights, axis=1),
+            (((1,), (1,)), ((), ())), preferred_element_type=jnp.float32,
         )
         return 0
 
-    lax.fori_loop(0, RT // step, rows_of, 0)
+    lax.fori_loop(0, NCELL, cell, 0)
+
+
+def gram_total(acc, gram):
     high = acc[0 : V * XR, :]
     total = high + pltpu.roll(high, 128 - XR, 1) + acc[V * XR : 2 * V * XR, :]
     lane = lax.broadcasted_iota(jnp.int32, total.shape, 1)
@@ -600,14 +626,15 @@
 
     f32, i32, bf16 = jnp.float32, jnp.int32, jnp.bfloat16
 
-    sent_shape = shape(patches * BLOCK, 128)
-    sent_image, sent_variance, sent_cell, table = pl.pallas_call(
+    sent_shape, part_shape = shape(patches * BLOCK, 128), shape(patches * PART, 128)
+    sent_image, sent_first, sent_last, sent_cell, table = pl.pallas_call(
         pack_kernel,
         out_shape=(
-            sent_shape, sent_shape, shape(patches, 1, 128, dtype=i32), shape(1, 128, dtype=i32),
+            sent_shape, part_shape, part_shape, shape(patches, 1, 128, dtype=i32),
+            shape(1, 128, dtype=i32),
         ),
         in_specs=[far] * 7 + [SCALARS],
-        out_specs=(WHOLE,) * 4,
+        out_specs=(WHOLE,) * 5,
         scratch_shapes=[
             vmem((pieces, CR, CW), f32), vmem((pieces, CR, CW), f32),
             smem((pieces,), i32), smem((pieces,), i32),
@@ -632,26 +659,27 @@
         out_shape=(
             shape(V, CE, CW), shape(V * CE, CW), shape(NB, CE, CW), shape(subtiles, 2 * XR, 128), field,
         ),
-        in_specs=[WHOLE] * 4 + [far] * 3,
+        in_specs=[WHOLE] * 5 + [far] * 3,
         out_specs=(WHOLE,) * 5,
         scratch_shapes=[
-            vmem((patches * BLOCK, 128), f32), vmem((patches * BLOCK, 128), f32),
+            vmem((patches * BLOCK, 128), f32),
+            vmem((patches * PART, 128), f32), vmem((patches * PART, 128), f32),
             vmem((patches, 1, 128), i32), vmem((2, 1, 128), i32),
             vmem((V * RT, 128), f32), vmem((V * RT, 128), f32), vmem((RT, CW), f32),
             rim, rim, rim, rim,
             vmem((TE, CW), f32), vmem((NT, TE, CW), f32),
             vmem((RT * XR, 128), f32), vmem((RT * XR, 128), f32), vmem((RT, CW), f32),
-            vmem((V, CE, CW), f32), small_rim, small_rim, small_rim, small_rim,
-            vmem((V, RT, CW), f32), vmem((2 * V * XR, 128), f32), vmem((2 * XR, 128), f32),
+            vmem((2, NCELL * RC, CW), f32), vmem((V, NCELL * RC, CW), f32), small_rim, small_rim, small_rim, small_rim,
+            vmem((V, NCELL * RC, CW), f32), vmem((2 * V * XR, 128), f32), vmem((2 * XR, 128), f32),
             vmem(row_bands.shape, bf16), vmem(cols.shape, bf16), vmem(rows.shape, bf16),
-            dma((3, patches)), dma((3, patches)), dma((3, 2)), dma((3, 2)),
-            dma((subtiles - 1,)), dma((subtiles - 1,)), dma((7,)),
+            dma((4,)), dma((4,)), dma((3, 2)), dma((3, 2)),
+            dma((subtiles - 1,)), dma((subtiles - 1,)), dma((8,)),
         ],
         compiler_params=pltpu.CompilerParams(
             vmem_limit_bytes=32 * 1024 * 1024, collective_id=0, has_side_effects=True
         ),
         name="front",
-    )(sent_image, sent_variance, sent_cell, table, row_bands, cols, rows)
+    )(sent_image, sent_first, sent_last, sent_cell, table, row_bands, cols, rows)
 
     normalizer = float(subtiles * slots * (2 * SH + 1) ** 2)
     difference, significance = pl.pallas_call(

time: 85.9 us -> 79.2 us (0.922)
  Pallas kernels: 84.5 us -> 77.7 us
    pallas_call x1, Pallas kernels: 76.1 us -> 69.3 us  [local(): pl.pallas_call(functools.partial(front_kernel, slots), out_shape=(shape(V...]
where the time goes in v5:
time: 79.2 us; the launch traced here: 79 us
  Pallas kernels  77.7 us (98%)
  between operations  1.29 us (2%)
    pallas_call x1, Pallas kernels, local(): pl.pallas_call(functools.partial(front_kernel, slots), out_shape=(shape(V...  69.3 us
    pallas_call x1, Pallas kernels, local(): pl.pallas_call(functools.partial(final_kernel, normalizer), out_shape=(fi...  6.51 us
    pallas_call x1, Pallas kernels, local(): pl.pallas_call(pack_kernel, out_shape=(sent_shape, part_shape, part_shape...  1.9 us

profile of v5, /device:TPU:1, one launch (start us, length us, event | category | flops | bytes accessed | tf_op | source)
XLA Modules:
  0.0 79.0 jit_solution(10278991779085563564)
XLA Ops:
  1.3 1.9 %pack.1 = (f32[2048,128]{1,0:T(8,128)S(1)}, f32[1024,128]{1,0:T(8,128)S(1)}, f32[1024,128]{1,0:T(8,128)S(1)}, s32[64,1,128]{2,1,0:T(1,128)S(1)}, s32[1,128]{1,0:T(1,128)S(1)}) custom-call(s32[32]{0:T(128)} %bitcast.8, s32[32]{0:T(128)} %bitcast.9, f32[1,32,8,256]{3,2,1,0:T(8,128)} %image.1, f32[1,32,8,256]{3,2,1,0:T(8,128)} %variance.1, s32[1,12]{1,0:T(1,128)} %row.1, ...), custom_call_target="tpu_custom_call" | custom-call | tf_op jit(solution)/shard_map/pack/pallas_call | solution.py:630
  3.2 69.3 %front.1 = (f32[4,96,256]{2,1,0:T(8,128)S(1)}, f32[384,256]{1,0:T(8,128)S(1)}, f32[40,96,256]{2,1,0:T(8,128)S(1)}, f32[4,96,128]{2,1,0:T(8,128)S(1)}, f32[4,64,256]{2,1,0:T(8,128)S(1)}) custom-call(f32[2048,128]{1,0:T(8,128)S(1)} %get-tuple-element.14.sent_image, f32[1024,128]{1,0:T(8,128)S(1)} %get-tuple-element.15.sent_first, ...), custom_call_target="tpu_custom_call" | custom-call | tf_op jit(solution)/shard_map/front/pallas_call | solution.py:657
  72.5 6.5 %final.1 = (f32[4,64,256]{2,1,0:T(8,128)}, f32[4,64,256]{2,1,0:T(8,128)}) custom-call(f32[4,96,128]{2,1,0:T(8,128)S(1)} %get-tuple-element.19.gathered, f32[40,96,256]{2,1,0:T(8,128)S(1)} %get-tuple-element.20.basis, f32[4,96,256]{2,1,0:T(8,128)S(1)} %get-tuple-element.21.science, f32[384,256]{1,0:T(8,128)S(1)} %get-tuple-element.22.inverse, ...), custom_call_target="tpu_custom_call" | custom-call | tf_op jit(solution)/shard_map/final/pallas_call | solution.py:685

commit v6 on v5

--- a/solution.py
+++ b/solution.py
@@ -38,6 +38,7 @@
 BLOCK = 4 * CR
 RC = CR // 2
 PART = 4 * RC
+PLANE = 8
 NS = 12
 OFFSETS = 2 * NS + 1
 VMEM_LIMIT = 16 * 1024 * 1024
@@ -86,7 +87,12 @@
 
 def constants():
     taps = tap_values()
-    bands = np.concatenate([band(taps[j], CE, TE, SR) for j in range(NT)], axis=0)
+    every = [band(taps[j], CE, TE, SR) for j in range(NT)]
+    bands = np.concatenate(
+        [b[SR : SR + RT] for b in every]
+        + [np.concatenate([b[0:SR], b[SR + RT : CE]], axis=0) for b in every],
+        axis=0,
+    )
     hi, lo = split_np(bands)
     row_bands = np.concatenate([hi, lo], axis=1)
     p = psf_values()
@@ -120,29 +126,24 @@
     return jnp.dot(a, b, preferred_element_type=jnp.float32)
 
 
-def pack_kernel(
-    patch, cell, image, variance, row, col, warp, live,
-    out_image, out_first, out_last, out_cell, table,
-    image_in, variance_in, patch_in, cell_in, row_in, col_in, warp_in,
-    count, slot_cell, sems,
+def plan_kernel(
+    patch, cell, row, col, warp, live,
+    out_index, out_cell, table,
+    patch_in, cell_in, row_in, col_in, warp_in, count, slot_cell, slot_index, sems,
 ):
     patches = out_cell.shape[0]
+    pieces = patch.shape[0]
     slots = row.shape[1]
-    pairs = (
-        (patch, patch_in), (cell, cell_in), (image.at[0], image_in), (variance.at[0], variance_in),
-        (row, row_in), (col, col_in), (warp, warp_in),
-    )
+    pairs = ((patch, patch_in), (cell, cell_in), (row, row_in), (col, col_in), (warp, warp_in))
     copies = [pltpu.make_async_copy(x, y, sems.at[n]) for n, (x, y) in enumerate(pairs)]
     for c in copies:
         c.start()
-    out_image[...] = jnp.zeros_like(out_image)
-    for ref in (out_first, out_last):
-        ref[...] = jnp.zeros_like(ref)
 
     def clear(n, _):
         count[n] = 0
-        slot_cell[2 * n] = -1
-        slot_cell[2 * n + 1] = -1
+        for rank in range(2):
+            slot_cell[2 * n + rank] = -1
+            slot_index[2 * n + rank] = pieces
         return 0
 
     lax.fori_loop(0, patches, clear, 0)
@@ -154,27 +155,18 @@
         rank = count[q]
         count[q] = rank + 1
         slot_cell[2 * q + rank] = cell_in[n]
-        a, b = image_in[n], variance_in[n]
-        mine = upper == rank
-        for half in range(2):
-            lanes = slice(half * 128, (half + 1) * 128)
-            at = pl.multiple_of(q * BLOCK + half * 2 * CR + rank * CR, CR)
-            out_image[pl.ds(at, CR), :] = a[:, lanes]
-            at = pl.ds(pl.multiple_of(q * PART + half * CR, CR), CR)
-            for k, y in enumerate((out_first, out_last)):
-                rows = b[k * RC : (k + 1) * RC, lanes]
-                y[at, :] = jnp.where(mine, jnp.concatenate([rows, rows], axis=0), y[at, :])
+        slot_index[2 * q + rank] = n
         return 0
 
-    upper = lax.broadcasted_iota(jnp.int32, (CR, 128), 0) // RC
-    lax.fori_loop(0, image_in.shape[0], place, 0)
+    lax.fori_loop(0, pieces, place, 0)
     lane = lax.broadcasted_iota(jnp.int32, (1, 128), 1)
 
-    def tell(q, _):
+    def tell(q, line):
         out_cell[q] = jnp.where(lane == 0, slot_cell[2 * q], slot_cell[2 * q + 1])
-        return 0
-
-    lax.fori_loop(0, patches, tell, 0)
+        line = jnp.where(lane == 2 * q, slot_index[2 * q], line)
+        return jnp.where(lane == 2 * q + 1, slot_index[2 * q + 1], line)
+
+    out_index[...] = lax.fori_loop(0, patches, tell, jnp.zeros((1, 128), jnp.int32))
     values = [row_in[0, n] for n in range(slots)] + [col_in[0, n] for n in range(slots)]
     values += [live[0, 0]] + [warp_in[v] for v in range(V)]
     line = jnp.zeros((1, 128), jnp.int32)
@@ -246,11 +238,13 @@
 
 
 def front_kernel(
-    slots, sent_image, sent_first, sent_last, cells, stamps, row_bands_in, cols_in, rows_in,
+    slots, index, cells, stamps, image_in, variance_in, row_bands_in, cols_in, rows_in,
     science, inverse, basis, gathered, root,
+    held_0, held_1, held_2, held_3, held_4, held_5, near_index, index_of, sent_image, sent_first, sent_last,
     got_image, got_first, got_last, got_cells, got_stamps, left, right, template, up, down, above, below,
     text, filt, xleft, xright, mask, half_mask, wide, wup, wdown, wabove, wbelow, weight, acc, gram,
-    row_bands, cols, rows, send, recv, ring_send, ring_recv, all_send, all_recv, own,
+    row_bands, cols, rows, send, recv, ring_send, ring_recv, all_send, all_recv,
+    far_send, far_recv, index_send, index_recv, own,
 ):
     patches = cells.shape[0]
     subtiles = gathered.shape[0]
@@ -259,6 +253,11 @@
     next_sub, last_sub = peers[0], peers[-1]
     has_above = (sub > 0).astype(jnp.float32)
     has_below = (sub < subtiles - 1).astype(jnp.float32)
+    held = (held_0, held_1, held_2, held_3, held_4, held_5)
+    pieces = image_in.shape[1]
+    planes = patches // PLANE
+    z, flat = me // PLANE, lax.rem(me, PLANE)
+    after, before = lax.rem(z + 1, planes), lax.rem(z + planes - 1, planes)
     barrier = pltpu.get_barrier_semaphore()
 
     def greet(d, _):
@@ -269,34 +268,122 @@
     lax.fori_loop(1, patches, greet, 0)
     for s in peers:
         pl.semaphore_signal(barrier, inc=1, device_id={"sub": s}, device_id_type=MESH)
+    mine = [
+        pltpu.make_async_copy(x, y, own.at[n])
+        for n, (x, y) in enumerate(
+            (
+                (image_in.at[0], held[0].at[pl.ds(0, pieces)]),
+                (variance_in.at[0], held[3].at[pl.ds(0, pieces)]),
+                (index, index_of.at[0]),
+                (cells.at[pl.ds(me, 1)], got_cells.at[pl.ds(me, 1)]),
+                (row_bands_in, row_bands), (cols_in, cols), (rows_in, rows),
+            )
+        )
+    ]
+    for c in mine:
+        c.start()
+    for n in range(6):
+        held[n][pieces] = jnp.zeros((CR, CW), jnp.float32)
     pl.semaphore_wait(barrier, patches - 1 + subtiles - 1)
+
+    far = [
+        pltpu.make_async_remote_copy(
+            src_ref=x.at[0], dst_ref=held[3 * kind + 1 + side].at[pl.ds(0, pieces)],
+            send_sem=far_send.at[2 * kind + side], recv_sem=far_recv.at[2 * kind + side],
+            device_id={"patch": to * PLANE + flat}, device_id_type=MESH,
+        )
+        for kind, x in enumerate((image_in, variance_in))
+        for side, to in enumerate((after, before))
+    ]
+    told = [
+        pltpu.make_async_remote_copy(
+            src_ref=index, dst_ref=near_index.at[side], send_sem=index_send.at[side],
+            recv_sem=index_recv.at[side], device_id={"patch": to * PLANE + flat},
+            device_id_type=MESH,
+        )
+        for side, to in enumerate((after, before))
+    ]
+    for c in told + far[0:2]:
+        c.start()
 
     pairs = (
         (cells, got_cells, 1), (sent_image, got_image, BLOCK),
         (sent_first, got_first, PART), (sent_last, got_last, PART),
     )
 
-    def ends(n, to, source):
-        src, dst, size = pairs[n]
-        src_at = pl.ds(pl.multiple_of(to * size, size), size)
-        dst_at = pl.ds(pl.multiple_of(source * size, size), size)
-        return src.at[src_at], dst.at[dst_at]
-
-    def start(n, d):
-        to = lax.rem(me + d, patches)
-        src, dst = ends(n, to, me)
+    def rows_at(n, q):
+        size = pairs[n][2]
+        return pl.ds(pl.multiple_of(q * size, size), size)
+
+    def send_to(n, block, to, source):
+        src, dst, _ = pairs[n]
         pltpu.make_async_remote_copy(
-            src_ref=src, dst_ref=dst, send_sem=send.at[n], recv_sem=recv.at[n],
+            src_ref=src.at[rows_at(n, block)], dst_ref=dst.at[rows_at(n, source)],
+            send_sem=send.at[n], recv_sem=recv.at[n],
             device_id={"patch": to}, device_id_type=MESH,
         ).start()
 
     def whole(n):
         src, dst, size = pairs[n]
-        at = pl.ds(0, (patches - 1) * size)
+        at = pl.ds(0, (patches - (1 if n == 0 else 3)) * size)
         return pltpu.make_async_remote_copy(
             src_ref=src.at[at], dst_ref=dst.at[at], send_sem=send.at[n], recv_sem=recv.at[n],
             device_id={"patch": lax.rem(me + 1, patches)}, device_id_type=MESH,
         )
+
+    sources = [q * PLANE + flat for q in (z, before, after)]
+    signs = (0, 1, planes - 1)
+    half = planes // 2
+    shares = ((1, half, half - 1), (1, half - 1, half))
+
+    def first_block(kind, role):
+        return PLANE * sum(shares[kind][0:role])
+
+    def target(role, i):
+        plane = lax.rem(z + signs[role] * (i // PLANE), planes)
+        return plane * PLANE + lax.rem(i + flat, PLANE)
+
+    def pack(kind, role):
+        first = first_block(kind, role)
+
+        def body(i, _):
+            q = target(role, i)
+            x = [held[3 * kind + role][index_of[role, 0, 2 * q + rank]] for rank in range(2)]
+            if kind == 0:
+                tall = [jnp.concatenate([a[:, h : h + 128] for a in x], axis=0) for h in (0, 128)]
+                values = [(1, jnp.concatenate(tall, axis=0))]
+            else:
+                values = []
+                for k in range(2):
+                    cut = slice(k * RC, (k + 1) * RC)
+                    tall = [jnp.concatenate([a[cut, h : h + 128] for a in x], axis=0) for h in (0, 128)]
+                    values.append((2 + k, jnp.concatenate(tall, axis=0)))
+            for n, value in values:
+                pairs[n][0][rows_at(n, first + i), :] = value
+
+            @pl.when(q == me)
+            def _():
+                for n, value in values:
+                    pairs[n][1][rows_at(n, sources[role]), :] = value
+
+            return 0
+
+        lax.fori_loop(0, PLANE * shares[kind][role], body, 0)
+
+    def dispatch(n, role):
+        kind = min(n - 1, 1)
+        first = first_block(kind, role)
+
+        def body(i, _):
+            q = target(role, i)
+
+            @pl.when(q != me)
+            def _():
+                send_to(n, first + i, q, sources[role])
+
+            return 0
+
+        lax.fori_loop(0, PLANE * shares[kind][role], body, 0)
 
     def ring(n, src, dst):
         return [
@@ -307,30 +394,42 @@
             for k, (s, r, to) in enumerate(zip(src, dst, (next_sub, last_sub)))
         ]
 
-    def start_first(d, _):
-        start(0, d)
-        start(1, d)
+    def tell_cells(d, _):
+        q = lax.rem(me + d, patches)
+        send_to(0, q, q, me)
         return 0
 
-    lax.fori_loop(1, patches, start_first, 0)
+    lax.fori_loop(1, patches, tell_cells, 0)
     table_ring = ring(0, (stamps, stamps), (got_stamps.at[0], got_stamps.at[1]))
-    for c in table_ring:
-        c.start()
-
-    for n in (2, 3):
-
-        def start_chunk(d, _):
-            start(n, d)
-            return 0
-
-        lax.fori_loop(1, patches, start_chunk, 0)
-    mine = [pltpu.make_async_copy(*ends(n, me, me), own.at[n]) for n in range(4)]
-    fixed = ((row_bands_in, row_bands), (cols_in, cols), (rows_in, rows))
-    mine += [pltpu.make_async_copy(x, y, own.at[4 + n]) for n, (x, y) in enumerate(fixed)]
-    for c in mine:
+    for c in table_ring + far[2:4]:
         c.start()
     for c in mine:
         c.wait()
+    pack(0, 0)
+    pack(1, 0)
+    dispatch(1, 0)
+    moves = []
+    for side, c in enumerate(told):
+        c.wait()
+        moves.append(pltpu.make_async_copy(near_index.at[side], index_of.at[1 + side], own.at[side]))
+        moves[side].start()
+    for c in moves:
+        c.wait()
+    for c in far[0:2]:
+        c.wait_recv()
+    for role in (1, 2):
+        pack(0, role)
+        dispatch(1, role)
+    for c in far[2:4]:
+        c.wait_recv()
+    for role in (1, 2):
+        pack(1, role)
+        dispatch(2, role)
+    dispatch(2, 0)
+    for role in (1, 2, 0):
+        dispatch(3, role)
+    for c in far:
+        c.wait_send()
     for c in table_ring:
         c.wait()
     stamp_mask(mask, stamps, got_stamps, sub, subtiles, slots)
@@ -339,6 +438,12 @@
         for k in range(2):
             half_mask[k, c * RC : (c + 1) * RC, :] = mask[c * CR + k * RC : c * CR + (k + 1) * RC, :]
     acc[...] = jnp.zeros_like(acc)
+    for at in (slice(0, 16), slice(112, TE)):
+        filt[:, at, :] = jnp.zeros((NT, 16, CW), jnp.float32)
+        text[at, :] = jnp.zeros((16, CW), jnp.float32)
+    for k in (NB,) + tuple(range(NB + 1 + V, XR)):
+        for ref in (xleft, xright):
+            ref[pl.ds(k, RT, stride=XR), :] = jnp.full((RT, 128), float(k == NB), jnp.float32)
     whole(0).wait_recv()
     whole(1).wait_recv()
     table = stamps[...]
@@ -359,16 +464,30 @@
     rims = ring(1, (down, up), (above, below))
     for c in rims:
         c.start()
+    text[32:96, :] = template[...]
+    filter_columns(text, filt, (8, lambda i: i + 4))
     for c in rims:
         c.wait()
-    above[...] = above[...] * has_above
-    below[...] = below[...] * has_below
+    text[8:32, :] = above[0:TH, :] * has_above
+    text[96:120, :] = below[0:TH, :] * has_below
+    filter_columns(text, filt, (4, lambda i: i + 2 + 8 * (i // 2)))
+
+    def put(k, image):
+        at = pl.ds(k, RT, stride=XR)
+        xleft[at, :] = image[:, 0:128]
+        xright[at, :] = image[:, 128:CW]
+
+    def keep_inner(k, image):
+        basis[k, SR : SR + RT, :] = image
+        put(k, image)
+
+    def keep_rim(k, image):
+        basis[k, 0:SR, :] = image[0:SR, :]
+        basis[k, SR + RT : CE, :] = image[SR : 2 * SR, :]
+
+    filter_rows(row_bands, filt, 0, RT, keep_inner)
     for v in range(V):
-        at = TH + v * SR
-        science[v, 0:SR, :] = above[at : at + SR, :]
-        science[v, SR + RT : CE, :] = below[at : at + SR, :]
-    basis_images(science, template, above, below, row_bands, basis, xleft, xright, text, filt)
-
+        put(NB + 1 + v, science[v, SR : SR + RT, :])
     whole(0).wait_send()
     whole(1).wait_send()
 
@@ -416,6 +535,12 @@
         planes = [ref[v * SR : (v + 1) * SR, :] for v in range(V)]
         for v, inv in enumerate(invert(planes)):
             inverse[v * CE + first : v * CE + first + SR, :] = inv * has
+    for v in range(V):
+        at = TH + v * SR
+        science[v, 0:SR, :] = above[at : at + SR, :] * has_above
+        science[v, SR + RT : CE, :] = below[at : at + SR, :] * has_below
+    filter_columns(text, filt, (2, lambda i: 1 + 13 * i))
+    filter_rows(row_bands, filt, NT * RT, 2 * SR, keep_rim)
     for v, den in enumerate(smooth(inverse[...], cols[2], cols[3], rows[1])):
         root[v] = lax.rsqrt(den)
     my_part.wait()
@@ -431,22 +556,8 @@
     whole(3).wait_send()
 
 
-def basis_images(
-    science, template, above, below, row_bands, basis, xleft, xright, text, filt,
-):
+def filter_columns(text, filt, blocks):
     taps = tap_values()
-
-    def put(k, image):
-        at = pl.ds(k, RT, stride=XR)
-        xleft[at, :] = image[:, 0:128]
-        xright[at, :] = image[:, 128:CW]
-
-    zero8 = jnp.zeros((8, CW), jnp.float32)
-    text[0:8, :] = zero8
-    text[8:32, :] = above[0:TH, :]
-    text[32:96, :] = template[...]
-    text[96:120, :] = below[0:TH, :]
-    text[120:128, :] = zero8
     col = lax.broadcasted_iota(jnp.int32, (8, CW), 1)
 
     def columns(i, _):
@@ -473,24 +584,20 @@
             filt[j, rows, :] = sums[j]
         return 0
 
-    lax.fori_loop(0, TE // 8, columns, 0)
-
+    count, place = blocks
+    lax.fori_loop(0, count, lambda i, _: columns(place(i), _), 0)
+
+
+def filter_rows(row_bands, filt, first_row, size, keep):
     for first_tap, degree, index in members_of():
         for j in range(degree + 1):
             count = degree + 1 - j
-            lhs = row_bands[first_tap * CE : (first_tap + count) * CE, :]
+            at = first_row + first_tap * size
+            lhs = row_bands[at : at + count * size, :]
             fh, fl = split(filt[first_tap + j])
             y = mm(lhs, jnp.concatenate([fh, fh], axis=0)) + mm(lhs[:, 0:TE], fl)
             for i in range(count):
-                k = index[(i, j)]
-                image = y[i * CE : (i + 1) * CE, :]
-                basis[k] = image
-                put(k, image[SR : SR + RT, :])
-    put(NB, jnp.ones((RT, CW), jnp.float32))
-    for v in range(V):
-        put(NB + 1 + v, science[v, SR : SR + RT, :])
-    for n in range(NB + 1 + V, XR):
-        put(n, jnp.zeros((RT, CW), jnp.float32))
+                keep(index[(i, j)], y[i * size : (i + 1) * size, :])
 
 
 def gram_of(k, weight, xleft, xright, acc):
@@ -626,27 +733,24 @@
 
     f32, i32, bf16 = jnp.float32, jnp.int32, jnp.bfloat16
 
-    sent_shape, part_shape = shape(patches * BLOCK, 128), shape(patches * PART, 128)
-    sent_image, sent_first, sent_last, sent_cell, table = pl.pallas_call(
-        pack_kernel,
-        out_shape=(
-            sent_shape, part_shape, part_shape, shape(patches, 1, 128, dtype=i32),
-            shape(1, 128, dtype=i32),
-        ),
-        in_specs=[far] * 7 + [SCALARS],
-        out_specs=(WHOLE,) * 5,
+    sent_shape, part_shape = vmem((patches * BLOCK, 128), f32), vmem((patches * PART, 128), f32)
+    pieces_image, pieces_variance = keep(pieces_image, pieces_variance)
+    line = shape(1, 128, dtype=i32)
+    index, sent_cell, table = pl.pallas_call(
+        plan_kernel,
+        out_shape=(line, shape(patches, 1, 128, dtype=i32), line),
+        in_specs=[far] * 5 + [SCALARS],
+        out_specs=(WHOLE,) * 3,
         scratch_shapes=[
-            vmem((pieces, CR, CW), f32), vmem((pieces, CR, CW), f32),
             smem((pieces,), i32), smem((pieces,), i32),
             smem((1, slots), i32), smem((1, slots), i32), smem((V,), i32),
-            smem((patches,), i32), smem((2 * patches,), i32), dma((7,)),
+            smem((patches,), i32), smem((2 * patches,), i32), smem((2 * patches,), i32), dma((5,)),
         ],
         compiler_params=params(),
-        name="pack",
+        name="plan",
     )(
         *keep(
-            piece_patch.reshape(-1), piece_cell.reshape(-1), pieces_image, pieces_variance,
-            stamp_row, stamp_col, warp_offsets,
+            piece_patch.reshape(-1), piece_cell.reshape(-1), stamp_row, stamp_col, warp_offsets,
         ),
         stamp_count,
     )
@@ -659,11 +763,11 @@
         out_shape=(
             shape(V, CE, CW), shape(V * CE, CW), shape(NB, CE, CW), shape(subtiles, 2 * XR, 128), field,
         ),
-        in_specs=[WHOLE] * 5 + [far] * 3,
+        in_specs=[WHOLE] * 3 + [far] * 5,
         out_specs=(WHOLE,) * 5,
         scratch_shapes=[
-            vmem((patches * BLOCK, 128), f32),
-            vmem((patches * PART, 128), f32), vmem((patches * PART, 128), f32),
+            *[vmem((pieces + 1, CR, CW), f32)] * 6, vmem((2, 1, 128), i32), smem((3, 1, 128), i32),
+            sent_shape, part_shape, part_shape, sent_shape, part_shape, part_shape,
             vmem((patches, 1, 128), i32), vmem((2, 1, 128), i32),
             vmem((V * RT, 128), f32), vmem((V * RT, 128), f32), vmem((RT, CW), f32),
             rim, rim, rim, rim,
@@ -673,13 +777,14 @@
             vmem((V, NCELL * RC, CW), f32), vmem((2 * V * XR, 128), f32), vmem((2 * XR, 128), f32),
             vmem(row_bands.shape, bf16), vmem(cols.shape, bf16), vmem(rows.shape, bf16),
             dma((4,)), dma((4,)), dma((3, 2)), dma((3, 2)),
-            dma((subtiles - 1,)), dma((subtiles - 1,)), dma((8,)),
+            dma((subtiles - 1,)), dma((subtiles - 1,)),
+            dma((4,)), dma((4,)), dma((2,)), dma((2,)), dma((8,)),
         ],
         compiler_params=pltpu.CompilerParams(
             vmem_limit_bytes=32 * 1024 * 1024, collective_id=0, has_side_effects=True
         ),
         name="front",
-    )(sent_image, sent_first, sent_last, sent_cell, table, row_bands, cols, rows)
+    )(index, sent_cell, table, pieces_image, pieces_variance, row_bands, cols, rows)
 
     normalizer = float(subtiles * slots * (2 * SH + 1) ** 2)
     difference, significance = pl.pallas_call(

time: 79.2 us -> 75 us (0.947)
  Pallas kernels: 77.7 us -> 73.6 us
    pallas_call x1, Pallas kernels: 69.3 us -> 65.5 us  [local(): pl.pallas_call(functools.partial(front_kernel, slots), out_shape=(shape(V...]
where the time goes in v6:
time: 75 us; the launch traced here: 74.9 us
  Pallas kernels  73.6 us (98%)
  between operations  1.29 us (2%)
    pallas_call x1, Pallas kernels, local(): pl.pallas_call(functools.partial(front_kernel, slots), out_shape=(shape(V...  65.5 us
    pallas_call x1, Pallas kernels, local(): pl.pallas_call(functools.partial(final_kernel, normalizer), out_shape=(fi...  6.45 us
    pallas_call x1, Pallas kernels, local(): pl.pallas_call(plan_kernel, out_shape=(line, shape(patches, 1, 128, dtype...  1.63 us

profile of v6, /device:TPU:1, one launch (start us, length us, event | category | flops | bytes accessed | tf_op | source)
XLA Modules:
  0.0 74.9 jit_solution(8026832485813498177)
XLA Ops:
  1.3 1.6 %plan.1 = (s32[1,128]{1,0:T(1,128)S(1)}, s32[64,1,128]{2,1,0:T(1,128)S(1)}, s32[1,128]{1,0:T(1,128)S(1)}) custom-call(s32[32]{0:T(128)} %bitcast.8, s32[32]{0:T(128)} %bitcast.9, s32[1,12]{1,0:T(1,128)} %row.1, s32[1,12]{1,0:T(1,128)} %col.1, s32[4]{0:T(128)} %warp.1, s32[1,1]{1,0:T(1,128)S(6)} %copy.15.live), custom_call_target="tpu_custom_call" | custom-call | tf_op jit(solution)/shard_map/plan/pallas_call | solution.py:739
  2.9 65.5 %front.1 = (f32[4,96,256]{2,1,0:T(8,128)S(1)}, f32[384,256]{1,0:T(8,128)S(1)}, f32[40,96,256]{2,1,0:T(8,128)S(1)}, f32[4,96,128]{2,1,0:T(8,128)S(1)}, f32[4,64,256]{2,1,0:T(8,128)S(1)}) custom-call(s32[1,128]{1,0:T(1,128)S(1)} %get-tuple-element.12.index, s32[64,1,128]{2,1,0:T(1,128)S(1)} %get-tuple-element.13.cells, s32[1,128]{1,0:T(1,128)S(1)} %get-tuple-element.14.stamps, ...), custom_call_target="tpu_custom_call" | custom-call | tf_op jit(solution)/shard_map/front/pallas_call | solution.py:761
  68.4 6.5 %final.1 = (f32[4,64,256]{2,1,0:T(8,128)}, f32[4,64,256]{2,1,0:T(8,128)}) custom-call(f32[4,96,128]{2,1,0:T(8,128)S(1)} %get-tuple-element.15.gathered, f32[40,96,256]{2,1,0:T(8,128)S(1)} %get-tuple-element.16.basis, f32[4,96,256]{2,1,0:T(8,128)S(1)} %get-tuple-element.17.science, f32[384,256]{1,0:T(8,128)S(1)} %get-tuple-element.18.inverse, ...), custom_call_target="tpu_custom_call" | custom-call | tf_op jit(solution)/shard_map/final/pallas_call | solution.py:790

commit v7 on v6

--- a/solution.py
+++ b/solution.py
@@ -585,7 +585,7 @@
         return 0
 
     count, place = blocks
-    lax.fori_loop(0, count, lambda i, _: columns(place(i), _), 0)
+    lax.fori_loop(0, count, lambda i, _: columns(place(i), _), 0, unroll=2)
 
 
 def filter_rows(row_bands, filt, first_row, size, keep):
@@ -621,7 +621,7 @@
         )
         return 0
 
-    lax.fori_loop(0, NCELL, cell, 0)
+    lax.fori_loop(0, NCELL, cell, 0, unroll=4)
 
 
 def gram_total(acc, gram):
@@ -665,7 +665,18 @@
         system = system + jnp.where(row == j, RIDGE, 0.0)
         halves.append(system)
         scales.append(e_col)
-    for k in range(NB + 1):
+    for k in range(0, NB, 2):
+        for half in range(2):
+            m = halves[half]
+            top = jnp.broadcast_to(m[k : k + 1, :], (XR, 128))
+            low = jnp.broadcast_to(m[k + 1 : k + 2, :], (XR, 128))
+            a, b, d = pick(top, base + k), pick(top, base + k + 1), pick(low, base + k + 1)
+            scale = 1.0 / (a * d - b * b)
+            left, right = pick(m, base + k), pick(m, base + k + 1)
+            left = jnp.where(row == k, a - 1.0, left)
+            right = jnp.where(row == k + 1, d - 1.0, right)
+            halves[half] = m - left * ((d * top - b * low) * scale) - right * ((a * low - b * top) * scale)
+    for k in (NB,):
         for half in range(2):
             a = halves[half]
             pivot_row = jnp.broadcast_to(a[k : k + 1, :], (XR, 128))

time: 75 us -> 71.1 us (0.948)
  Pallas kernels: 73.6 us -> 69.7 us
    pallas_call x1, Pallas kernels: 65.5 us -> 63.1 us  [local(): pl.pallas_call(functools.partial(front_kernel, slots), out_shape=(shape(V...]
    pallas_call x1, Pallas kernels: 6.45 us -> 5.05 us  [local(): pl.pallas_call(functools.partial(final_kernel, normalizer), out_shape=(fi...]
where the time goes in v7:
time: 71.1 us; the launch traced here: 71 us
  Pallas kernels  69.7 us (98%)
  between operations  1.29 us (2%)
    pallas_call x1, Pallas kernels, local(): pl.pallas_call(functools.partial(front_kernel, slots), out_shape=(shape(V...  63.1 us
    pallas_call x1, Pallas kernels, local(): pl.pallas_call(functools.partial(final_kernel, normalizer), out_shape=(fi...  5.05 us
    pallas_call x1, Pallas kernels, local(): pl.pallas_call(plan_kernel, out_shape=(line, shape(patches, 1, 128, dtype...  1.63 us

profile of v7, /device:TPU:1, one launch (start us, length us, event | category | flops | bytes accessed | tf_op | source)
XLA Modules:
  0.0 71.0 jit_solution(6174712943343382336)
XLA Ops:
  1.3 1.6 %plan.1 = (s32[1,128]{1,0:T(1,128)S(1)}, s32[64,1,128]{2,1,0:T(1,128)S(1)}, s32[1,128]{1,0:T(1,128)S(1)}) custom-call(s32[32]{0:T(128)} %bitcast.8, s32[32]{0:T(128)} %bitcast.9, s32[1,12]{1,0:T(1,128)} %row.1, s32[1,12]{1,0:T(1,128)} %col.1, s32[4]{0:T(128)} %warp.1, s32[1,1]{1,0:T(1,128)S(6)} %copy.15.live), custom_call_target="tpu_custom_call" | custom-call | tf_op jit(solution)/shard_map/plan/pallas_call | solution.py:750
  2.9 63.1 %front.1 = (f32[4,96,256]{2,1,0:T(8,128)S(1)}, f32[384,256]{1,0:T(8,128)S(1)}, f32[40,96,256]{2,1,0:T(8,128)S(1)}, f32[4,96,128]{2,1,0:T(8,128)S(1)}, f32[4,64,256]{2,1,0:T(8,128)S(1)}) custom-call(s32[1,128]{1,0:T(1,128)S(1)} %get-tuple-element.12.index, s32[64,1,128]{2,1,0:T(1,128)S(1)} %get-tuple-element.13.cells, s32[1,128]{1,0:T(1,128)S(1)} %get-tuple-element.14.stamps, ...), custom_call_target="tpu_custom_call" | custom-call | tf_op jit(solution)/shard_map/front/pallas_call | solution.py:772
  66.0 5.1 %final.1 = (f32[4,64,256]{2,1,0:T(8,128)}, f32[4,64,256]{2,1,0:T(8,128)}) custom-call(f32[4,96,128]{2,1,0:T(8,128)S(1)} %get-tuple-element.15.gathered, f32[40,96,256]{2,1,0:T(8,128)S(1)} %get-tuple-element.16.basis, f32[4,96,256]{2,1,0:T(8,128)S(1)} %get-tuple-element.17.science, f32[384,256]{1,0:T(8,128)S(1)} %get-tuple-element.18.inverse, ...), custom_call_target="tpu_custom_call" | custom-call | tf_op jit(solution)/shard_map/final/pallas_call | solution.py:801

commit v8 on v7

--- a/solution.py
+++ b/solution.py
@@ -265,7 +265,7 @@
         pl.semaphore_signal(barrier, inc=1, device_id={"patch": q}, device_id_type=MESH)
         return 0
 
-    lax.fori_loop(1, patches, greet, 0)
+    lax.fori_loop(1, patches, greet, 0, unroll=9)
     for s in peers:
         pl.semaphore_signal(barrier, inc=1, device_id={"sub": s}, device_id_type=MESH)
     mine = [
@@ -383,7 +383,7 @@
 
             return 0
 
-        lax.fori_loop(0, PLANE * shares[kind][role], body, 0)
+        lax.fori_loop(0, PLANE * shares[kind][role], body, 0, unroll=4)
 
     def ring(n, src, dst):
         return [
@@ -399,13 +399,13 @@
         send_to(0, q, q, me)
         return 0
 
-    lax.fori_loop(1, patches, tell_cells, 0)
     table_ring = ring(0, (stamps, stamps), (got_stamps.at[0], got_stamps.at[1]))
     for c in table_ring + far[2:4]:
         c.start()
     for c in mine:
         c.wait()
     pack(0, 0)
+    lax.fori_loop(1, patches, tell_cells, 0, unroll=9)
     pack(1, 0)
     dispatch(1, 0)
     moves = []

time: 71.1 us -> 71 us (level)
  no operation moved by 1% of the time
where the time goes in v8:
time: 71 us; the launch traced here: 70.9 us
  Pallas kernels  69.6 us (98%)
  between operations  1.29 us (2%)
    pallas_call x1, Pallas kernels, local(): pl.pallas_call(functools.partial(front_kernel, slots), out_shape=(shape(V...  62.9 us
    pallas_call x1, Pallas kernels, local(): pl.pallas_call(functools.partial(final_kernel, normalizer), out_shape=(fi...  5.05 us
    pallas_call x1, Pallas kernels, local(): pl.pallas_call(plan_kernel, out_shape=(line, shape(patches, 1, 128, dtype...  1.63 us

profile of v8, /device:TPU:1, one launch (start us, length us, event | category | flops | bytes accessed | tf_op | source)
XLA Modules:
  0.0 70.9 jit_solution(340716264530252185)
XLA Ops:
  1.3 1.6 %plan.1 = (s32[1,128]{1,0:T(1,128)S(1)}, s32[64,1,128]{2,1,0:T(1,128)S(1)}, s32[1,128]{1,0:T(1,128)S(1)}) custom-call(s32[32]{0:T(128)} %bitcast.8, s32[32]{0:T(128)} %bitcast.9, s32[1,12]{1,0:T(1,128)} %row.1, s32[1,12]{1,0:T(1,128)} %col.1, s32[4]{0:T(128)} %warp.1, s32[1,1]{1,0:T(1,128)S(6)} %copy.15.live), custom_call_target="tpu_custom_call" | custom-call | tf_op jit(solution)/shard_map/plan/pallas_call | solution.py:750
  2.9 62.9 %front.1 = (f32[4,96,256]{2,1,0:T(8,128)S(1)}, f32[384,256]{1,0:T(8,128)S(1)}, f32[40,96,256]{2,1,0:T(8,128)S(1)}, f32[4,96,128]{2,1,0:T(8,128)S(1)}, f32[4,64,256]{2,1,0:T(8,128)S(1)}) custom-call(s32[1,128]{1,0:T(1,128)S(1)} %get-tuple-element.12.index, s32[64,1,128]{2,1,0:T(1,128)S(1)} %get-tuple-element.13.cells, s32[1,128]{1,0:T(1,128)S(1)} %get-tuple-element.14.stamps, ...), custom_call_target="tpu_custom_call" | custom-call | tf_op jit(solution)/shard_map/front/pallas_call | solution.py:772
  65.8 5.1 %final.1 = (f32[4,64,256]{2,1,0:T(8,128)}, f32[4,64,256]{2,1,0:T(8,128)}) custom-call(f32[4,96,128]{2,1,0:T(8,128)S(1)} %get-tuple-element.15.gathered, f32[40,96,256]{2,1,0:T(8,128)S(1)} %get-tuple-element.16.basis, f32[4,96,256]{2,1,0:T(8,128)S(1)} %get-tuple-element.17.science, f32[384,256]{1,0:T(8,128)S(1)} %get-tuple-element.18.inverse, ...), custom_call_target="tpu_custom_call" | custom-call | tf_op jit(solution)/shard_map/final/pallas_call | solution.py:801
